TPU v7x, 128 devices: a whole 4x4x4 slice. The times are simulated.
128 devices in a mesh: row: 16 (over x, z), col: 8 (over y, core).
Axes of the slice: x: 4, y: 4, z: 4, core: 2. Of those that a mesh axis runs over, the one named last changes fastest.
Arguments:
- t_upper: bfloat16 [3, 4096, 4096], P(None, 'row', 'col'), may hold values from -0.03125 to 0.03125
- t_old: bfloat16 [3, 4096, 24576], P(None, 'row', 'col'), may hold values from -0.03125 to 0.03125
- inverses: bfloat16 [3, 4096, 4096], P(None, 'row', 'col'), may hold values from -1 to 1.5, as said below
- forcing: float32 [3, 4096, 128], P(None, 'row'), may hold values from -6 to 6
- x_old: bfloat16 [24576, 128], P('col'), may hold values from -6 to 6
- offsets: float32 [128], replicated, may hold values from -0.5 to 0.5
- starts: int32 [128], replicated, may hold values from 0 to 36864
- column_map: int32 [128], replicated, may hold values from 0 to 127, each once
- z_cols: bfloat16 [49152, 3, 4096], P('row', None, 'col'), may hold values from -0.0546875 to 0.0546875
- acc: float32 [49152, 128], P(('row', 'col')), may hold values from -6 to 6
Outputs:
- solved: float32 [3, 4096, 128], P(None, ('row', 'col'))
- acc_out: float32 [49152, 128], P(('row', 'col'))
Inputs may be any that keep to these rules, and one draw needn't show every extreme that they name: `inverses`: dense matrices with a dominant positive diagonal.
All inputs are finite; a program needn't handle non-finite values.
Results may differ from a plain program's by a relative error of at most 0.0003.
Values may be sent and summed in bfloat16 or wider, within the bound.
No kernel may reach another device: no remote copies, remote signals or barrier semaphores. Data moves between devices by JAX's collectives and lax.ppermute only.
A program may use at most 128 MiB of HBM per device.

v0:
```python
import jax
import jax.numpy as jnp
from jax import lax
from jax.sharding import PartitionSpec as P

NEUMANN = 3


def split_pair(values):
    upper = values.astype(jnp.bfloat16)
    lower = (values - lax.optimization_barrier(upper).astype(jnp.float32)).astype(jnp.bfloat16)
    return jnp.concatenate([upper, lower], axis=-1)


def body(t_upper, t_old, inverses, forcing, x_old, offsets, starts, column_map, z_cols, acc):
    n_col = lax.axis_size("col")
    row_idx = lax.axis_index("row")
    col_idx = lax.axis_index("col")
    steps = forcing.shape[0]
    row_block = t_upper.shape[1]
    col_block = t_upper.shape[2]
    width = forcing.shape[2]
    old_cols = x_old.shape[0]
    full_rows = col_block * n_col
    share = row_block // n_col
    pairs = {}
    count = 0
    for first in range(steps):
        for second in range(first + 1, steps):
            pairs[first, second] = count
            count = count + 1

    def fold_pair(product):
        return product[:, :width] + product[:, width:]

    old_rows = steps * full_rows + col_idx * old_cols + jnp.arange(old_cols, dtype=jnp.int32)
    old_live = old_rows[:, None] < starts[None, :]
    old_vals = jnp.where(old_live, x_old, jnp.zeros_like(x_old))
    local_start = row_idx * row_block

    def reduce_rows(partial_value):
        return lax.psum(partial_value, "col")

    def spread_rows(values):
        return lax.all_gather(values, "row", axis=0, tiled=True)

    def own_cols(whole):
        return lax.dynamic_slice_in_dim(whole, col_idx * col_block, col_block, 0)

    solved_full = {}
    pieces = {}
    for step in reversed(range(steps)):
        partial_value = -jnp.dot(t_old[step], old_vals, preferred_element_type=jnp.float32)
        for later in range(step + 1, steps):
            partial_value = partial_value - fold_pair(
                jnp.dot(
                    t_upper[pairs[step, later]],
                    own_cols(solved_full[later]),
                    preferred_element_type=jnp.float32,
                )
            )
        rhs = reduce_rows(partial_value) + forcing[step]
        gathered = spread_rows(split_pair(rhs))
        term = reduce_rows(
            fold_pair(
                jnp.dot(inverses[step], own_cols(gathered), preferred_element_type=jnp.float32)
            )
        )
        total = term
        for extra in range(1, NEUMANN):
            gathered = spread_rows(split_pair(term))
            term = (
                reduce_rows(
                    fold_pair(
                        jnp.dot(
                            inverses[step], own_cols(gathered), preferred_element_type=jnp.float32
                        )
                    )
                )
                * offsets[None, :]
            )
            total = total + term
        rows = step * full_rows + local_start + jnp.arange(row_block, dtype=jnp.int32)
        total = jnp.where(rows[:, None] < starts[None, :], total, jnp.zeros_like(total))
        pieces[step] = lax.dynamic_slice_in_dim(total, col_idx * share, share, 0)
        solved_full[step] = spread_rows(split_pair(total))
    stacked = jnp.concatenate([own_cols(solved_full[step]) for step in range(steps)], axis=0)
    one_hot = (jnp.arange(width, dtype=jnp.int32)[:, None] == column_map[None, :]).astype(
        jnp.bfloat16
    )
    picked_upper = jnp.dot(stacked[:, :width], one_hot, preferred_element_type=jnp.float32).astype(
        jnp.bfloat16
    )
    picked_lower = jnp.dot(stacked[:, width:], one_hot, preferred_element_type=jnp.float32).astype(
        jnp.bfloat16
    )
    picked = jnp.concatenate([picked_upper, picked_lower], axis=1)
    z_rows = z_cols.shape[0]
    z_flat = z_cols.reshape(z_rows, steps * col_block)
    contribution = lax.psum_scatter(
        fold_pair(jnp.dot(z_flat, picked, preferred_element_type=jnp.float32)),
        "col",
        scatter_dimension=0,
        tiled=True,
    )
    solved = jnp.stack([pieces[step] for step in range(steps)])
    return (solved, acc + contribution)


def solution(mesh):
    placed = (
        P(None, "row", "col"),
        P(None, "row", "col"),
        P(None, "row", "col"),
        P(None, "row", None),
        P("col", None),
        P(),
        P(),
        P(),
        P("row", None, "col"),
        P(("row", "col"), None),
    )
    return jax.shard_map(
        body,
        mesh=mesh,
        in_specs=placed,
        out_specs=(P(None, ("row", "col"), None), P(("row", "col"), None)),
        check_vma=False,
    )
```

profile of v0, /device:TPU:1, one launch (start us, length us, event | category | flops | bytes accessed | tf_op | source)
XLA Modules:
  0.0 1394.4 jit_solution(2241294068387488249)
XLA Ops:
  7.2 3.6 fusion.33
  11.0 60.8 %all-reduce.13.cloned.1.call-done = f32[256,128]{0,1:T(8,128)} async-done(((f32[256,128]{0,1:T(8,128)}), f32[256,128]{0,1:T(8,128)}) %all-reduce.13.cloned.1.call-update) | async-done | bytes 131088 | tf_op jit(solution)/shard_map/psum | solution.py:42
  74.5 46.8 %all-gather.13.cloned.1.call-done = bf16[4096,256]{0,1:T(8,128)(2,1)} async-done(((bf16[256,256]{0,1:T(8,128)(2,1)}), bf16[4096,256]{0,1:T(8,128)(2,1)}) %all-gather.13.cloned.1.call-update) | async-done | bytes 2097168 | tf_op jit(solution)/shard_map/all_gather | solution.py:45
  121.3 1.2 convolution_bitcast_fusion.12
  123.3 59.6 %all-reduce.15.cloned.1.call-done = f32[256,128]{0,1:T(8,128)} async-done(((f32[256,128]{0,1:T(8,128)}), f32[256,128]{0,1:T(8,128)}) %all-reduce.15.cloned.1.call-update) | async-done | bytes 131088 | tf_op jit(solution)/shard_map/psum | solution.py:42
  185.5 46.8 %all-gather.15.cloned.1.call-done = bf16[4096,256]{0,1:T(8,128)(2,1)} async-done(((bf16[256,256]{0,1:T(8,128)(2,1)}), bf16[4096,256]{0,1:T(8,128)(2,1)}) %all-gather.15.cloned.1.call-update) | async-done | bytes 2097168 | tf_op jit(solution)/shard_map/all_gather | solution.py:45
  232.4 1.2 convolution_bitcast_fusion.11
  234.3 59.4 %all-reduce.17.cloned.1.call-done = f32[256,128]{0,1:T(8,128)} async-done(((f32[256,128]{0,1:T(8,128)}), f32[256,128]{0,1:T(8,128)}) %all-reduce.17.cloned.1.call-update) | async-done | bytes 131088 | tf_op jit(solution)/shard_map/psum | solution.py:42
  293.8 1.1 multiply_convert_fusion.2
  294.9 1.0 subtract_convert_fusion.9
  296.6 46.8 %all-gather.17.cloned.1.call-done = bf16[4096,256]{0,1:T(8,128)(2,1)} async-done(((bf16[256,256]{0,1:T(8,128)(2,1)}), bf16[4096,256]{0,1:T(8,128)(2,1)}) %all-gather.17.cloned.1.call-update) | async-done | bytes 2097168 | tf_op jit(solution)/shard_map/all_gather | solution.py:45
  343.4 1.2 convolution_bitcast_fusion.10
  345.4 59.6 %all-reduce.19.cloned.1.call-done = f32[256,128]{0,1:T(8,128)} async-done(((f32[256,128]{0,1:T(8,128)}), f32[256,128]{0,1:T(8,128)}) %all-reduce.19.cloned.1.call-update) | async-done | bytes 131088 | tf_op jit(solution)/shard_map/psum | solution.py:42
  405.0 1.0 fusion.91
  406.8 47.7 %all-gather.19.cloned.1.call-done = bf16[4096,256]{0,1:T(8,128)(2,1)} async-done(((bf16[256,256]{0,1:T(8,128)(2,1)}), bf16[4096,256]{0,1:T(8,128)(2,1)}) %all-gather.19.cloned.1.call-update) | async-done | bytes 2097168 | tf_op jit(solution)/shard_map/all_gather | solution.py:45
  455.7 3.5 fusion.27
  459.4 58.7 %all-reduce.21.cloned.1.call-done = f32[256,128]{0,1:T(8,128)} async-done(((f32[256,128]{0,1:T(8,128)}), f32[256,128]{0,1:T(8,128)}) %all-reduce.21.cloned.1.call-update) | async-done | bytes 131088 | tf_op jit(solution)/shard_map/psum | solution.py:42
  520.6 46.8 %all-gather.21.cloned.1.call-done = bf16[4096,256]{0,1:T(8,128)(2,1)} async-done(((bf16[256,256]{0,1:T(8,128)(2,1)}), bf16[4096,256]{0,1:T(8,128)(2,1)}) %all-gather.21.cloned.1.call-update) | async-done | bytes 2097168 | tf_op jit(solution)/shard_map/all_gather | solution.py:45
  567.5 1.2 convolution_bitcast_fusion.8
  569.4 59.6 %all-reduce.23.cloned.1.call-done = f32[256,128]{0,1:T(8,128)} async-done(((f32[256,128]{0,1:T(8,128)}), f32[256,128]{0,1:T(8,128)}) %all-reduce.23.cloned.1.call-update) | async-done | bytes 131088 | tf_op jit(solution)/shard_map/psum | solution.py:42
  631.7 46.8 %all-gather.23.cloned.1.call-done = bf16[4096,256]{0,1:T(8,128)(2,1)} async-done(((bf16[256,256]{0,1:T(8,128)(2,1)}), bf16[4096,256]{0,1:T(8,128)(2,1)}) %all-gather.23.cloned.1.call-update) | async-done | bytes 2097168 | tf_op jit(solution)/shard_map/all_gather | solution.py:45
  678.5 1.2 convolution_bitcast_fusion.7
  680.5 59.6 %all-reduce.25.cloned.1.call-done = f32[256,128]{0,1:T(8,128)} async-done(((f32[256,128]{0,1:T(8,128)}), f32[256,128]{0,1:T(8,128)}) %all-reduce.25.cloned.1.call-update) | async-done | bytes 131088 | tf_op jit(solution)/shard_map/psum | solution.py:42
  740.1 1.1 multiply_convert_fusion.1
  742.9 46.8 %all-gather.25.cloned.1.call-done = bf16[4096,256]{0,1:T(8,128)(2,1)} async-done(((bf16[256,256]{0,1:T(8,128)(2,1)}), bf16[4096,256]{0,1:T(8,128)(2,1)}) %all-gather.25.cloned.1.call-update) | async-done | bytes 2097168 | tf_op jit(solution)/shard_map/all_gather | solution.py:45
  789.7 1.2 convolution_bitcast_fusion.6
  791.7 59.4 %all-reduce.27.cloned.1.call-done = f32[256,128]{0,1:T(8,128)} async-done(((f32[256,128]{0,1:T(8,128)}), f32[256,128]{0,1:T(8,128)}) %all-reduce.27.cloned.1.call-update) | async-done | bytes 131088 | tf_op jit(solution)/shard_map/psum | solution.py:42
  851.1 1.0 fusion.90
  853.2 47.3 %all-gather.27.cloned.1.call-done = bf16[4096,256]{0,1:T(8,128)(2,1)} async-done(((bf16[256,256]{0,1:T(8,128)(2,1)}), bf16[4096,256]{0,1:T(8,128)(2,1)}) %all-gather.27.cloned.1.call-update) | async-done | bytes 2097168 | tf_op jit(solution)/shard_map/all_gather | solution.py:45
  901.7 3.5 fusion.18
  905.4 58.7 %all-reduce.29.cloned.1.call-done = f32[256,128]{0,1:T(8,128)} async-done(((f32[256,128]{0,1:T(8,128)}), f32[256,128]{0,1:T(8,128)}) %all-reduce.29.cloned.1.call-update) | async-done | bytes 131088 | tf_op jit(solution)/shard_map/psum | solution.py:42
  966.6 46.8 %all-gather.29.cloned.1.call-done = bf16[4096,256]{0,1:T(8,128)(2,1)} async-done(((bf16[256,256]{0,1:T(8,128)(2,1)}), bf16[4096,256]{0,1:T(8,128)(2,1)}) %all-gather.29.cloned.1.call-update) | async-done | bytes 2097168 | tf_op jit(solution)/shard_map/all_gather | solution.py:45
  1013.4 1.2 convolution_bitcast_fusion.3
  1015.4 59.6 %all-reduce.31.cloned.1.call-done = f32[256,128]{0,1:T(8,128)} async-done(((f32[256,128]{0,1:T(8,128)}), f32[256,128]{0,1:T(8,128)}) %all-reduce.31.cloned.1.call-update) | async-done | bytes 131088 | tf_op jit(solution)/shard_map/psum | solution.py:42
  1077.7 46.8 %all-gather.31.cloned.1.call-done = bf16[4096,256]{0,1:T(8,128)(2,1)} async-done(((bf16[256,256]{0,1:T(8,128)(2,1)}), bf16[4096,256]{0,1:T(8,128)(2,1)}) %all-gather.31.cloned.1.call-update) | async-done | bytes 2097168 | tf_op jit(solution)/shard_map/all_gather | solution.py:45
  1124.5 1.2 convolution_bitcast_fusion.2
  1126.4 59.6 %all-reduce.33.cloned.1.call-done = f32[256,128]{0,1:T(8,128)} async-done(((f32[256,128]{0,1:T(8,128)}), f32[256,128]{0,1:T(8,128)}) %all-reduce.33.cloned.1.call-update) | async-done | bytes 131088 | tf_op jit(solution)/shard_map/psum | solution.py:42
  1186.1 1.1 multiply_convert_fusion
  1187.1 1.0 subtract_convert_fusion.1
  1188.9 46.8 %all-gather.33.cloned.1.call-done = bf16[4096,256]{0,1:T(8,128)(2,1)} async-done(((bf16[256,256]{0,1:T(8,128)(2,1)}), bf16[4096,256]{0,1:T(8,128)(2,1)}) %all-gather.33.cloned.1.call-update) | async-done | bytes 2097168 | tf_op jit(solution)/shard_map/all_gather | solution.py:45
  1235.7 1.2 convolution_bitcast_fusion.1
  1237.7 59.6 %all-reduce.35.cloned.1.call-done = f32[256,128]{0,1:T(8,128)} async-done(((f32[256,128]{0,1:T(8,128)}), f32[256,128]{0,1:T(8,128)}) %all-reduce.35.cloned.1.call-update) | async-done | bytes 131088 | tf_op jit(solution)/shard_map/psum | solution.py:42
  1297.3 1.0 fusion.89
  1299.0 12.6 copy.23
  1311.7 34.9 %all-gather.35.cloned.1.call-done = bf16[4096,256]{0,1:T(8,128)(2,1)} async-done(((bf16[256,256]{0,1:T(8,128)(2,1)}), bf16[4096,256]{0,1:T(8,128)(2,1)}) %all-gather.35.cloned.1.call-update) | async-done | bytes 2097168 | tf_op jit(solution)/shard_map/all_gather | solution.py:45
  1348.2 5.2 convolution_bitcast_fusion
  1353.4 1.3 slice_add_fusion
  1356.1 30.0 %reduce-scatter.2.cloned.1.call-done = f32[384,128]{0,1:T(8,128)} async-done(((f32[3072,128]{0,1:T(8,128)}), f32[384,128]{0,1:T(8,128)}) %reduce-scatter.2.cloned.1.call-update) | async-done | bytes 196624 | tf_op jit(solution)/shard_map/reduce_scatter | solution.py:100
  (140 shorter events, 35.4 us)
Async XLA Ops:
  7.2 3.7 copy-start.8
  7.2 64.7 %all-reduce.13.cloned.1.call-start = ((), (), s32[]{:S(2)}) async-start(), calls=%async_computation.1 | async-start | bytes 262144 | tf_op jit(solution)/shard_map/psum | solution.py:42
  10.8 110.5 %copy-start = (bf16[3,256,512]{2,1,0:T(8,128)(2,1)S(1)}, bf16[3,256,512]{2,1,0:T(8,128)(2,1)}, u32[]{:S(2)}) copy-start(bf16[3,256,512]{2,1,0:T(8,128)(2,1)} %param.12) | copy-start | bytes 2359300
  10.8 110.5 %all-gather.13.cloned.1.call-start = ((), (), s32[]{:S(2)}) async-start(), calls=%async_computation.2 | async-start | bytes 2228224 | tf_op jit(solution)/shard_map/all_gather | solution.py:45
  72.8 221.0 %copy-start.10 = (f32[128]{0:T(128)S(1)}, f32[128]{0:T(128)}, u32[]{:S(2)}) copy-start(f32[128]{0:T(128)} %param.15) | copy-start | bytes 1540
  74.4 108.5 %all-reduce.15.cloned.1.call-start = ((), (), s32[]{:S(2)}) async-start(), calls=%async_computation.3 | async-start | bytes 262144 | tf_op jit(solution)/shard_map/psum | solution.py:42
  123.2 109.1 %all-gather.15.cloned.1.call-start = ((), (), s32[]{:S(2)}) async-start(), calls=%async_computation.4 | async-start | bytes 2228224 | tf_op jit(solution)/shard_map/all_gather | solution.py:45
  183.8 221.2 %copy-start.1 = (f32[256,128]{0,1:T(8,128)S(1)}, f32[256,128]{0,1:T(8,128)}, u32[]{:S(2)}) copy-start(f32[256,128]{0,1:T(8,128)} %all-reduce.15.cloned.1.call-done) | copy-start | bytes 393220
  183.8 221.2 %copy-start.11 = (s32[128]{0:T(128)S(1)}, s32[128]{0:T(128)}, u32[]{:S(2)}) copy-start(s32[128]{0:T(128)} %param.16) | copy-start | bytes 1540
  185.5 108.3 %all-reduce.17.cloned.1.call-start = ((), (), s32[]{:S(2)}) async-start(), calls=%async_computation.5 | async-start | bytes 262144 | tf_op jit(solution)/shard_map/psum | solution.py:42
  234.3 221.2 %copy-start.7 = (bf16[3,256,512]{2,1,0:T(8,128)(2,1)S(1)}, bf16[3,256,512]{2,1,0:T(8,128)(2,1)}, u32[]{:S(2)}) copy-start(bf16[3,256,512]{2,1,0:T(8,128)(2,1)} %param.10) | copy-start | bytes 2359300
  234.3 109.1 %all-gather.17.cloned.1.call-start = ((), (), s32[]{:S(2)}) async-start(), calls=%async_computation.6 | async-start | bytes 2228224 | tf_op jit(solution)/shard_map/all_gather | solution.py:45
  293.8 111.2 %copy-start.4 = (f32[256,128]{0,1:T(8,128)S(1)}, f32[256,128]{0,1:T(8,128)}, u32[]{:S(2)}) copy-start(f32[256,128]{0,1:T(8,128)} %all-reduce.17.cloned.1.call-done) | copy-start | bytes 393220
  296.5 108.4 %all-reduce.19.cloned.1.call-start = ((), (), s32[]{:S(2)}) async-start(), calls=%async_computation.7 | async-start | bytes 262144 | tf_op jit(solution)/shard_map/psum | solution.py:42
  345.3 109.1 %all-gather.19.cloned.1.call-start = ((), (), s32[]{:S(2)}) async-start(), calls=%async_computation.8 | async-start | bytes 2228224 | tf_op jit(solution)/shard_map/all_gather | solution.py:45
  406.7 111.3 %all-reduce.21.cloned.1.call-start = ((), (), s32[]{:S(2)}) async-start(), calls=%async_computation.9 | async-start | bytes 262144 | tf_op jit(solution)/shard_map/psum | solution.py:42
  459.2 108.2 %all-gather.21.cloned.1.call-start = ((), (), s32[]{:S(2)}) async-start(), calls=%async_computation.10 | async-start | bytes 2228224 | tf_op jit(solution)/shard_map/all_gather | solution.py:45
  520.6 108.5 %all-reduce.23.cloned.1.call-start = ((), (), s32[]{:S(2)}) async-start(), calls=%async_computation.11 | async-start | bytes 262144 | tf_op jit(solution)/shard_map/psum | solution.py:42
  569.4 109.1 %all-gather.23.cloned.1.call-start = ((), (), s32[]{:S(2)}) async-start(), calls=%async_computation.12 | async-start | bytes 2228224 | tf_op jit(solution)/shard_map/all_gather | solution.py:45
  629.9 221.2 %copy-start.2 = (f32[256,128]{0,1:T(8,128)S(1)}, f32[256,128]{0,1:T(8,128)}, u32[]{:S(2)}) copy-start(f32[256,128]{0,1:T(8,128)} %all-reduce.23.cloned.1.call-done) | copy-start | bytes 393220
  631.6 108.4 %all-reduce.25.cloned.1.call-start = ((), (), s32[]{:S(2)}) async-start(), calls=%async_computation.13 | async-start | bytes 262144 | tf_op jit(solution)/shard_map/psum | solution.py:42
  680.4 109.3 %all-gather.25.cloned.1.call-start = ((), (), s32[]{:S(2)}) async-start(), calls=%async_computation.14 | async-start | bytes 2228224 | tf_op jit(solution)/shard_map/all_gather | solution.py:45
  740.1 111.1 %copy-start.5 = (f32[256,128]{0,1:T(8,128)S(1)}, f32[256,128]{0,1:T(8,128)}, u32[]{:S(2)}) copy-start(f32[256,128]{0,1:T(8,128)} %all-reduce.25.cloned.1.call-done) | copy-start | bytes 393220
  742.8 108.3 %all-reduce.27.cloned.1.call-start = ((), (), s32[]{:S(2)}) async-start(), calls=%async_computation.15 | async-start | bytes 262144 | tf_op jit(solution)/shard_map/psum | solution.py:42
  791.6 108.8 %all-gather.27.cloned.1.call-start = ((), (), s32[]{:S(2)}) async-start(), calls=%async_computation.16 | async-start | bytes 2228224 | tf_op jit(solution)/shard_map/all_gather | solution.py:45
  852.8 111.2 %all-reduce.29.cloned.1.call-start = ((), (), s32[]{:S(2)}) async-start(), calls=%async_computation.17 | async-start | bytes 262144 | tf_op jit(solution)/shard_map/psum | solution.py:42
  905.2 108.2 %all-gather.29.cloned.1.call-start = ((), (), s32[]{:S(2)}) async-start(), calls=%async_computation.18 | async-start | bytes 2228224 | tf_op jit(solution)/shard_map/all_gather | solution.py:45
  966.6 108.4 %all-reduce.31.cloned.1.call-start = ((), (), s32[]{:S(2)}) async-start(), calls=%async_computation.19 | async-start | bytes 262144 | tf_op jit(solution)/shard_map/psum | solution.py:42
  1015.4 109.1 %all-gather.31.cloned.1.call-start = ((), (), s32[]{:S(2)}) async-start(), calls=%async_computation.20 | async-start | bytes 2228224 | tf_op jit(solution)/shard_map/all_gather | solution.py:45
  1075.9 221.3 %copy-start.3 = (f32[256,128]{0,1:T(8,128)S(1)}, f32[256,128]{0,1:T(8,128)}, u32[]{:S(2)}) copy-start(f32[256,128]{0,1:T(8,128)} %all-reduce.31.cloned.1.call-done) | copy-start | bytes 393220
  1077.6 108.5 %all-reduce.33.cloned.1.call-start = ((), (), s32[]{:S(2)}) async-start(), calls=%async_computation.21 | async-start | bytes 262144 | tf_op jit(solution)/shard_map/psum | solution.py:42
  1126.4 109.3 %all-gather.33.cloned.1.call-start = ((), (), s32[]{:S(2)}) async-start(), calls=%async_computation.22 | async-start | bytes 2228224 | tf_op jit(solution)/shard_map/all_gather | solution.py:45
  1186.1 111.2 %copy-start.6 = (f32[256,128]{0,1:T(8,128)S(1)}, f32[256,128]{0,1:T(8,128)}, u32[]{:S(2)}) copy-start(f32[256,128]{0,1:T(8,128)} %all-reduce.33.cloned.1.call-done) | copy-start | bytes 393220
  1188.8 108.5 %all-reduce.35.cloned.1.call-start = ((), (), s32[]{:S(2)}) async-start(), calls=%async_computation.23 | async-start | bytes 262144 | tf_op jit(solution)/shard_map/psum | solution.py:42
  1237.6 109.0 %all-gather.35.cloned.1.call-start = ((), (), s32[]{:S(2)}) async-start(), calls=%async_computation.24 | async-start | bytes 2228224 | tf_op jit(solution)/shard_map/all_gather | solution.py:45
  1299.0 87.1 %reduce-scatter.2.cloned.1.call-start = ((), (), s32[]{:S(2)}) async-start(), calls=%async_computation.25 | async-start | bytes 1769472 | tf_op jit(solution)/shard_map/reduce_scatter | solution.py:100
  1311.7 36.0 %copy-start.12 = (s32[128]{0:T(128)S(1)}, s32[128]{0:T(128)}, u32[]{:S(2)}) copy-start(s32[128]{0:T(128)} %param.17) | copy-start | bytes 1540
  1353.4 1.4 copy-start.9
Sparse Core Ops, SparseCore 0:
  11.0 60.8 all-reduce.12
  74.6 46.7 all-gather.12
  124.2 58.6 all-reduce.14
  185.6 46.7 all-gather.14
  235.1 58.6 all-reduce.16
  296.7 46.7 all-gather.16
  346.3 58.6 all-reduce.18
  407.7 46.7 all-gather.18
  459.3 58.6 all-reduce.20
  520.7 46.7 all-gather.20
  570.3 58.6 all-reduce.22
  631.7 46.7 all-gather.22
  681.4 58.6 all-reduce.24
  742.9 46.7 all-gather.24
  792.4 58.6 all-reduce.26
  853.7 46.7 all-gather.26
  905.3 58.6 all-reduce.28
  966.7 46.7 all-gather.28
  1016.3 58.6 all-reduce.30
  1077.7 46.7 all-gather.30
  1127.4 58.6 all-reduce.32
  1188.9 46.7 all-gather.32
  1238.6 58.6 all-reduce.34
  1299.8 46.7 all-gather.34
  1354.9 31.0 reduce-scatter.1
where the time goes:
time: 1400 us; the launch traced here: 1390 us
  waiting for transfers between devices  1300 us (93%)
  other arithmetic  37.5 us (3%)
  matrix products  28 us (2%)
  local copies, waits for them, and re-layouts  17.3 us (1%)
  between operations  14.6 us (1%)
    psum x12, waiting for transfers between devices, reduce_rows(): return lax.psum(partial_value, 'col')  714 us
    all_gather x12, waiting for transfers between devices, spread_rows(): return lax.all_gather(values, 'row', axis=0, tiled=True)  551 us
    reduce_scatter x1, waiting for transfers between devices, body(): lax.psum_scatter(fold_pair(jnp.dot(z_flat, picked, preferred_element_type...  30 us
  transfers between devices with their start and end apart: 25, of which 25 were waited for; matrix products, arithmetic and copies ran while one was open for 1% of the time, Pallas kernels for 0%

commit v1 on v0

v1 whole, which is shorter than its diff:
```python
import jax
import jax.numpy as jnp
from jax import lax
from jax.sharding import PartitionSpec as P

NEUMANN = 3


def split_pair(values):
    upper = values.astype(jnp.bfloat16)
    lower = (values - lax.optimization_barrier(upper).astype(jnp.float32)).astype(jnp.bfloat16)
    return jnp.concatenate([upper, lower], axis=0)


def body(t_upper, t_old, inverses, forcing, x_old, offsets, starts, column_map, z_cols, acc):
    n_col = lax.axis_size("col")
    n_row = lax.axis_size("row")
    row_idx = lax.axis_index("row")
    col_idx = lax.axis_index("col")
    steps, row_block, width = forcing.shape
    col_block = t_upper.shape[2]
    old_cols = x_old.shape[0]
    full_rows = col_block * n_col
    group = width // n_col
    share = row_block // n_col

    inv_last = lax.all_gather(inverses[2], "col", axis=1, tiled=True)
    second = lax.all_gather(
        jnp.stack([t_upper[2], inverses[1]]), "col", axis=2, tiled=True
    )
    third = lax.all_gather(
        jnp.concatenate([t_upper[:2], inverses[:1]]), "col", axis=2, tiled=True
    )
    inv = {2: inv_last, 1: second[1], 0: third[2]}
    upper_of = {(1, 2): second[0], (0, 1): third[0], (0, 2): third[1]}

    def own_group(values):
        return lax.dynamic_slice_in_dim(values, col_idx * group, group, 0)

    my_starts = own_group(starts)[:, None]
    my_offsets = own_group(offsets)[:, None]

    old_rows = steps * full_rows + col_idx * old_cols + jnp.arange(old_cols, dtype=jnp.int32)
    old_vals = jnp.where(old_rows[:, None] < starts[None, :], x_old, jnp.zeros_like(x_old))
    old_part = lax.dot_general(
        old_vals,
        t_old.reshape(steps * row_block, old_cols),
        (((0,), (1,)), ((), ())),
        preferred_element_type=jnp.float32,
    )
    old_part = lax.all_to_all(
        old_part.reshape(n_col, group, steps * row_block), "col", 0, 0
    ).sum(0)
    forcing_t = lax.dynamic_slice_in_dim(
        forcing.reshape(steps * row_block, width), col_idx * group, group, 1
    ).T
    rhs_all = forcing_t - old_part

    def spread(values):
        pair = split_pair(values)
        got = lax.all_to_all(
            jnp.broadcast_to(pair[None], (n_row, *pair.shape)), "row", 0, 0
        )
        return jnp.swapaxes(got, 0, 1).reshape(2 * group, full_rows)

    def product(matrix, pairs):
        out = lax.dot_general(
            pairs, matrix, (((1,), (1,)), ((), ())), preferred_element_type=jnp.float32
        )
        return out[:group] + out[group:]

    whole = {}
    own = {}
    for step in reversed(range(steps)):
        rhs = rhs_all[:, step * row_block : (step + 1) * row_block]
        for later in range(step + 1, steps):
            rhs = rhs - product(upper_of[step, later], whole[later])
        term = product(inv[step], spread(rhs))
        total = term
        for extra in range(1, NEUMANN):
            term = product(inv[step], spread(term)) * my_offsets
            total = total + term
        rows = step * full_rows + row_idx * row_block + jnp.arange(row_block, dtype=jnp.int32)
        total = jnp.where(rows[None, :] < my_starts, total, jnp.zeros_like(total))
        own[step] = total
        whole[step] = spread(total)

    mine = jnp.stack([own[step] for step in range(steps)])
    solved = lax.all_gather(mine, "col", axis=1, tiled=True)
    solved = lax.dynamic_slice_in_dim(solved, col_idx * share, share, 2)
    solved = jnp.swapaxes(solved, 1, 2)

    send = jnp.stack([whole[step].reshape(2 * group, n_col, col_block) for step in range(steps)])
    send = jnp.transpose(send, (2, 0, 1, 3))
    got = lax.all_to_all(send, "col", 0, 0)
    got = got.reshape(n_col, steps, 2, group, col_block)
    got = jnp.transpose(got, (2, 0, 3, 1, 4)).reshape(2, width, steps * col_block)
    one_hot = (jnp.arange(width, dtype=jnp.int32)[:, None] == column_map[None, :]).astype(
        jnp.bfloat16
    )
    picked = [
        lax.dot_general(
            got[half], one_hot, (((0,), (0,)), ((), ())), preferred_element_type=jnp.float32
        ).astype(jnp.bfloat16)
        for half in range(2)
    ]
    picked = jnp.concatenate(picked, axis=1)
    z_rows = z_cols.shape[0]
    product_z = jnp.dot(
        z_cols.reshape(z_rows, steps * col_block), picked, preferred_element_type=jnp.float32
    )
    part = product_z[:, :width] + product_z[:, width:]
    part = lax.all_to_all(part.reshape(n_col, z_rows // n_col, width), "col", 0, 0).sum(0)
    return (solved, acc + part)


def solution(mesh):
    placed = (
        P(None, "row", "col"),
        P(None, "row", "col"),
        P(None, "row", "col"),
        P(None, "row", None),
        P("col", None),
        P(),
        P(),
        P(),
        P("row", None, "col"),
        P(("row", "col"), None),
    )
    return jax.shard_map(
        body,
        mesh=mesh,
        in_specs=placed,
        out_specs=(P(None, ("row", "col"), None), P(("row", "col"), None)),
        check_vma=False,
    )
```

time: 1400 us -> 283 us (0.20)
  waiting for transfers between devices: 1300 us -> 50.2 us
  blocking collectives: 0 us -> 109 us
  starting transfers between devices: 1.04 us -> 48.7 us
  other arithmetic: 37.5 us -> 3.19 us
    psum x12 -> x0, waiting for transfers between devices: 714 us -> none  [reduce_rows(): return lax.psum(partial_value, 'col')]
    all_gather x12 -> x3, waiting for transfers between devices: 551 us -> 0.06 us  [the longest x1 0.02 us: body(): inv_last = lax.all_gather(inverses[2], 'col', axis=1, tiled=True)]
    all_to_all x0 -> x7, blocking collectives: none -> 80.2 us  [spread(): lax.all_to_all(jnp.broadcast_to(pair[None], (n_row, *pair.shape)), 'row',...]
    all_to_all x0 -> x8, waiting for transfers between devices: none -> 50 us  [the longest x5 38 us: spread(): lax.all_to_all(jnp.broadcast_to(pair[None], (n_row, *pair.shape)), 'row',...]
    all_to_all x0 -> x8, starting transfers between devices: none -> 48.6 us  [the longest x1 19.2 us: body(): got = lax.all_to_all(send, 'col', 0, 0)]
    reduce_scatter x1 -> x0, waiting for transfers between devices: 30 us -> none  [body(): lax.psum_scatter(fold_pair(jnp.dot(z_flat, picked, preferred_element_type...]
    all_gather x0 -> x1, blocking collectives: none -> 28.4 us  [body(): solved = lax.all_gather(mine, 'col', axis=1, tiled=True)]
    dot_general x18 -> x16, matrix products: 28 us -> 30.9 us  [the longest x12 20.3 us: product(): lax.dot_general(pairs, matrix, (((1,), (1,)), ((), ())), preferred_elemen...]
  transfers between devices with their start and end apart: 25 -> 11, of which waited for: 25 -> 6; matrix products, arithmetic and copies ran while one was open for 1% -> 13% of each run, Pallas kernels for 0% -> 0%
where the time goes in v1:
time: 283 us; the launch traced here: 282 us
  blocking collectives  109 us (39%)
  waiting for transfers between devices  50.2 us (18%)
  starting transfers between devices  48.7 us (17%)
  matrix products  30.9 us (11%)
  local copies, waits for them, and re-layouts  25.7 us (9%)
  between operations  14.5 us (5%)
  other arithmetic  3.19 us (1%)
    all_to_all x7, blocking collectives, spread(): lax.all_to_all(jnp.broadcast_to(pair[None], (n_row, *pair.shape)), 'row',...  80.2 us
    all_to_all x5, waiting for transfers between devices, spread(): lax.all_to_all(jnp.broadcast_to(pair[None], (n_row, *pair.shape)), 'row',...  38 us
    all_gather x1, blocking collectives, body(): solved = lax.all_gather(mine, 'col', axis=1, tiled=True)  28.4 us
    dot_general x12, matrix products, product(): lax.dot_general(pairs, matrix, (((1,), (1,)), ((), ())), preferred_elemen...  20.3 us
    all_to_all x1, starting transfers between devices, body(): got = lax.all_to_all(send, 'col', 0, 0)  19.2 us
    all_to_all x5, starting transfers between devices, spread(): lax.all_to_all(jnp.broadcast_to(pair[None], (n_row, *pair.shape)), 'row',...  18.5 us
    unnamed x28, local copies, waits for them, and re-layouts  15 us
    all_to_all x1, waiting for transfers between devices, body(): lax.all_to_all(old_part.reshape(n_col, group, steps * row_block), 'col',...  12 us
  transfers between devices with their start and end apart: 11, of which 6 were waited for; matrix products, arithmetic and copies ran while one was open for 13% of the time, Pallas kernels for 0%

profile of v1, /device:TPU:1, one launch (start us, length us, event | category | flops | bytes accessed | tf_op | source)
XLA Modules:
  0.0 281.8 jit_solution(16074638776969399112)
XLA Ops:
  7.2 1.9 fusion.55
  9.3 0.8 pad_maximum_fusion.1
  10.3 1.0 pad_maximum_fusion
  11.9 4.8 %fusion.56 = f32[8,16,768]{2,1,0:T(8,128)} fusion(bf16[8,16,3072]{2,1,0:T(8,128)(2,1)S(1)} %bitcast.114, bf16[768,3072,1]{1,0,2:T(8,128)(2,1)} %bitcast.111), kind=kOutput, calls=%fused_computation.110 | convolution fusion | flops 603979776 | bytes 5898240 | tf_op jit(solution)/shard_map/dot_general | solution.py:45
  16.7 6.0 %all-to-all-start = ((f32[8,16,768]{2,1,0:T(8,128)}), f32[8,16,768]{2,1,0:T(8,128)S(1)}, u32[]{:S(2)}, u32[]{:S(2)}) async-start(f32[8,16,768]{2,1,0:T(8,128)} %fusion.56), calls=%async_computation | async-start | bytes 786432 | tf_op jit(solution)/shard_map/all_to_all | solution.py:51
  22.9 12.0 %all-to-all-done = f32[8,16,768]{2,1,0:T(8,128)S(1)} async-done(((f32[8,16,768]{2,1,0:T(8,128)}), f32[8,16,768]{2,1,0:T(8,128)S(1)}, u32[]{:S(2)}, u32[]{:S(2)}) %all-to-all-start) | async-done | bytes 393248 | tf_op jit(solution)/shard_map/all_to_all | solution.py:51
  35.1 14.9 %all_to_all.75 = bf16[16,32,256]{2,1,0:T(8,128)(2,1)S(1)} all-to-all(bf16[16,32,256]{2,1,0:T(8,128)(2,1)S(1)} %broadcast_in_dim.27), channel_id=1, replica_groups=mesh['row'=16,'col'=8] {'row'}, dimensions={0} | all-to-all | bytes 524288 | tf_op jit(solution)/shard_map/all_to_all | solution.py:61
  50.1 2.5 fusion.7
  52.6 0.7 broadcast_in_dim.28
  53.4 3.6 %all-to-all-start.2 = ((bf16[16,32,256]{2,1,0:T(8,128)(2,1)}), bf16[16,32,256]{2,1,0:T(8,128)(2,1)S(1)}, u32[]{:S(2)}, u32[]{:S(2)}) async-start(bf16[16,32,256]{2,1,0:T(8,128)(2,1)} %broadcast_in_dim.28), calls=%async_computation.2 | async-start | bytes 524288 | tf_op jit(solution)/shard_map/all_to_all | solution.py:61
  57.0 7.4 %all-to-all-done.2 = bf16[16,32,256]{2,1,0:T(8,128)(2,1)S(1)} async-done(((bf16[16,32,256]{2,1,0:T(8,128)(2,1)}), bf16[16,32,256]{2,1,0:T(8,128)(2,1)S(1)}, u32[]{:S(2)}, u32[]{:S(2)}) %all-to-all-start.2) | async-done | bytes 262176 | tf_op jit(solution)/shard_map/all_to_all | solution.py:61
  64.4 0.7 fusion.5
  65.3 0.8 broadcast_in_dim.29
  66.0 3.6 %all-to-all-start.3 = ((bf16[16,32,256]{2,1,0:T(8,128)(2,1)}), bf16[16,32,256]{2,1,0:T(8,128)(2,1)S(1)}, u32[]{:S(2)}, u32[]{:S(2)}) async-start(bf16[16,32,256]{2,1,0:T(8,128)(2,1)} %broadcast_in_dim.29), calls=%async_computation.3 | async-start | bytes 524288 | tf_op jit(solution)/shard_map/all_to_all | solution.py:61
  69.8 7.2 %all-to-all-done.3 = bf16[16,32,256]{2,1,0:T(8,128)(2,1)S(1)} async-done(((bf16[16,32,256]{2,1,0:T(8,128)(2,1)}), bf16[16,32,256]{2,1,0:T(8,128)(2,1)S(1)}, u32[]{:S(2)}, u32[]{:S(2)}) %all-to-all-start.3) | async-done | bytes 262176 | tf_op jit(solution)/shard_map/all_to_all | solution.py:61
  77.0 0.7 fusion.3
  77.9 10.9 %all_to_all.76 = bf16[16,32,256]{2,1,0:T(8,128)(2,1)S(1)} all-to-all(bf16[16,32,256]{2,1,0:T(8,128)(2,1)S(1)} %broadcast_in_dim.30), channel_id=1, replica_groups=mesh['row'=16,'col'=8] {'row'}, dimensions={0} | all-to-all | bytes 524288 | tf_op jit(solution)/shard_map/all_to_all | solution.py:61
  88.8 2.3 fusion.2
  91.2 10.7 %all_to_all.77 = bf16[16,32,256]{2,1,0:T(8,128)(2,1)S(1)} all-to-all(bf16[16,32,256]{2,1,0:T(8,128)(2,1)S(1)} %broadcast_in_dim.31), channel_id=1, replica_groups=mesh['row'=16,'col'=8] {'row'}, dimensions={0} | all-to-all | bytes 524288 | tf_op jit(solution)/shard_map/all_to_all | solution.py:61
  101.9 2.5 fusion.11
  104.5 11.0 %all_to_all.78 = bf16[16,32,256]{2,1,0:T(8,128)(2,1)S(1)} all-to-all(bf16[16,32,256]{2,1,0:T(8,128)(2,1)S(1)} %broadcast_in_dim.32), channel_id=1, replica_groups=mesh['row'=16,'col'=8] {'row'}, dimensions={0} | all-to-all | bytes 524288 | tf_op jit(solution)/shard_map/all_to_all | solution.py:61
  115.5 0.7 fusion.10
  116.3 0.8 broadcast_in_dim.33
  117.1 3.8 %all-to-all-start.7 = ((bf16[16,32,256]{2,1,0:T(8,128)(2,1)}), bf16[16,32,256]{2,1,0:T(8,128)(2,1)S(1)}, u32[]{:S(2)}, u32[]{:S(2)}) async-start(bf16[16,32,256]{2,1,0:T(8,128)(2,1)} %broadcast_in_dim.33), calls=%async_computation.7 | async-start | bytes 524288 | tf_op jit(solution)/shard_map/all_to_all | solution.py:61
  120.9 7.3 %all-to-all-done.7 = bf16[16,32,256]{2,1,0:T(8,128)(2,1)S(1)} async-done(((bf16[16,32,256]{2,1,0:T(8,128)(2,1)}), bf16[16,32,256]{2,1,0:T(8,128)(2,1)S(1)}, u32[]{:S(2)}, u32[]{:S(2)}) %all-to-all-start.7) | async-done | bytes 262176 | tf_op jit(solution)/shard_map/all_to_all | solution.py:61
  128.2 2.3 fusion.9
  130.7 10.5 %all_to_all.79 = bf16[16,32,256]{2,1,0:T(8,128)(2,1)S(1)} all-to-all(bf16[16,32,256]{2,1,0:T(8,128)(2,1)S(1)} %broadcast_in_dim.34), channel_id=1, replica_groups=mesh['row'=16,'col'=8] {'row'}, dimensions={0} | all-to-all | bytes 524288 | tf_op jit(solution)/shard_map/all_to_all | solution.py:61
  141.3 2.5 fusion
  143.7 2.3 fusion.1
  146.1 10.5 %all_to_all.80 = bf16[16,32,256]{2,1,0:T(8,128)(2,1)S(1)} all-to-all(bf16[16,32,256]{2,1,0:T(8,128)(2,1)S(1)} %broadcast_in_dim.35), channel_id=1, replica_groups=mesh['row'=16,'col'=8] {'row'}, dimensions={0} | all-to-all | bytes 524288 | tf_op jit(solution)/shard_map/all_to_all | solution.py:61
  156.7 0.7 fusion.14
  157.5 11.7 %all_to_all.81 = bf16[16,32,256]{2,1,0:T(8,128)(2,1)S(1)} all-to-all(bf16[16,32,256]{2,1,0:T(8,128)(2,1)S(1)} %broadcast_in_dim.36), channel_id=1, replica_groups=mesh['row'=16,'col'=8] {'row'}, dimensions={0} | all-to-all | bytes 524288 | tf_op jit(solution)/shard_map/all_to_all | solution.py:61
  169.2 0.7 fusion.13
  170.1 0.7 broadcast_in_dim.37
  170.8 3.7 %all-to-all-start.11 = ((bf16[16,32,256]{2,1,0:T(8,128)(2,1)}), bf16[16,32,256]{2,1,0:T(8,128)(2,1)S(1)}, u32[]{:S(2)}, u32[]{:S(2)}) async-start(bf16[16,32,256]{2,1,0:T(8,128)(2,1)} %broadcast_in_dim.37), calls=%async_computation.11 | async-start | bytes 524288 | tf_op jit(solution)/shard_map/all_to_all | solution.py:61
  174.5 8.3 %all-to-all-done.11 = bf16[16,32,256]{2,1,0:T(8,128)(2,1)S(1)} async-done(((bf16[16,32,256]{2,1,0:T(8,128)(2,1)}), bf16[16,32,256]{2,1,0:T(8,128)(2,1)S(1)}, u32[]{:S(2)}, u32[]{:S(2)}) %all-to-all-start.11) | async-done | bytes 262176 | tf_op jit(solution)/shard_map/all_to_all | solution.py:61
  182.8 2.3 fusion.12
  186.0 3.8 %all-to-all-start.12 = ((bf16[16,32,256]{2,1,0:T(8,128)(2,1)}), bf16[16,32,256]{2,1,0:T(8,128)(2,1)S(1)}, u32[]{:S(2)}, u32[]{:S(2)}) async-start(bf16[16,32,256]{2,1,0:T(8,128)(2,1)} %broadcast_in_dim.38), calls=%async_computation.12 | async-start | bytes 524288 | tf_op jit(solution)/shard_map/all_to_all | solution.py:61
  190.3 7.8 %all-to-all-done.12 = bf16[16,32,256]{2,1,0:T(8,128)(2,1)S(1)} async-done(((bf16[16,32,256]{2,1,0:T(8,128)(2,1)}), bf16[16,32,256]{2,1,0:T(8,128)(2,1)S(1)}, u32[]{:S(2)}, u32[]{:S(2)}) %all-to-all-start.12) | async-done | bytes 262176 | tf_op jit(solution)/shard_map/all_to_all | solution.py:61
  198.4 1.1 copy.36
  199.6 19.2 %all-to-all-start.13 = ((bf16[8,3,32,512]{3,2,1,0:T(8,128)(2,1)}), bf16[8,3,32,512]{3,2,1,0:T(8,128)(2,1)S(1)}, u32[]{:S(2)}, u32[]{:S(2)}) async-start(bf16[8,3,32,512]{3,2,1,0:T(8,128)(2,1)} %copy.36), calls=%async_computation.13 | async-start | bytes 1572864 | tf_op jit(solution)/shard_map/all_to_all | solution.py:95
  218.7 12.6 %copy.38 = bf16[3072,3,512]{0,2,1:T(8,128)(2,1)} copy(bf16[3072,3,512]{2,0,1:T(8,128)(2,1)} %param.18) | data formatting | bytes 18874368 | tf_op args[8]
  233.3 5.2 %convolution_bitcast_fusion = f32[3072,256]{0,1:T(8,128)S(1)} fusion(bf16[3072,1536]{0,1:T(8,128)(2,1)} %bitcast.112, bf16[1536,128]{0,1:T(8,128)(2,1)S(1)} %convolution_convert_fusion, bf16[1536,128]{0,1:T(8,128)(2,1)S(1)} %convolution_convert_fusion.1), kind=kOutput, calls=%fused_computation | convolution fusion | flops 2417491968 | bytes 13369344 | tf_op jit(solution)/shard_map/dot_general | solution.py:109
  238.7 1.3 copy.62
  240.0 5.0 %all-to-all-start.14 = ((f32[8,384,128]{1,2,0:T(8,128)}), f32[8,384,128]{1,2,0:T(8,128)S(1)}, u32[]{:S(2)}, u32[]{:S(2)}) async-start(f32[8,384,128]{1,2,0:T(8,128)} %bitcast.108), calls=%async_computation.14 | async-start | bytes 3145728 | tf_op jit(solution)/shard_map/all_to_all | solution.py:113
  245.1 28.4 %all_gather.15 = f32[3,128,256]{2,1,0:T(8,128)S(1)} all-gather(f32[3,16,256]{2,1,0:T(8,128)S(1)} %pad_maximum_fusion.2), channel_id=1, replica_groups=mesh['row'=16,'col'=8] {'col'}, dimensions={1}, use_global_device_ids=true | all-gather | bytes 442368 | tf_op jit(solution)/shard_map/all_gather | solution.py:89
  273.6 0.7 copy.42
  274.4 0.8 copy.43
  (121 shorter events, 6.4 us)
Async XLA Ops:
  7.2 15.5 %copy-start = (f32[3,256,128]{2,1,0:T(8,128)S(1)}, f32[3,256,128]{2,1,0:T(8,128)}, u32[]{:S(2)}) copy-start(f32[3,256,128]{2,1,0:T(8,128)} %param.13) | copy-start | bytes 1179652
  7.2 2.1 slice-start
  7.2 42.9 %all-gather.9.cloned.1.call-start = ((), (), s32[]{:S(2)}) async-start(), calls=%async_computation.17 | async-start | bytes 2359296 | tf_op jit(solution)/shard_map/all_gather | solution.py:27
  9.2 1.1 slice-start.1
  9.2 79.6 %all-gather.5.cloned.1.call-start = ((), (), s32[]{:S(2)}) async-start(), calls=%async_computation.15 | async-start | bytes 4718592 | tf_op jit(solution)/shard_map/all_gather | solution.py:28
  10.1 1.2 copy-start.3
  10.1 131.1 %all-gather.7.cloned.1.call-start = ((), (), s32[]{:S(2)}) async-start(), calls=%async_computation.16 | async-start | bytes 7077888 | tf_op jit(solution)/shard_map/all_gather | solution.py:31
  10.2 1.4 copy-start.6
  16.7 18.3 %all-to-all-start = ((f32[8,16,768]{2,1,0:T(8,128)}), f32[8,16,768]{2,1,0:T(8,128)S(1)}, u32[]{:S(2)}, u32[]{:S(2)}) async-start(f32[8,16,768]{2,1,0:T(8,128)} %fusion.56), calls=%async_computation | async-start | bytes 786432 | tf_op jit(solution)/shard_map/all_to_all | solution.py:51
  35.1 21.8 %copy-start.9 = (f32[128]{0:T(128)S(1)}, f32[128]{0:T(128)}, u32[]{:S(2)}) copy-start(f32[128]{0:T(128)} %param.15) | copy-start | bytes 1540
  50.1 14.3 %copy-start.2 = (bf16[1,256,4096]{2,1,0:T(8,128)(2,1)S(1)}, bf16[1,256,4096]{2,1,0:T(8,128)(2,1)}, u32[]{:S(2)}) copy-start(bf16[1,256,4096]{2,1,0:T(8,128)(2,1)} %all-gather.9.cloned.1.call-done) | copy-start | bytes 6291460
  53.4 11.0 %all-to-all-start.2 = ((bf16[16,32,256]{2,1,0:T(8,128)(2,1)}), bf16[16,32,256]{2,1,0:T(8,128)(2,1)S(1)}, u32[]{:S(2)}, u32[]{:S(2)}) async-start(bf16[16,32,256]{2,1,0:T(8,128)(2,1)} %broadcast_in_dim.28), calls=%async_computation.2 | async-start | bytes 524288 | tf_op jit(solution)/shard_map/all_to_all | solution.py:61
  66.0 11.0 %all-to-all-start.3 = ((bf16[16,32,256]{2,1,0:T(8,128)(2,1)}), bf16[16,32,256]{2,1,0:T(8,128)(2,1)S(1)}, u32[]{:S(2)}, u32[]{:S(2)}) async-start(bf16[16,32,256]{2,1,0:T(8,128)(2,1)} %broadcast_in_dim.29), calls=%async_computation.3 | async-start | bytes 524288 | tf_op jit(solution)/shard_map/all_to_all | solution.py:61
  101.9 13.6 %copy-start.8 = (bf16[2,256,4096]{2,1,0:T(8,128)(2,1)S(1)}, bf16[2,256,4096]{2,1,0:T(8,128)(2,1)}, u32[]{:S(2)}) copy-start(bf16[2,256,4096]{2,1,0:T(8,128)(2,1)} %all-gather.5.cloned.1.call-done) | copy-start | bytes 12582916
  117.1 11.1 %all-to-all-start.7 = ((bf16[16,32,256]{2,1,0:T(8,128)(2,1)}), bf16[16,32,256]{2,1,0:T(8,128)(2,1)S(1)}, u32[]{:S(2)}, u32[]{:S(2)}) async-start(bf16[16,32,256]{2,1,0:T(8,128)(2,1)} %broadcast_in_dim.33), calls=%async_computation.7 | async-start | bytes 524288 | tf_op jit(solution)/shard_map/all_to_all | solution.py:61
  141.2 15.4 %copy-start.7 = (bf16[3,256,4096]{2,1,0:T(8,128)(2,1)S(1)}, bf16[3,256,4096]{2,1,0:T(8,128)(2,1)}, u32[]{:S(2)}) copy-start(bf16[3,256,4096]{2,1,0:T(8,128)(2,1)} %all-gather.7.cloned.1.call-done) | copy-start | bytes 18874372
  170.8 12.0 %all-to-all-start.11 = ((bf16[16,32,256]{2,1,0:T(8,128)(2,1)}), bf16[16,32,256]{2,1,0:T(8,128)(2,1)S(1)}, u32[]{:S(2)}, u32[]{:S(2)}) async-start(bf16[16,32,256]{2,1,0:T(8,128)(2,1)} %broadcast_in_dim.37), calls=%async_computation.11 | async-start | bytes 524288 | tf_op jit(solution)/shard_map/all_to_all | solution.py:61
  186.0 12.1 %all-to-all-start.12 = ((bf16[16,32,256]{2,1,0:T(8,128)(2,1)}), bf16[16,32,256]{2,1,0:T(8,128)(2,1)S(1)}, u32[]{:S(2)}, u32[]{:S(2)}) async-start(bf16[16,32,256]{2,1,0:T(8,128)(2,1)} %broadcast_in_dim.38), calls=%async_computation.12 | async-start | bytes 524288 | tf_op jit(solution)/shard_map/all_to_all | solution.py:61
  199.6 31.8 %all-to-all-start.13 = ((bf16[8,3,32,512]{3,2,1,0:T(8,128)(2,1)}), bf16[8,3,32,512]{3,2,1,0:T(8,128)(2,1)S(1)}, u32[]{:S(2)}, u32[]{:S(2)}) async-start(bf16[8,3,32,512]{3,2,1,0:T(8,128)(2,1)} %copy.36), calls=%async_computation.13 | async-start | bytes 1572864 | tf_op jit(solution)/shard_map/all_to_all | solution.py:95
  232.0 0.7 copy-start.5
  240.0 5.0 %copy-start.4 = (f32[384,128]{1,0:T(8,128)S(1)}, f32[384,128]{1,0:T(8,128)}, u32[]{:S(2)}) copy-start(f32[384,128]{1,0:T(8,128)} %param.19) | copy-start | bytes 589828
  240.0 34.3 %all-to-all-start.14 = ((f32[8,384,128]{1,2,0:T(8,128)}), f32[8,384,128]{1,2,0:T(8,128)S(1)}, u32[]{:S(2)}, u32[]{:S(2)}) async-start(f32[8,384,128]{1,2,0:T(8,128)} %bitcast.108), calls=%async_computation.14 | async-start | bytes 3145728 | tf_op jit(solution)/shard_map/all_to_all | solution.py:113
  244.9 30.3 %copy-start.1 = (f32[3,256,128]{2,1,0:T(8,128)S(1)}, f32[3,256,128]{2,1,0:T(8,128)}, u32[]{:S(2)}) copy-start(f32[3,256,128]{2,1,0:T(8,128)} %param.13) | copy-start | bytes 1179652
Sparse Core Ops, SparseCore 0:
  9.7 31.4 all-gather.8
  42.9 32.9 all-gather.4
  77.5 40.7 all-gather.6

commit v2 on v1

v2 whole, which is shorter than its diff:
```python
import functools

import jax
import jax.numpy as jnp
from jax import lax
from jax.experimental import pallas as pl
from jax.experimental.pallas import tpu as pltpu
from jax.sharding import PartitionSpec as P

NEUMANN = 3
F32 = jnp.float32
BF16 = jnp.bfloat16
VMEM_LIMIT = 16 << 20


def rows_product(pairs_ref, rows_ref, which):
    blocks, _, width = pairs_ref.shape
    per = blocks // rows_ref.shape[0]
    out = None
    for block in range(blocks):
        first = (block % per) * width
        part = lax.dot_general(
            pairs_ref[block],
            rows_ref[block // per, which, :, first : first + width],
            (((1,), (1,)), ((), ())),
            preferred_element_type=F32,
        )
        out = part if out is None else out + part
    half = out.shape[0] // 2
    return out[:half] + out[half:]


def pair_of(values):
    upper = values.astype(BF16)
    lower = (values - upper.astype(F32)).astype(BF16)
    return jnp.concatenate([upper, lower], axis=0)


def send_to_all(send_ref, pair):
    for peer in range(send_ref.shape[0]):
        send_ref[peer] = pair


def first_kernel(step, parts_ref, forcing_ref, rhs_ref, send_ref):
    width = send_ref.shape[2]
    rhs = forcing_ref[...] - jnp.sum(parts_ref[...], axis=0)
    rhs_ref[...] = rhs
    send_to_all(send_ref, pair_of(rhs[:, step * width : (step + 1) * width]))


def rhs_kernel(step, uses, *refs):
    rhs_ref, send_ref = refs[-2:]
    width = send_ref.shape[2]
    rhs = rhs_ref[:, step * width : (step + 1) * width]
    for k, which in enumerate(uses):
        rhs = rhs - rows_product(refs[2 * k], refs[2 * k + 1], which)
    send_to_all(send_ref, pair_of(rhs))


def first_term_kernel(which, pairs_ref, rows_ref, send_ref, total_ref):
    term = rows_product(pairs_ref, rows_ref, which)
    total_ref[...] = term
    send_to_all(send_ref, pair_of(term))


def next_term_kernel(which, pairs_ref, rows_ref, scale_ref, old_ref, send_ref, total_ref):
    term = rows_product(pairs_ref, rows_ref, which) * scale_ref[...]
    total_ref[...] = old_ref[...] + term
    send_to_all(send_ref, pair_of(term))


def last_term_kernel(which, pairs_ref, rows_ref, scale_ref, old_ref, limit_ref, send_ref, own_ref):
    term = rows_product(pairs_ref, rows_ref, which) * scale_ref[...]
    total = old_ref[...] + term
    row = lax.broadcasted_iota(jnp.int32, total.shape, 1)
    pair = pair_of(jnp.where(row < limit_ref[...], total, 0.0))
    own_ref[...] = pair
    send_to_all(send_ref, pair)


def columns_kernel(steps, *refs):
    send_ref = refs[-1]
    n_col = send_ref.shape[0]
    lanes = 128
    for step in range(steps):
        whole_ref, own_ref = refs[2 * step], refs[2 * step + 1]
        blocks, _, width = whole_ref.shape
        per = blocks // n_col
        share = width // n_col
        for col in range(n_col):
            for k in range(per):
                send_ref[col, step, :, k * width : (k + 1) * width] = whole_ref[col * per + k]
            first = col * share // lanes * lanes
            send_ref[col, step, :, per * width :] = own_ref[:, first : first + lanes]


def z_first_kernel(place_ref, got_ref, hot_ref, z_ref, out_ref, picked_ref):
    steps, _, depth = z_ref.shape

    @pl.when(pl.program_id(0) == 0)
    def _():
        for step in range(steps):
            whole = jnp.concatenate(
                [got_ref[k, step, :, :depth] for k in range(got_ref.shape[0])], axis=0
            )
            picked_ref[step] = lax.dot_general(
                whole, hot_ref[...], (((0,), (0,)), ((), ())), preferred_element_type=F32
            ).astype(BF16)

    z_tile(z_ref, picked_ref, out_ref)


def z_next_kernel(place_ref, picked_ref, z_ref, out_ref):
    z_tile(z_ref, picked_ref, out_ref)


def z_tile(z_ref, picked_ref, out_ref):
    out = None
    for step in range(z_ref.shape[0]):
        part = jnp.dot(z_ref[step], picked_ref[step], preferred_element_type=F32)
        out = part if out is None else out + part
    half = out.shape[1] // 2
    out_ref[0] = out[:, :half] + out[:, half:]


def call(kernel, outs, *args, flops=0):
    size = sum(a.size * a.dtype.itemsize for a in args)
    return pl.pallas_call(
        kernel,
        out_shape=outs,
        in_specs=[pl.BlockSpec(memory_space=pltpu.VMEM)] * len(args),
        out_specs=[pl.BlockSpec(memory_space=pltpu.VMEM)] * len(outs),
        compiler_params=pltpu.CompilerParams(vmem_limit_bytes=VMEM_LIMIT),
        cost_estimate=pl.CostEstimate(flops=flops, bytes_accessed=size, transcendentals=0),
    )(*args)


def in_vmem(values):
    return pltpu.with_memory_space_constraint(values, pltpu.VMEM)


def body(t_upper, t_old, inverses, forcing, x_old, offsets, starts, column_map, z_cols, acc):
    n_col = lax.axis_size("col")
    n_row = lax.axis_size("row")
    row_idx = lax.axis_index("row")
    col_idx = lax.axis_index("col")
    steps, row_block, width = forcing.shape
    col_block = t_upper.shape[2]
    old_cols = x_old.shape[0]
    full_rows = col_block * n_col
    group = width // n_col
    share = row_block // n_col
    shape = jax.ShapeDtypeStruct

    gather = functools.partial(lax.all_gather, axis_name="col", axis=0)
    set_a = gather(inverses[2:3])
    set_b = gather(jnp.concatenate([t_upper[2:3], inverses[1:2]]))
    set_c = gather(jnp.concatenate([t_upper[:2], inverses[:1]]))
    inv = {2: (set_a, 0), 1: (set_b, 1), 0: (set_c, 2)}
    upper_of = {(1, 2): (set_b, 0), (0, 1): (set_c, 0), (0, 2): (set_c, 1)}

    def own_group(values):
        return lax.dynamic_slice_in_dim(values, col_idx * group, group, 0)

    my_starts = own_group(starts)[:, None]
    my_offsets = own_group(offsets)[:, None]

    old_rows = steps * full_rows + col_idx * old_cols + jnp.arange(old_cols, dtype=jnp.int32)
    old_vals = jnp.where(old_rows[:, None] < starts[None, :], x_old, jnp.zeros_like(x_old))
    old_part = lax.dot_general(
        old_vals,
        t_old.reshape(steps * row_block, old_cols),
        (((0,), (1,)), ((), ())),
        preferred_element_type=F32,
    )
    old_part = lax.all_to_all(old_part.reshape(n_col, group, steps * row_block), "col", 0, 0)
    forcing_t = lax.dynamic_slice_in_dim(
        forcing.reshape(steps * row_block, width), col_idx * group, group, 1
    ).T

    send_shape = shape((n_row, 2 * group, row_block), BF16)
    vec_shape = shape((group, row_block), F32)
    own_shape = shape((2 * group, row_block), BF16)
    flops = 4 * group * row_block * full_rows

    def spread(send):
        return lax.all_to_all(send, "row", 0, 0)

    rhs_all, send = call(
        functools.partial(first_kernel, steps - 1),
        [shape((group, steps * row_block), F32), send_shape],
        old_part,
        forcing_t,
    )
    whole = {}
    own = {}
    for step in reversed(range(steps)):
        if step < steps - 1:
            args = []
            uses = []
            for later in range(step + 1, steps):
                rows, which = upper_of[step, later]
                args += [whole[later], in_vmem(rows)]
                uses.append(which)
            (send,) = call(
                functools.partial(rhs_kernel, step, uses),
                [send_shape],
                *args,
                rhs_all,
                flops=flops * len(uses),
            )
        rows, which = inv[step]
        rows = in_vmem(rows)
        send, total = call(
            functools.partial(first_term_kernel, which),
            [send_shape, vec_shape],
            spread(send),
            rows,
            flops=flops,
        )
        for extra in range(1, NEUMANN):
            if extra < NEUMANN - 1:
                send, total = call(
                    functools.partial(next_term_kernel, which),
                    [send_shape, vec_shape],
                    spread(send),
                    rows,
                    my_offsets,
                    total,
                    flops=flops,
                )
            else:
                limit = my_starts - (step * full_rows + row_idx * row_block)
                send, own[step] = call(
                    functools.partial(last_term_kernel, which),
                    [send_shape, own_shape],
                    spread(send),
                    rows,
                    my_offsets,
                    total,
                    limit,
                    flops=flops,
                )
        whole[step] = spread(send)

    lanes = 128
    args = []
    for step in range(steps):
        args += [whole[step], own[step]]
    (send,) = call(
        functools.partial(columns_kernel, steps),
        [shape((n_col, steps, 2 * group, col_block + lanes), BF16)],
        *args,
    )
    got = lax.all_to_all(send, "col", 0, 0)

    mine = lax.dynamic_slice_in_dim(
        got, col_block + col_idx % (lanes // share) * share, share, 3
    ).astype(F32)
    mine = mine[:, :, :group] + mine[:, :, group:]
    solved = jnp.transpose(mine, (1, 3, 0, 2)).reshape(steps, share, width)

    order = jnp.arange(2 * width, dtype=jnp.int32)
    half_of = order // group % 2
    value_of = order // (2 * group) * group + order % group
    target = jnp.concatenate([column_map, column_map + width])
    hot = ((half_of * width + value_of)[:, None] == target[None, :]).astype(BF16)

    z_rows = z_cols.shape[0]
    z_block = z_rows // n_col
    z_t = jnp.transpose(z_cols, (1, 0, 2))
    core = col_idx % 2
    z_spec = pl.BlockSpec((steps, z_block, col_block), lambda i, place: (0, 2 * i + place[0], 0))
    out_spec = pl.BlockSpec((1, z_block, width), lambda i, place: (i, 0, 0))
    z_params = pltpu.CompilerParams(vmem_limit_bytes=VMEM_LIMIT)
    cost = pl.CostEstimate(
        flops=2 * z_rows * steps * col_block * width,
        bytes_accessed=z_cols.size,
        transcendentals=0,
    )
    part_shape = shape((n_col // 2, z_block, width), F32)
    picked_shape = shape((steps, col_block, 2 * width), BF16)

    def fixed(array_shape):
        return pl.BlockSpec(array_shape, lambda i, place: (0,) * len(array_shape))

    theirs, picked = pl.pallas_call(
        z_first_kernel,
        out_shape=[part_shape, picked_shape],
        grid_spec=pltpu.PrefetchScalarGridSpec(
            num_scalar_prefetch=1,
            grid=(n_col // 2,),
            in_specs=[fixed(got.shape), fixed(hot.shape), z_spec],
            out_specs=[out_spec, fixed(picked_shape.shape)],
        ),
        compiler_params=z_params,
        cost_estimate=cost,
    )((1 - core)[None], got, hot, z_t)
    swapped = lax.ppermute(theirs, "col", [(i, i ^ 1) for i in range(n_col)])
    (ours,) = pl.pallas_call(
        z_next_kernel,
        out_shape=[part_shape],
        grid_spec=pltpu.PrefetchScalarGridSpec(
            num_scalar_prefetch=1,
            grid=(n_col // 2,),
            in_specs=[fixed(picked_shape.shape), z_spec],
            out_specs=[out_spec],
        ),
        compiler_params=z_params,
        cost_estimate=cost,
    )(core[None], picked, z_t)
    part = lax.all_to_all(
        ours + swapped,
        "col",
        0,
        0,
        axis_index_groups=[list(range(c, n_col, 2)) for c in range(2)],
    )
    return (solved, acc + part.sum(0))


def solution(mesh):
    placed = (
        P(None, "row", "col"),
        P(None, "row", "col"),
        P(None, "row", "col"),
        P(None, "row", None),
        P("col", None),
        P(),
        P(),
        P(),
        P("row", None, "col"),
        P(("row", "col"), None),
    )
    return jax.shard_map(
        body,
        mesh=mesh,
        in_specs=placed,
        out_specs=(P(None, ("row", "col"), None), P(("row", "col"), None)),
        check_vma=False,
    )
```

time: 283 us -> 272 us (0.961)
  matrix products: 30.9 us -> 4.83 us
  Pallas kernels: 0 us -> 17.5 us
  waiting for transfers between devices: 50.2 us -> 67.2 us
  blocking collectives: 109 us -> 92.8 us
  starting transfers between devices: 48.7 us -> 44.9 us
    all_gather x1 -> x0, blocking collectives: 28.4 us -> none  [body(): solved = lax.all_gather(mine, 'col', axis=1, tiled=True)]
    dot_general x15 -> x0, matrix products: 26.1 us -> none  [the longest x12 20.3 us: product(): lax.dot_general(pairs, matrix, (((1,), (1,)), ((), ())), preferred_elemen...]
    pallas_call x0 -> x15, Pallas kernels: none -> 17.5 us  [the longest x13 12.6 us: call(): pl.pallas_call(kernel, out_shape=outs, in_specs=[pl.BlockSpec(memory_spac...]
    all_to_all x1, waiting for transfers between devices: 0.01 us -> 14.2 us  [body(): got = lax.all_to_all(send, 'col', 0, 0)]
    all_to_all x7 -> x8, blocking collectives: 80.2 us -> 92.8 us  [spread(): return lax.all_to_all(send, 'row', 0, 0)]
    unnamed x28 -> x37, local copies, waits for them, and re-layouts: 15 us -> 21.8 us
    all_to_all x6 -> x5, starting transfers between devices: 23.4 us -> 18.3 us  [the longest x4 14.9 us: spread(): return lax.all_to_all(send, 'row', 0, 0)]
    broadcast_in_dim x12 -> x2, local copies, waits for them, and re-layouts: 3.83 us -> 0.17 us  [body(): my_offsets = own_group(offsets)[:, None]]
  transfers between devices with their start and end apart: 11 -> 11, of which waited for: 6 -> 7; matrix products, arithmetic and copies ran while one was open for 13% -> 4% of each run, Pallas kernels for 0% -> 4%
where the time goes in v2:
time: 272 us; the launch traced here: 271 us
  blocking collectives  92.8 us (34%)
  waiting for transfers between devices  67.2 us (25%)
  starting transfers between devices  44.9 us (17%)
  local copies, waits for them, and re-layouts  25.4 us (9%)
  Pallas kernels  17.5 us (6%)
  between operations  14.1 us (5%)
  matrix products  4.83 us (2%)
  other arithmetic  4.13 us (2%)
    all_to_all x8, blocking collectives, spread(): return lax.all_to_all(send, 'row', 0, 0)  92.8 us
    all_to_all x4, waiting for transfers between devices, spread(): return lax.all_to_all(send, 'row', 0, 0)  29.5 us
    unnamed x37, local copies, waits for them, and re-layouts  21.8 us
    all_to_all x1, starting transfers between devices, body(): got = lax.all_to_all(send, 'col', 0, 0)  19.3 us
    all_to_all x4, starting transfers between devices, spread(): return lax.all_to_all(send, 'row', 0, 0)  14.9 us
    all_to_all x1, waiting for transfers between devices, body(): got = lax.all_to_all(send, 'col', 0, 0)  14.2 us
    pallas_call x13, Pallas kernels, call(): pl.pallas_call(kernel, out_shape=outs, in_specs=[pl.BlockSpec(memory_spac...  12.6 us
    all_to_all x1, waiting for transfers between devices, body(): lax.all_to_all(old_part.reshape(n_col, group, steps * row_block), 'col',...  12.1 us
  transfers between devices with their start and end apart: 11, of which 7 were waited for; matrix products, arithmetic and copies ran while one was open for 4% of the time, Pallas kernels for 4%

profile of v2, /device:TPU:1, one launch (start us, length us, event | category | flops | bytes accessed | tf_op | source)
XLA Modules:
  0.0 271.0 jit_solution(393661833939253619)
XLA Ops:
  7.3 2.0 fusion.9
  9.3 1.0 slice.22
  10.3 0.8 pad_maximum_fusion.1
  11.2 1.0 pad_maximum_fusion
  12.8 4.8 %fusion.10 = f32[8,16,768]{2,1,0:T(8,128)} fusion(bf16[8,16,3072]{2,1,0:T(8,128)(2,1)S(1)} %bitcast.44, bf16[768,3072,1]{1,0,2:T(8,128)(2,1)} %bitcast.43), kind=kOutput, calls=%fused_computation.35 | convolution fusion | flops 603979776 | bytes 5898240 | tf_op jit(solution)/shard_map/dot_general | solution.py:170
  17.6 6.1 %all-to-all-start = ((f32[8,16,768]{2,1,0:T(8,128)}), f32[8,16,768]{2,1,0:T(8,128)S(1)}, u32[]{:S(2)}, u32[]{:S(2)}) async-start(f32[8,16,768]{2,1,0:T(8,128)} %fusion.10), calls=%async_computation | async-start | bytes 786432 | tf_op jit(solution)/shard_map/all_to_all | solution.py:176
  24.0 12.1 %all-to-all-done.parts_ref = f32[8,16,768]{2,1,0:T(8,128)S(1)} async-done(((f32[8,16,768]{2,1,0:T(8,128)}), f32[8,16,768]{2,1,0:T(8,128)S(1)}, u32[]{:S(2)}, u32[]{:S(2)}) %all-to-all-start) | async-done | bytes 393248 | tf_op jit(solution)/shard_map/all_to_all | solution.py:176
  36.2 15.1 %all_to_all.75.pairs_ref = bf16[16,32,256]{2,1,0:T(8,128)(2,1)S(1)} all-to-all(bf16[16,32,256]{2,1,0:T(8,128)(2,1)S(1)} %get-tuple-element.24), channel_id=1, replica_groups=mesh['row'=16,'col'=8] {'row'}, dimensions={0} | all-to-all | bytes 524288 | tf_op jit(solution)/shard_map/all_to_all | solution.py:187
  51.2 1.7 copy-done.9
  52.9 1.4 shard_map.114
  54.4 3.5 %all-to-all-start.2 = ((bf16[16,32,256]{2,1,0:T(8,128)(2,1)}), bf16[16,32,256]{2,1,0:T(8,128)(2,1)S(1)}, u32[]{:S(2)}, u32[]{:S(2)}) async-start(bf16[16,32,256]{2,1,0:T(8,128)(2,1)} %get-tuple-element.25), calls=%async_computation.2 | async-start | bytes 524288 | tf_op jit(solution)/shard_map/all_to_all | solution.py:187
  58.1 7.2 %all-to-all-done.2.pairs_ref = bf16[16,32,256]{2,1,0:T(8,128)(2,1)S(1)} async-done(((bf16[16,32,256]{2,1,0:T(8,128)(2,1)}), bf16[16,32,256]{2,1,0:T(8,128)(2,1)S(1)}, u32[]{:S(2)}, u32[]{:S(2)}) %all-to-all-start.2) | async-done | bytes 262176 | tf_op jit(solution)/shard_map/all_to_all | solution.py:187
  65.3 1.6 copy-done.10
  66.9 1.5 shard_map.115
  68.4 3.7 %all-to-all-start.3 = ((bf16[16,32,256]{2,1,0:T(8,128)(2,1)}), bf16[16,32,256]{2,1,0:T(8,128)(2,1)S(1)}, u32[]{:S(2)}, u32[]{:S(2)}) async-start(bf16[16,32,256]{2,1,0:T(8,128)(2,1)} %get-tuple-element.27), calls=%async_computation.3 | async-start | bytes 524288 | tf_op jit(solution)/shard_map/all_to_all | solution.py:187
  72.3 7.1 %all-to-all-done.3.pairs_ref = bf16[16,32,256]{2,1,0:T(8,128)(2,1)S(1)} async-done(((bf16[16,32,256]{2,1,0:T(8,128)(2,1)}), bf16[16,32,256]{2,1,0:T(8,128)(2,1)S(1)}, u32[]{:S(2)}, u32[]{:S(2)}) %all-to-all-start.3) | async-done | bytes 262176 | tf_op jit(solution)/shard_map/all_to_all | solution.py:187
  79.4 0.7 shard_map.116
  80.2 10.5 %all_to_all.76.refs_0_.refs_2_.refs_4_ = bf16[16,32,256]{2,1,0:T(8,128)(2,1)S(1)} all-to-all(bf16[16,32,256]{2,1,0:T(8,128)(2,1)S(1)} %get-tuple-element.29), channel_id=1, replica_groups=mesh['row'=16,'col'=8] {'row'}, dimensions={0} | all-to-all | bytes 524288 | tf_op jit(solution)/shard_map/all_to_all | solution.py:187
  90.7 2.2 copy-done.4
  93.6 11.1 %all_to_all.77.pairs_ref = bf16[16,32,256]{2,1,0:T(8,128)(2,1)S(1)} all-to-all(bf16[16,32,256]{2,1,0:T(8,128)(2,1)S(1)} %shard_map.117), channel_id=1, replica_groups=mesh['row'=16,'col'=8] {'row'}, dimensions={0} | all-to-all | bytes 524288 | tf_op jit(solution)/shard_map/all_to_all | solution.py:187
  105.5 10.9 %all_to_all.78.pairs_ref = bf16[16,32,256]{2,1,0:T(8,128)(2,1)S(1)} all-to-all(bf16[16,32,256]{2,1,0:T(8,128)(2,1)S(1)} %get-tuple-element.31), channel_id=1, replica_groups=mesh['row'=16,'col'=8] {'row'}, dimensions={0} | all-to-all | bytes 524288 | tf_op jit(solution)/shard_map/all_to_all | solution.py:187
  116.4 1.4 shard_map.119
  117.8 3.8 %all-to-all-start.7 = ((bf16[16,32,256]{2,1,0:T(8,128)(2,1)}), bf16[16,32,256]{2,1,0:T(8,128)(2,1)S(1)}, u32[]{:S(2)}, u32[]{:S(2)}) async-start(bf16[16,32,256]{2,1,0:T(8,128)(2,1)} %get-tuple-element.33), calls=%async_computation.7 | async-start | bytes 524288 | tf_op jit(solution)/shard_map/all_to_all | solution.py:187
  121.7 7.2 %all-to-all-done.7.pairs_ref = bf16[16,32,256]{2,1,0:T(8,128)(2,1)S(1)} async-done(((bf16[16,32,256]{2,1,0:T(8,128)(2,1)}), bf16[16,32,256]{2,1,0:T(8,128)(2,1)S(1)}, u32[]{:S(2)}, u32[]{:S(2)}) %all-to-all-start.7) | async-done | bytes 262176 | tf_op jit(solution)/shard_map/all_to_all | solution.py:187
  128.9 2.2 copy-done.6
  131.1 0.7 shard_map.120
  131.9 10.5 %all_to_all.79.refs_0_.refs_2_ = bf16[16,32,256]{2,1,0:T(8,128)(2,1)S(1)} all-to-all(bf16[16,32,256]{2,1,0:T(8,128)(2,1)S(1)} %get-tuple-element.35), channel_id=1, replica_groups=mesh['row'=16,'col'=8] {'row'}, dimensions={0} | all-to-all | bytes 524288 | tf_op jit(solution)/shard_map/all_to_all | solution.py:187
  142.4 2.8 %copy-done.1 = bf16[24,256,512]{2,1,0:T(8,128)(2,1)S(1)} copy-done((bf16[24,256,512]{2,1,0:T(8,128)(2,1)S(1)}, bf16[24,256,512]{2,1,0:T(8,128)(2,1)}, u32[]{:S(2)}) %copy-start.1) | copy-done | bytes 6291480
  145.2 1.3 shard_map.121
  146.5 10.6 %all_to_all.80.pairs_ref = bf16[16,32,256]{2,1,0:T(8,128)(2,1)S(1)} all-to-all(bf16[16,32,256]{2,1,0:T(8,128)(2,1)S(1)} %shard_map.121), channel_id=1, replica_groups=mesh['row'=16,'col'=8] {'row'}, dimensions={0} | all-to-all | bytes 524288 | tf_op jit(solution)/shard_map/all_to_all | solution.py:187
  157.9 11.7 %all_to_all.81.pairs_ref = bf16[16,32,256]{2,1,0:T(8,128)(2,1)S(1)} all-to-all(bf16[16,32,256]{2,1,0:T(8,128)(2,1)S(1)} %get-tuple-element.36), channel_id=1, replica_groups=mesh['row'=16,'col'=8] {'row'}, dimensions={0} | all-to-all | bytes 524288 | tf_op jit(solution)/shard_map/all_to_all | solution.py:187
  169.6 1.4 shard_map.123
  171.0 3.8 %all-to-all-start.11 = ((bf16[16,32,256]{2,1,0:T(8,128)(2,1)}), bf16[16,32,256]{2,1,0:T(8,128)(2,1)S(1)}, u32[]{:S(2)}, u32[]{:S(2)}) async-start(bf16[16,32,256]{2,1,0:T(8,128)(2,1)} %get-tuple-element.38), calls=%async_computation.11 | async-start | bytes 524288 | tf_op jit(solution)/shard_map/all_to_all | solution.py:187
  174.9 7.9 %all-to-all-done.11.pairs_ref = bf16[16,32,256]{2,1,0:T(8,128)(2,1)S(1)} async-done(((bf16[16,32,256]{2,1,0:T(8,128)(2,1)}), bf16[16,32,256]{2,1,0:T(8,128)(2,1)S(1)}, u32[]{:S(2)}, u32[]{:S(2)}) %all-to-all-start.11) | async-done | bytes 262176 | tf_op jit(solution)/shard_map/all_to_all | solution.py:187
  182.8 2.8 %copy-done.3 = bf16[24,256,512]{2,1,0:T(8,128)(2,1)S(1)} copy-done((bf16[24,256,512]{2,1,0:T(8,128)(2,1)S(1)}, bf16[24,256,512]{2,1,0:T(8,128)(2,1)}, u32[]{:S(2)}) %copy-start.3) | copy-done | bytes 6291480
  185.6 0.7 shard_map.124
  186.4 12.4 %all_to_all.82.refs_0_ = bf16[16,32,256]{2,1,0:T(8,128)(2,1)S(1)} all-to-all(bf16[16,32,256]{2,1,0:T(8,128)(2,1)S(1)} %get-tuple-element.40), channel_id=1, replica_groups=mesh['row'=16,'col'=8] {'row'}, dimensions={0} | all-to-all | bytes 524288 | tf_op jit(solution)/shard_map/all_to_all | solution.py:187
  198.7 1.1 shard_map.125
  199.8 19.3 %all-to-all-start.13 = ((bf16[8,3,32,640]{3,2,1,0:T(8,128)(2,1)}), bf16[8,3,32,640]{3,2,1,0:T(8,128)(2,1)S(1)}, u32[]{:S(2)}, u32[]{:S(2)}) async-start(bf16[8,3,32,640]{3,2,1,0:T(8,128)(2,1)} %shard_map.125), calls=%async_computation.13 | async-start | bytes 1966080 | tf_op jit(solution)/shard_map/all_to_all | solution.py:255
  219.2 14.2 %all-to-all-done.13.got_ref = bf16[8,3,32,640]{3,2,1,0:T(8,128)(2,1)S(1)} async-done(((bf16[8,3,32,640]{3,2,1,0:T(8,128)(2,1)}), bf16[8,3,32,640]{3,2,1,0:T(8,128)(2,1)S(1)}, u32[]{:S(2)}, u32[]{:S(2)}) %all-to-all-start.13) | async-done | bytes 983072 | tf_op jit(solution)/shard_map/all_to_all | solution.py:255
  233.4 3.7 %copy-done.7 = bf16[3072,3,512]{2,0,1:T(8,128)(2,1)S(1)} copy-done((bf16[3072,3,512]{2,0,1:T(8,128)(2,1)S(1)}, bf16[3072,3,512]{2,0,1:T(8,128)(2,1)}, u32[]{:S(2)}) %copy-start.7) | copy-done | bytes 9437208
  237.1 2.7 %shard_map.126 = (f32[4,384,128]{2,1,0:T(8,128)S(1)}, bf16[3,512,256]{2,1,0:T(8,128)(2,1)S(1)}) custom-call(s32[1]{0:T(128)} %bitcast.16.place_ref, bf16[8,3,32,640]{3,2,1,0:T(8,128)(2,1)S(1)} %all-to-all-done.13.got_ref, bf16[256,256]{1,0:T(8,128)(2,1)S(1)} %compare_convert_fusion.hot_ref, bf16[3,3072,512]{2,1,0:T(8,128)(2,1)S(1)} %bitcast.37), custom_call_target="tpu_custom_call" | custom-call | flops 1207959552 | bytes 4718592 | tf_op jit(solution)/shard_map/pallas_call | solution.py:287
  239.8 1.0 collective-permute-start
  240.8 3.7 %copy-done.8 = bf16[3072,3,512]{2,0,1:T(8,128)(2,1)S(1)} copy-done((bf16[3072,3,512]{2,0,1:T(8,128)(2,1)S(1)}, bf16[3072,3,512]{2,0,1:T(8,128)(2,1)}, u32[]{:S(2)}) %copy-start.8) | copy-done | bytes 9437208
  244.5 2.3 shard_map.127
  246.8 1.0 add.97
  247.8 3.5 %all-to-all-start.14 = ((f32[4,384,128]{2,1,0:T(8,128)}), f32[4,384,128]{2,1,0:T(8,128)S(1)}, u32[]{:S(2)}, u32[]{:S(2)}) async-start(f32[4,384,128]{2,1,0:T(8,128)} %add.97), calls=%async_computation.14 | async-start | bytes 1572864 | tf_op jit(solution)/shard_map/all_to_all | solution.py:312
  252.3 11.4 %all-to-all-done.14 = f32[4,384,128]{2,1,0:T(8,128)S(1)} async-done(((f32[4,384,128]{2,1,0:T(8,128)}), f32[4,384,128]{2,1,0:T(8,128)S(1)}, u32[]{:S(2)}, u32[]{:S(2)}) %all-to-all-start.14) | async-done | bytes 786464 | tf_op jit(solution)/shard_map/all_to_all | solution.py:312
  (62 shorter events, 5.5 us)
Async XLA Ops:
  7.2 16.5 %copy-start = (f32[3,256,128]{2,1,0:T(8,128)S(1)}, f32[3,256,128]{2,1,0:T(8,128)}, u32[]{:S(2)}) copy-start(f32[3,256,128]{2,1,0:T(8,128)} %param.13) | copy-start | bytes 1179652
  7.2 4.0 %slice-start = ((bf16[3,256,512]{2,1,0:T(8,128)(2,1)}), bf16[2,256,512]{2,1,0:T(8,128)(2,1)S(1)}, s32[]{:S(2)}) async-start(bf16[3,256,512]{2,1,0:T(8,128)(2,1)} %param.10), calls=%async_computation.18 | async-start | bytes 1048576 | tf_op jit(solution)/shard_map/slice | solution.py:158
  7.2 5.0 %copy-start.12 = (bf16[3072,128]{1,0:T(8,128)(2,1)S(1)}, bf16[3072,128]{1,0:T(8,128)(2,1)}, u32[]{:S(2)}) copy-start(bf16[3072,128]{1,0:T(8,128)(2,1)} %param.14) | copy-start | bytes 2359300
  7.2 5.3 %copy-start.14 = (s32[128]{0:T(128)S(1)}, s32[128]{0:T(128)}, u32[]{:S(2)}) copy-start(s32[128]{0:T(128)} %param.16) | copy-start | bytes 1540
  7.2 44.0 %all-gather.7.cloned.1.call-start = ((), (), s32[]{:S(2)}) async-start(), calls=%async_computation.15 | async-start | bytes 2359296 | tf_op jit(solution)/shard_map/all_gather | solution.py:156
  9.3 81.4 %all-gather.9.cloned.1.call-start = ((), (), s32[]{:S(2)}) async-start(), calls=%async_computation.16 | async-start | bytes 4718592 | tf_op jit(solution)/shard_map/all_gather | solution.py:157
  11.2 131.2 %all-gather.11.cloned.1.call-start = ((), (), s32[]{:S(2)}) async-start(), calls=%async_computation.17 | async-start | bytes 7077888 | tf_op jit(solution)/shard_map/all_gather | solution.py:158
  17.6 40.3 %copy-start.16 = (f32[128]{0:T(128)S(1)}, f32[128]{0:T(128)}, u32[]{:S(2)}) copy-start(f32[128]{0:T(128)} %param.15) | copy-start | bytes 1540
  17.6 18.5 %all-to-all-start = ((f32[8,16,768]{2,1,0:T(8,128)}), f32[8,16,768]{2,1,0:T(8,128)S(1)}, u32[]{:S(2)}, u32[]{:S(2)}) async-start(f32[8,16,768]{2,1,0:T(8,128)} %fusion.10), calls=%async_computation | async-start | bytes 786432 | tf_op jit(solution)/shard_map/all_to_all | solution.py:176
  51.2 1.7 copy-start.9
  52.9 26.5 %copy-start.11 = (bf16[8,256,512]{2,1,0:T(8,128)(2,1)S(1)}, bf16[8,256,512]{2,1,0:T(8,128)(2,1)}, u32[]{:S(2)}) copy-start(bf16[8,256,512]{2,1,0:T(8,128)(2,1)} %all-gather.7.cloned.1.call-done) | copy-start | bytes 6291460
  54.4 10.9 %all-to-all-start.2 = ((bf16[16,32,256]{2,1,0:T(8,128)(2,1)}), bf16[16,32,256]{2,1,0:T(8,128)(2,1)S(1)}, u32[]{:S(2)}, u32[]{:S(2)}) async-start(bf16[16,32,256]{2,1,0:T(8,128)(2,1)} %get-tuple-element.25), calls=%async_computation.2 | async-start | bytes 524288 | tf_op jit(solution)/shard_map/all_to_all | solution.py:187
  65.3 1.6 copy-start.10
  68.4 11.0 %all-to-all-start.3 = ((bf16[16,32,256]{2,1,0:T(8,128)(2,1)}), bf16[16,32,256]{2,1,0:T(8,128)(2,1)S(1)}, u32[]{:S(2)}, u32[]{:S(2)}) async-start(bf16[16,32,256]{2,1,0:T(8,128)(2,1)} %get-tuple-element.27), calls=%async_computation.3 | async-start | bytes 524288 | tf_op jit(solution)/shard_map/all_to_all | solution.py:187
  90.7 2.2 copy-start.4
  92.9 11.8 %copy-start.5 = (bf16[16,256,512]{2,1,0:T(8,128)(2,1)S(1)}, bf16[16,256,512]{2,1,0:T(8,128)(2,1)}, u32[]{:S(2)}) copy-start(bf16[16,256,512]{2,1,0:T(8,128)(2,1)} %all-gather.9.cloned.1.call-done) | copy-start | bytes 12582916
  117.8 11.1 %all-to-all-start.7 = ((bf16[16,32,256]{2,1,0:T(8,128)(2,1)}), bf16[16,32,256]{2,1,0:T(8,128)(2,1)S(1)}, u32[]{:S(2)}, u32[]{:S(2)}) async-start(bf16[16,32,256]{2,1,0:T(8,128)(2,1)} %get-tuple-element.33), calls=%async_computation.7 | async-start | bytes 524288 | tf_op jit(solution)/shard_map/all_to_all | solution.py:187
  128.9 2.2 copy-start.6
  142.4 2.8 %copy-start.1 = (bf16[24,256,512]{2,1,0:T(8,128)(2,1)S(1)}, bf16[24,256,512]{2,1,0:T(8,128)(2,1)}, u32[]{:S(2)}) copy-start(bf16[24,256,512]{2,1,0:T(8,128)(2,1)} %all-gather.11.cloned.1.call-done) | copy-start | bytes 18874372
  145.2 12.0 %copy-start.2 = (bf16[24,256,512]{2,1,0:T(8,128)(2,1)S(1)}, bf16[24,256,512]{2,1,0:T(8,128)(2,1)}, u32[]{:S(2)}) copy-start(bf16[24,256,512]{2,1,0:T(8,128)(2,1)} %all-gather.11.cloned.1.call-done) | copy-start | bytes 18874372
  171.0 11.8 %all-to-all-start.11 = ((bf16[16,32,256]{2,1,0:T(8,128)(2,1)}), bf16[16,32,256]{2,1,0:T(8,128)(2,1)S(1)}, u32[]{:S(2)}, u32[]{:S(2)}) async-start(bf16[16,32,256]{2,1,0:T(8,128)(2,1)} %get-tuple-element.38), calls=%async_computation.11 | async-start | bytes 524288 | tf_op jit(solution)/shard_map/all_to_all | solution.py:187
  182.8 2.8 %copy-start.3 = (bf16[24,256,512]{2,1,0:T(8,128)(2,1)S(1)}, bf16[24,256,512]{2,1,0:T(8,128)(2,1)}, u32[]{:S(2)}) copy-start(bf16[24,256,512]{2,1,0:T(8,128)(2,1)} %all-gather.11.cloned.1.call-done) | copy-start | bytes 18874372
  185.6 33.5 %copy-start.15 = (s32[128]{0:T(128)S(1)}, s32[128]{0:T(128)}, u32[]{:S(2)}) copy-start(s32[128]{0:T(128)} %param.17) | copy-start | bytes 1540
  199.8 33.6 %all-to-all-start.13 = ((bf16[8,3,32,640]{3,2,1,0:T(8,128)(2,1)}), bf16[8,3,32,640]{3,2,1,0:T(8,128)(2,1)S(1)}, u32[]{:S(2)}, u32[]{:S(2)}) async-start(bf16[8,3,32,640]{3,2,1,0:T(8,128)(2,1)} %shard_map.125), calls=%async_computation.13 | async-start | bytes 1966080 | tf_op jit(solution)/shard_map/all_to_all | solution.py:255
  233.4 3.7 %copy-start.7 = (bf16[3072,3,512]{2,0,1:T(8,128)(2,1)S(1)}, bf16[3072,3,512]{2,0,1:T(8,128)(2,1)}, u32[]{:S(2)}) copy-start(bf16[3072,3,512]{2,0,1:T(8,128)(2,1)} %param.18) | copy-start | bytes 28311556
  239.8 7.0 %collective-permute-start = (f32[4,384,128]{2,1,0:T(8,128)S(1)}, f32[4,384,128]{2,1,0:T(8,128)S(1)}, u32[]{:S(2)}, u32[]{:S(2)}) collective-permute-start(f32[4,384,128]{2,1,0:T(8,128)S(1)} %get-tuple-element.45), channel_id=1, source_target_pairs={{0,1},{1,0},{2,3},{3,2},{4,5},{5,4},{6,7},{7,6},{8,9},{9,8},{10,11... | collective-permute-start | bytes 2359304 | tf_op jit(solution)/shard_map/ppermute | solution.py:299
  240.8 3.7 %copy-start.8 = (bf16[3072,3,512]{2,0,1:T(8,128)(2,1)S(1)}, bf16[3072,3,512]{2,0,1:T(8,128)(2,1)}, u32[]{:S(2)}) copy-start(bf16[3072,3,512]{2,0,1:T(8,128)(2,1)} %param.18) | copy-start | bytes 28311556
  246.8 16.9 %copy-start.13 = (f32[384,128]{1,0:T(8,128)S(1)}, f32[384,128]{1,0:T(8,128)}, u32[]{:S(2)}) copy-start(f32[384,128]{1,0:T(8,128)} %param.19) | copy-start | bytes 589828
  247.8 15.8 %all-to-all-start.14 = ((f32[4,384,128]{2,1,0:T(8,128)}), f32[4,384,128]{2,1,0:T(8,128)S(1)}, u32[]{:S(2)}, u32[]{:S(2)}) async-start(f32[4,384,128]{2,1,0:T(8,128)} %add.97), calls=%async_computation.14 | async-start | bytes 1572864 | tf_op jit(solution)/shard_map/all_to_all | solution.py:312
Sparse Core Ops, SparseCore 0:
  9.7 31.6 all-gather.6
  43.2 31.9 all-gather.8
  76.9 40.7 all-gather.10

commit v3 on v2

--- a/solution.py
+++ b/solution.py
@@ -11,6 +11,8 @@
 F32 = jnp.float32
 BF16 = jnp.bfloat16
 VMEM_LIMIT = 16 << 20
+LANES = 128
+CHUNK = 512
 
 
 def rows_product(pairs_ref, rows_ref, which):
@@ -78,49 +80,95 @@
     send_to_all(send_ref, pair)
 
 
-def columns_kernel(steps, *refs):
-    send_ref = refs[-1]
+def columns_kernel(whole_ref, own_ref, send_ref):
     n_col = send_ref.shape[0]
-    lanes = 128
-    for step in range(steps):
-        whole_ref, own_ref = refs[2 * step], refs[2 * step + 1]
-        blocks, _, width = whole_ref.shape
-        per = blocks // n_col
-        share = width // n_col
-        for col in range(n_col):
-            for k in range(per):
-                send_ref[col, step, :, k * width : (k + 1) * width] = whole_ref[col * per + k]
-            first = col * share // lanes * lanes
-            send_ref[col, step, :, per * width :] = own_ref[:, first : first + lanes]
-
-
-def z_first_kernel(place_ref, got_ref, hot_ref, z_ref, out_ref, picked_ref):
-    steps, _, depth = z_ref.shape
+    blocks, _, width = whole_ref.shape
+    per = blocks // n_col
+    share = width // n_col
+    for col in range(n_col):
+        for k in range(per):
+            send_ref[col, :, k * width : (k + 1) * width] = whole_ref[col * per + k]
+        first = col * share // LANES * LANES
+        send_ref[col, :, per * width :] = own_ref[:, first : first + LANES]
+
+
+def pick(blocks, hot_ref):
+    return lax.dot_general(
+        jnp.concatenate(blocks, axis=0),
+        hot_ref[...],
+        (((0,), (0,)), ((), ())),
+        preferred_element_type=F32,
+    ).astype(BF16)
+
+
+def fold(product):
+    half = product.shape[1] // 2
+    return product[:, :half] + product[:, half:]
+
+
+def z_early_kernel(*refs):
+    hot_ref, z_ref, out_ref, picked_ref = refs[-4:]
+    gots = refs[:-4]
 
     @pl.when(pl.program_id(0) == 0)
     def _():
-        for step in range(steps):
-            whole = jnp.concatenate(
-                [got_ref[k, step, :, :depth] for k in range(got_ref.shape[0])], axis=0
+        for k, got_ref in enumerate(gots):
+            cols, per, _, width = got_ref.shape
+            for j in range(per):
+                blocks = [got_ref[col, j] for col in range(cols)]
+                picked_ref[k, j * width : (j + 1) * width] = pick(blocks, hot_ref)
+
+    out = None
+    for k in range(len(gots)):
+        part = jnp.dot(z_ref[k], picked_ref[k], preferred_element_type=F32)
+        out = part if out is None else out + part
+    out_ref[0] = fold(out)
+
+
+def z_first_kernel(place_ref, got_ref, hot_ref, z_ref, early_ref, out_ref, picked_ref):
+    depth = z_ref.shape[2]
+
+    @pl.when(pl.program_id(0) == 0)
+    def _():
+        blocks = [got_ref[k, :, :depth] for k in range(got_ref.shape[0])]
+        picked_ref[...] = pick(blocks, hot_ref)
+
+    z_next_kernel(place_ref, picked_ref, z_ref, early_ref, out_ref)
+
+
+def z_next_kernel(place_ref, picked_ref, z_ref, early_ref, out_ref):
+    product = jnp.dot(z_ref[0], picked_ref[...], preferred_element_type=F32)
+    out_ref[0] = early_ref[0] + fold(product)
+
+
+def old_kernel(base_ref, t_ref, old_ref, starts_ref, out_ref, sum_ref):
+    k = pl.program_id(0)
+    chunk = old_ref.shape[0]
+    row = base_ref[0] + k * chunk + lax.broadcasted_iota(jnp.int32, old_ref.shape, 0)
+    old = jnp.where(row < starts_ref[...], old_ref[...].astype(F32), 0.0).astype(BF16)
+    part = jnp.concatenate(
+        [
+            lax.dot_general(
+                old, t_ref[step], (((0,), (1,)), ((), ())), preferred_element_type=F32
             )
-            picked_ref[step] = lax.dot_general(
-                whole, hot_ref[...], (((0,), (0,)), ((), ())), preferred_element_type=F32
-            ).astype(BF16)
-
-    z_tile(z_ref, picked_ref, out_ref)
-
-
-def z_next_kernel(place_ref, picked_ref, z_ref, out_ref):
-    z_tile(z_ref, picked_ref, out_ref)
-
-
-def z_tile(z_ref, picked_ref, out_ref):
-    out = None
-    for step in range(z_ref.shape[0]):
-        part = jnp.dot(z_ref[step], picked_ref[step], preferred_element_type=F32)
-        out = part if out is None else out + part
-    half = out.shape[1] // 2
-    out_ref[0] = out[:, :half] + out[:, half:]
+            for step in range(t_ref.shape[0])
+        ],
+        axis=1,
+    )
+
+    @pl.when(k == 0)
+    def _():
+        sum_ref[...] = part
+
+    @pl.when(k > 0)
+    def _():
+        sum_ref[...] += part
+
+    @pl.when(k == pl.num_programs(0) - 1)
+    def _():
+        group = out_ref.shape[1]
+        for col in range(out_ref.shape[0]):
+            out_ref[col] = sum_ref[col * group : (col + 1) * group]
 
 
 def call(kernel, outs, *args, flops=0):
@@ -137,6 +185,10 @@
 
 def in_vmem(values):
     return pltpu.with_memory_space_constraint(values, pltpu.VMEM)
+
+
+def in_hbm(values):
+    return pltpu.with_memory_space_constraint(values, pltpu.HBM)
 
 
 def body(t_upper, t_old, inverses, forcing, x_old, offsets, starts, column_map, z_cols, acc):
@@ -152,31 +204,58 @@
     share = row_block // n_col
     shape = jax.ShapeDtypeStruct
 
+    def own_group(values):
+        return lax.dynamic_slice_in_dim(values, col_idx * group, group, 0)
+
     gather = functools.partial(lax.all_gather, axis_name="col", axis=0)
     set_a = gather(inverses[2:3])
-    set_b = gather(jnp.concatenate([t_upper[2:3], inverses[1:2]]))
-    set_c = gather(jnp.concatenate([t_upper[:2], inverses[:1]]))
+
+    old_base = steps * full_rows + col_idx * old_cols
+    (old_part,) = pl.pallas_call(
+        old_kernel,
+        out_shape=[shape((n_col, group, steps * row_block), F32)],
+        grid_spec=pltpu.PrefetchScalarGridSpec(
+            num_scalar_prefetch=1,
+            grid=(old_cols // CHUNK,),
+            in_specs=[
+                pl.BlockSpec((steps, row_block, CHUNK), lambda k, base: (0, 0, k)),
+                pl.BlockSpec((CHUNK, width), lambda k, base: (k, 0)),
+                pl.BlockSpec((1, width), lambda k, base: (0, 0)),
+            ],
+            out_specs=[
+                pl.BlockSpec((n_col, group, steps * row_block), lambda k, base: (0, 0, 0))
+            ],
+            scratch_shapes=[pltpu.VMEM((width, steps * row_block), F32)],
+        ),
+        compiler_params=pltpu.CompilerParams(vmem_limit_bytes=VMEM_LIMIT),
+        cost_estimate=pl.CostEstimate(
+            flops=2 * t_old.size * width, bytes_accessed=2 * t_old.size, transcendentals=0
+        ),
+    )(old_base[None], in_hbm(t_old), in_hbm(x_old), starts[None, :])
+    old_part, upper_later, inverses_later = lax.optimization_barrier(
+        (old_part, t_upper, inverses)
+    )
+    old_part = lax.all_to_all(old_part, "col", 0, 0)
+    set_b = gather(jnp.concatenate([upper_later[2:3], inverses_later[1:2]]))
+    set_c = gather(jnp.concatenate([upper_later[:2], inverses_later[:1]]))
     inv = {2: (set_a, 0), 1: (set_b, 1), 0: (set_c, 2)}
     upper_of = {(1, 2): (set_b, 0), (0, 1): (set_c, 0), (0, 2): (set_c, 1)}
 
-    def own_group(values):
-        return lax.dynamic_slice_in_dim(values, col_idx * group, group, 0)
-
+    core = col_idx % 2
     my_starts = own_group(starts)[:, None]
     my_offsets = own_group(offsets)[:, None]
-
-    old_rows = steps * full_rows + col_idx * old_cols + jnp.arange(old_cols, dtype=jnp.int32)
-    old_vals = jnp.where(old_rows[:, None] < starts[None, :], x_old, jnp.zeros_like(x_old))
-    old_part = lax.dot_general(
-        old_vals,
-        t_old.reshape(steps * row_block, old_cols),
-        (((0,), (1,)), ((), ())),
-        preferred_element_type=F32,
-    )
-    old_part = lax.all_to_all(old_part.reshape(n_col, group, steps * row_block), "col", 0, 0)
     forcing_t = lax.dynamic_slice_in_dim(
         forcing.reshape(steps * row_block, width), col_idx * group, group, 1
     ).T
+    limits = [my_starts - (step * full_rows + row_idx * row_block) for step in range(steps)]
+    order = jnp.arange(2 * width, dtype=jnp.int32)
+    half_of = order // group % 2
+    value_of = order // (2 * group) * group + order % group
+    target = jnp.concatenate([column_map, column_map + width])
+    hot = ((half_of * width + value_of)[:, None] == target[None, :]).astype(BF16)
+    old_part, my_offsets, forcing_t, limits, hot = lax.optimization_barrier(
+        (old_part, my_offsets, forcing_t, limits, hot)
+    )
 
     send_shape = shape((n_row, 2 * group, row_block), BF16)
     vec_shape = shape((group, row_block), F32)
@@ -230,7 +309,6 @@
                     flops=flops,
                 )
             else:
-                limit = my_starts - (step * full_rows + row_idx * row_block)
                 send, own[step] = call(
                     functools.partial(last_term_kernel, which),
                     [send_shape, own_shape],
@@ -238,64 +316,83 @@
                     rows,
                     my_offsets,
                     total,
-                    limit,
+                    limits[step],
                     flops=flops,
                 )
         whole[step] = spread(send)
 
-    lanes = 128
-    args = []
-    for step in range(steps):
-        args += [whole[step], own[step]]
-    (send,) = call(
-        functools.partial(columns_kernel, steps),
-        [shape((n_col, steps, 2 * group, col_block + lanes), BF16)],
-        *args,
-    )
-    got = lax.all_to_all(send, "col", 0, 0)
-
-    mine = lax.dynamic_slice_in_dim(
-        got, col_block + col_idx % (lanes // share) * share, share, 3
-    ).astype(F32)
-    mine = mine[:, :, :group] + mine[:, :, group:]
-    solved = jnp.transpose(mine, (1, 3, 0, 2)).reshape(steps, share, width)
-
-    order = jnp.arange(2 * width, dtype=jnp.int32)
-    half_of = order // group % 2
-    value_of = order // (2 * group) * group + order % group
-    target = jnp.concatenate([column_map, column_map + width])
-    hot = ((half_of * width + value_of)[:, None] == target[None, :]).astype(BF16)
-
+    early = list(range(1, steps))
+    per = n_row // n_col
     z_rows = z_cols.shape[0]
     z_block = z_rows // n_col
-    z_t = jnp.transpose(z_cols, (1, 0, 2))
-    core = col_idx % 2
-    z_spec = pl.BlockSpec((steps, z_block, col_block), lambda i, place: (0, 2 * i + place[0], 0))
-    out_spec = pl.BlockSpec((1, z_block, width), lambda i, place: (i, 0, 0))
+    z_t = in_hbm(jnp.transpose(z_cols, (1, 0, 2)))
     z_params = pltpu.CompilerParams(vmem_limit_bytes=VMEM_LIMIT)
-    cost = pl.CostEstimate(
-        flops=2 * z_rows * steps * col_block * width,
-        bytes_accessed=z_cols.size,
-        transcendentals=0,
-    )
-    part_shape = shape((n_col // 2, z_block, width), F32)
-    picked_shape = shape((steps, col_block, 2 * width), BF16)
+
+    def cost(parts):
+        return pl.CostEstimate(
+            flops=4 * z_rows * parts * col_block * width,
+            bytes_accessed=2 * z_rows * parts * col_block,
+            transcendentals=0,
+        )
+
+    gots = []
+    mine = []
+    for step in early:
+        all_cols = gather(whole[step])
+        gots.append(lax.dynamic_slice_in_dim(all_cols, per * col_idx, per, 1))
+        rows = lax.dynamic_index_in_dim(all_cols, row_idx, 1, keepdims=False)
+        mine.append(lax.dynamic_slice_in_dim(rows, col_idx * share, share, 2))
+    (early_part,) = pl.pallas_call(
+        z_early_kernel,
+        out_shape=[shape((n_col, z_block, width), F32)],
+        grid=(n_col,),
+        in_specs=[pl.BlockSpec(got.shape, lambda i: (0, 0, 0, 0)) for got in gots]
+        + [
+            pl.BlockSpec(hot.shape, lambda i: (0, 0)),
+            pl.BlockSpec((pl.Element(steps - 1), pl.Element(z_block), pl.Element(col_block)),
+                         lambda i: (1, i * z_block, 0)),
+        ],
+        out_specs=[pl.BlockSpec((1, z_block, width), lambda i: (i, 0, 0))],
+        scratch_shapes=[pltpu.VMEM((steps - 1, col_block, 2 * width), BF16)],
+        compiler_params=z_params,
+        cost_estimate=cost(steps - 1),
+    )(*gots, hot, z_t)
+
+    (send,) = call(
+        columns_kernel,
+        [shape((n_col, 2 * group, col_block + LANES), BF16)],
+        whole[0],
+        own[0],
+    )
+    got = lax.all_to_all(send, "col", 0, 0)
+
+    last = lax.dynamic_slice_in_dim(
+        got, col_block + col_idx % (LANES // share) * share, share, 2
+    )
+    mine = jnp.stack([last] + mine).astype(F32)
+    mine = mine[:, :, :group] + mine[:, :, group:]
+    solved = jnp.transpose(mine, (0, 3, 1, 2)).reshape(steps, share, width)
 
     def fixed(array_shape):
         return pl.BlockSpec(array_shape, lambda i, place: (0,) * len(array_shape))
 
+    z_spec = pl.BlockSpec((1, z_block, col_block), lambda i, place: (0, 2 * i + place[0], 0))
+    early_spec = pl.BlockSpec((1, z_block, width), lambda i, place: (2 * i + place[0], 0, 0))
+    out_spec = pl.BlockSpec((1, z_block, width), lambda i, place: (i, 0, 0))
+    part_shape = shape((n_col // 2, z_block, width), F32)
+    picked_shape = shape((col_block, 2 * width), BF16)
     theirs, picked = pl.pallas_call(
         z_first_kernel,
         out_shape=[part_shape, picked_shape],
         grid_spec=pltpu.PrefetchScalarGridSpec(
             num_scalar_prefetch=1,
             grid=(n_col // 2,),
-            in_specs=[fixed(got.shape), fixed(hot.shape), z_spec],
+            in_specs=[fixed(got.shape), fixed(hot.shape), z_spec, early_spec],
             out_specs=[out_spec, fixed(picked_shape.shape)],
         ),
         compiler_params=z_params,
-        cost_estimate=cost,
-    )((1 - core)[None], got, hot, z_t)
+        cost_estimate=cost(1),
+    )((1 - core)[None], got, hot, z_t, early_part)
     swapped = lax.ppermute(theirs, "col", [(i, i ^ 1) for i in range(n_col)])
     (ours,) = pl.pallas_call(
         z_next_kernel,
@@ -303,12 +400,12 @@
         grid_spec=pltpu.PrefetchScalarGridSpec(
             num_scalar_prefetch=1,
             grid=(n_col // 2,),
-            in_specs=[fixed(picked_shape.shape), z_spec],
+            in_specs=[fixed(picked_shape.shape), z_spec, early_spec],
             out_specs=[out_spec],
         ),
         compiler_params=z_params,
-        cost_estimate=cost,
-    )(core[None], picked, z_t)
+        cost_estimate=cost(1),
+    )(core[None], picked, z_t, early_part)
     part = lax.all_to_all(
         ours + swapped,
         "col",

time: 272 us -> 265 us (0.974)
  Pallas kernels: 17.5 us -> 34.5 us
  blocking collectives: 92.8 us -> 81.2 us
  waiting for transfers between devices: 67.2 us -> 58.8 us
  matrix products: 4.83 us -> 0 us
  local copies, waits for them, and re-layouts: 25.4 us -> 21.7 us
    all_to_all x1, waiting for transfers between devices: 14.2 us -> 0.01 us  [body(): got = lax.all_to_all(send, 'col', 0, 0)]
    pallas_call x0 -> x2, Pallas kernels: none -> 13.3 us  [the longest x1 7.02 us: body(): pl.pallas_call(z_early_kernel, out_shape=[shape((n_col, z_block, width),...]
    all_to_all x8 -> x7, blocking collectives: 92.8 us -> 81.2 us  [spread(): return lax.all_to_all(send, 'row', 0, 0)]
    all_to_all x4 -> x5, waiting for transfers between devices: 29.5 us -> 37.7 us  [spread(): return lax.all_to_all(send, 'row', 0, 0)]
    unnamed x37 -> x38, local copies, waits for them, and re-layouts: 21.8 us -> 15.2 us
    dot_general x1 -> x0, matrix products: 4.83 us -> none  [body(): lax.dot_general(old_vals, t_old.reshape(steps * row_block, old_cols), (((...]
    all_to_all x4 -> x5, starting transfers between devices: 14.9 us -> 18.1 us  [spread(): return lax.all_to_all(send, 'row', 0, 0)]
  transfers between devices with their start and end apart: 11 -> 14, of which waited for: 7 -> 7; matrix products, arithmetic and copies ran while one was open for 4% -> 3% of each run, Pallas kernels for 4% -> 12%
where the time goes in v3:
time: 265 us; the launch traced here: 263 us
  blocking collectives  81.2 us (31%)
  waiting for transfers between devices  58.8 us (22%)
  starting transfers between devices  47.6 us (18%)
  Pallas kernels  34.5 us (13%)
  local copies, waits for them, and re-layouts  21.7 us (8%)
  between operations  14.1 us (5%)
  other arithmetic  4.93 us (2%)
    all_to_all x7, blocking collectives, spread(): return lax.all_to_all(send, 'row', 0, 0)  81.2 us
    all_to_all x5, waiting for transfers between devices, spread(): return lax.all_to_all(send, 'row', 0, 0)  37.7 us
    all_to_all x1, starting transfers between devices, body(): got = lax.all_to_all(send, 'col', 0, 0)  18.7 us
    all_to_all x5, starting transfers between devices, spread(): return lax.all_to_all(send, 'row', 0, 0)  18.1 us
    unnamed x38, local copies, waits for them, and re-layouts  15.2 us
    pallas_call x13, Pallas kernels, call(): pl.pallas_call(kernel, out_shape=outs, in_specs=[pl.BlockSpec(memory_spac...  14.2 us
    all_to_all x1, waiting for transfers between devices, body(): old_part = lax.all_to_all(old_part, 'col', 0, 0)  11.9 us
    all_to_all x1, waiting for transfers between devices, body(): lax.all_to_all(ours + swapped, 'col', 0, 0, axis_index_groups=[list(range...  9.04 us
  transfers between devices with their start and end apart: 14, of which 7 were waited for; matrix products, arithmetic and copies ran while one was open for 3% of the time, Pallas kernels for 12%

profile of v3, /device:TPU:1, one launch (start us, length us, event | category | flops | bytes accessed | tf_op | source)
XLA Modules:
  0.0 262.9 jit_solution(8588656764763398875)
XLA Ops:
  7.2 1.7 slice.21
  9.7 6.3 %shard_map.113 = f32[8,16,768]{2,1,0:T(8,128)} custom-call(s32[1]{0:T(128)} %bitcast.base_ref, bf16[3,256,3072]{2,1,0:T(8,128)(2,1)} %t_ref.1, bf16[3072,128]{1,0:T(8,128)(2,1)} %old_ref.1, s32[1,128]{1,0:T(1,128)S(1)} %bitcast.43), custom_call_target="tpu_custom_call" | custom-call | flops 603979776 | bytes 4718592 | tf_op jit(solution)/shard_map/pallas_call | solution.py:214
  17.1 1.0 pad_maximum_fusion
  18.1 6.0 %all-to-all-start = ((f32[8,16,768]{2,1,0:T(8,128)}), f32[8,16,768]{2,1,0:T(8,128)S(1)}, u32[]{:S(2)}, u32[]{:S(2)}) async-start(f32[8,16,768]{2,1,0:T(8,128)} %shard_map.113), calls=%async_computation | async-start | bytes 786432 | tf_op jit(solution)/shard_map/all_to_all | solution.py:238
  24.7 11.9 %all-to-all-done.parts_ref = f32[8,16,768]{2,1,0:T(8,128)S(1)} async-done(((f32[8,16,768]{2,1,0:T(8,128)}), f32[8,16,768]{2,1,0:T(8,128)S(1)}, u32[]{:S(2)}, u32[]{:S(2)}) %all-to-all-start) | async-done | bytes 393248 | tf_op jit(solution)/shard_map/all_to_all | solution.py:238
  36.6 14.9 %all_to_all.75.pairs_ref = bf16[16,32,256]{2,1,0:T(8,128)(2,1)S(1)} all-to-all(bf16[16,32,256]{2,1,0:T(8,128)(2,1)S(1)} %get-tuple-element.35), channel_id=1, replica_groups=mesh['row'=16,'col'=8] {'row'}, dimensions={0} | all-to-all | bytes 524288 | tf_op jit(solution)/shard_map/all_to_all | solution.py:266
  51.6 1.7 copy-done.7
  53.3 1.4 shard_map.115
  54.7 3.5 %all-to-all-start.2 = ((bf16[16,32,256]{2,1,0:T(8,128)(2,1)}), bf16[16,32,256]{2,1,0:T(8,128)(2,1)S(1)}, u32[]{:S(2)}, u32[]{:S(2)}) async-start(bf16[16,32,256]{2,1,0:T(8,128)(2,1)} %get-tuple-element.36), calls=%async_computation.2 | async-start | bytes 524288 | tf_op jit(solution)/shard_map/all_to_all | solution.py:266
  58.4 7.3 %all-to-all-done.2.pairs_ref = bf16[16,32,256]{2,1,0:T(8,128)(2,1)S(1)} async-done(((bf16[16,32,256]{2,1,0:T(8,128)(2,1)}), bf16[16,32,256]{2,1,0:T(8,128)(2,1)S(1)}, u32[]{:S(2)}, u32[]{:S(2)}) %all-to-all-start.2) | async-done | bytes 262176 | tf_op jit(solution)/shard_map/all_to_all | solution.py:266
  65.7 1.4 shard_map.116
  67.1 3.7 %all-to-all-start.3 = ((bf16[16,32,256]{2,1,0:T(8,128)(2,1)}), bf16[16,32,256]{2,1,0:T(8,128)(2,1)S(1)}, u32[]{:S(2)}, u32[]{:S(2)}) async-start(bf16[16,32,256]{2,1,0:T(8,128)(2,1)} %get-tuple-element.39), calls=%async_computation.3 | async-start | bytes 524288 | tf_op jit(solution)/shard_map/all_to_all | solution.py:266
  70.9 7.2 %all-to-all-done.3.pairs_ref = bf16[16,32,256]{2,1,0:T(8,128)(2,1)S(1)} async-done(((bf16[16,32,256]{2,1,0:T(8,128)(2,1)}), bf16[16,32,256]{2,1,0:T(8,128)(2,1)S(1)}, u32[]{:S(2)}, u32[]{:S(2)}) %all-to-all-start.3) | async-done | bytes 262176 | tf_op jit(solution)/shard_map/all_to_all | solution.py:266
  78.1 1.3 shard_map.117
  79.5 10.6 %all_to_all.76.refs_0_.refs_2_ = bf16[16,32,256]{2,1,0:T(8,128)(2,1)} all-to-all(bf16[16,32,256]{2,1,0:T(8,128)(2,1)S(1)} %get-tuple-element.42), channel_id=1, replica_groups=mesh['row'=16,'col'=8] {'row'}, dimensions={0} | all-to-all | bytes 524288 | tf_op jit(solution)/shard_map/all_to_all | solution.py:266
  90.1 2.2 copy-done.4
  92.3 1.0 copy-done.9
  94.1 11.1 %all_to_all.77.pairs_ref = bf16[16,32,256]{2,1,0:T(8,128)(2,1)S(1)} all-to-all(bf16[16,32,256]{2,1,0:T(8,128)(2,1)S(1)} %shard_map.118), channel_id=1, replica_groups=mesh['row'=16,'col'=8] {'row'}, dimensions={0} | all-to-all | bytes 524288 | tf_op jit(solution)/shard_map/all_to_all | solution.py:266
  105.9 10.9 %all_to_all.78.pairs_ref = bf16[16,32,256]{2,1,0:T(8,128)(2,1)S(1)} all-to-all(bf16[16,32,256]{2,1,0:T(8,128)(2,1)S(1)} %get-tuple-element.46), channel_id=1, replica_groups=mesh['row'=16,'col'=8] {'row'}, dimensions={0} | all-to-all | bytes 524288 | tf_op jit(solution)/shard_map/all_to_all | solution.py:266
  116.8 1.4 shard_map.120
  118.2 3.8 %all-to-all-start.7 = ((bf16[16,32,256]{2,1,0:T(8,128)(2,1)}), bf16[16,32,256]{2,1,0:T(8,128)(2,1)S(1)}, u32[]{:S(2)}, u32[]{:S(2)}) async-start(bf16[16,32,256]{2,1,0:T(8,128)(2,1)} %get-tuple-element.48), calls=%async_computation.7 | async-start | bytes 524288 | tf_op jit(solution)/shard_map/all_to_all | solution.py:266
  122.1 7.2 %all-to-all-done.7.pairs_ref = bf16[16,32,256]{2,1,0:T(8,128)(2,1)S(1)} async-done(((bf16[16,32,256]{2,1,0:T(8,128)(2,1)}), bf16[16,32,256]{2,1,0:T(8,128)(2,1)S(1)}, u32[]{:S(2)}, u32[]{:S(2)}) %all-to-all-start.7) | async-done | bytes 262176 | tf_op jit(solution)/shard_map/all_to_all | solution.py:266
  129.3 2.2 copy-done.6
  131.5 1.3 shard_map.121
  132.9 10.7 %all_to_all.79.refs_0_ = bf16[16,32,256]{2,1,0:T(8,128)(2,1)} all-to-all(bf16[16,32,256]{2,1,0:T(8,128)(2,1)S(1)} %get-tuple-element.51), channel_id=1, replica_groups=mesh['row'=16,'col'=8] {'row'}, dimensions={0} | all-to-all | bytes 524288 | tf_op jit(solution)/shard_map/all_to_all | solution.py:266
  143.6 2.8 %copy-done.1 = bf16[24,256,512]{2,1,0:T(8,128)(2,1)S(1)} copy-done((bf16[24,256,512]{2,1,0:T(8,128)(2,1)S(1)}, bf16[24,256,512]{2,1,0:T(8,128)(2,1)}, u32[]{:S(2)}) %copy-start.1) | copy-done | bytes 6291480
  146.4 0.9 copy-done.11
  147.3 1.3 shard_map.122
  148.7 10.7 %all_to_all.80.pairs_ref = bf16[16,32,256]{2,1,0:T(8,128)(2,1)S(1)} all-to-all(bf16[16,32,256]{2,1,0:T(8,128)(2,1)S(1)} %shard_map.122), channel_id=1, replica_groups=mesh['row'=16,'col'=8] {'row'}, dimensions={0} | all-to-all | bytes 524288 | tf_op jit(solution)/shard_map/all_to_all | solution.py:266
  160.1 12.4 %all_to_all.81.pairs_ref = bf16[16,32,256]{2,1,0:T(8,128)(2,1)S(1)} all-to-all(bf16[16,32,256]{2,1,0:T(8,128)(2,1)S(1)} %get-tuple-element.52), channel_id=1, replica_groups=mesh['row'=16,'col'=8] {'row'}, dimensions={0} | all-to-all | bytes 524288 | tf_op jit(solution)/shard_map/all_to_all | solution.py:266
  172.4 1.5 shard_map.124
  173.9 3.5 %all-to-all-start.11 = ((bf16[16,32,256]{2,1,0:T(8,128)(2,1)}), bf16[16,32,256]{2,1,0:T(8,128)(2,1)S(1)}, u32[]{:S(2)}, u32[]{:S(2)}) async-start(bf16[16,32,256]{2,1,0:T(8,128)(2,1)} %get-tuple-element.54), calls=%async_computation.11 | async-start | bytes 524288 | tf_op jit(solution)/shard_map/all_to_all | solution.py:266
  177.5 8.7 %all-to-all-done.11.pairs_ref = bf16[16,32,256]{2,1,0:T(8,128)(2,1)S(1)} async-done(((bf16[16,32,256]{2,1,0:T(8,128)(2,1)}), bf16[16,32,256]{2,1,0:T(8,128)(2,1)S(1)}, u32[]{:S(2)}, u32[]{:S(2)}) %all-to-all-start.11) | async-done | bytes 262176 | tf_op jit(solution)/shard_map/all_to_all | solution.py:266
  186.2 2.8 %copy-done.3 = bf16[24,256,512]{2,1,0:T(8,128)(2,1)S(1)} copy-done((bf16[24,256,512]{2,1,0:T(8,128)(2,1)S(1)}, bf16[24,256,512]{2,1,0:T(8,128)(2,1)}, u32[]{:S(2)}) %copy-start.3) | copy-done | bytes 6291480
  189.0 1.5 shard_map.125
  190.4 3.5 %all-to-all-start.12 = ((bf16[16,32,256]{2,1,0:T(8,128)(2,1)}), bf16[16,32,256]{2,1,0:T(8,128)(2,1)S(1)}, u32[]{:S(2)}, u32[]{:S(2)}) async-start(bf16[16,32,256]{2,1,0:T(8,128)(2,1)} %get-tuple-element.57), calls=%async_computation.12 | async-start | bytes 524288 | tf_op jit(solution)/shard_map/all_to_all | solution.py:266
  194.0 7.3 %all-to-all-done.12.whole_ref = bf16[16,32,256]{2,1,0:T(8,128)(2,1)S(1)} async-done(((bf16[16,32,256]{2,1,0:T(8,128)(2,1)}), bf16[16,32,256]{2,1,0:T(8,128)(2,1)S(1)}, u32[]{:S(2)}, u32[]{:S(2)}) %all-to-all-start.12) | async-done | bytes 262176 | tf_op jit(solution)/shard_map/all_to_all | solution.py:266
  202.0 18.7 %all-to-all-start.13 = ((bf16[8,32,640]{2,1,0:T(8,128)(2,1)}), bf16[8,32,640]{2,1,0:T(8,128)(2,1)S(1)}, u32[]{:S(2)}, u32[]{:S(2)}) async-start(bf16[8,32,640]{2,1,0:T(8,128)(2,1)} %shard_map.126), calls=%async_computation.13 | async-start | bytes 655360 | tf_op jit(solution)/shard_map/all_to_all | solution.py:367
  220.7 1.0 constant_dynamic-slice_fusion.refs_1_
  221.7 1.0 constant_dynamic-slice_fusion.1.refs_0_
  222.7 7.0 %shard_map.127.early_ref = f32[8,384,128]{2,1,0:T(8,128)S(1)} custom-call(bf16[8,2,32,256]{3,2,1,0:T(8,128)(2,1)S(1)} %constant_dynamic-slice_fusion.1.refs_0_, bf16[8,2,32,256]{3,2,1,0:T(8,128)(2,1)S(1)} %constant_dynamic-slice_fusion.refs_1_, bf16[256,256]{1,0:T(8,128)(2,1)S(1)} %compare_convert_fusion.refs_2_.hot_ref, bf16[3,3072,512]{2,1,0:T(8,128)(2,1)} %bitcast.44), custom_call_target="tpu_custom_call" | custom-call | flops 1610612736 | bytes 6291456 | tf_op jit(solution)/shard_map/pallas_call | solution.py:345
  229.8 4.2 %shard_map.128 = (f32[4,384,128]{2,1,0:T(8,128)}, bf16[512,256]{1,0:T(8,128)(2,1)S(1)}) custom-call(s32[1]{0:T(128)} %bitcast.19.place_ref, bf16[8,32,640]{2,1,0:T(8,128)(2,1)S(1)} %all-to-all-done.13.got_ref, bf16[256,256]{1,0:T(8,128)(2,1)S(1)} %compare_convert_fusion.refs_2_.hot_ref, bf16[3,3072,512]{2,1,0:T(8,128)(2,1)} %bitcast.45, ...), custom_call_target="tpu_custom_call" | custom-call | flops 805306368 | bytes 3145728 | tf_op jit(solution)/shard_map/pallas_call | solution.py:384
  234.1 2.9 %shard_map.129 = f32[4,384,128]{2,1,0:T(8,128)S(1)} custom-call(s32[1]{0:T(128)} %bitcast.18.place_ref, bf16[512,256]{1,0:T(8,128)(2,1)S(1)} %get-tuple-element.60.picked_ref, bf16[3,3072,512]{2,1,0:T(8,128)(2,1)} %bitcast.46, f32[8,384,128]{2,1,0:T(8,128)S(1)} %shard_map.127.early_ref), custom_call_target="tpu_custom_call" | custom-call | flops 805306368 | bytes 3145728 | tf_op jit(solution)/shard_map/pallas_call | solution.py:397
  237.0 2.1 add.109
  239.1 4.5 %all-to-all-start.14 = ((f32[4,384,128]{2,1,0:T(8,128)}), f32[4,384,128]{2,1,0:T(8,128)S(1)}, u32[]{:S(2)}, u32[]{:S(2)}) async-start(f32[4,384,128]{2,1,0:T(8,128)} %add.109), calls=%async_computation.14 | async-start | bytes 1572864 | tf_op jit(solution)/shard_map/all_to_all | solution.py:409
  243.6 1.0 dynamic-slice_bitcast_fusion
  244.6 1.0 dynamic-slice_bitcast_fusion.1
  246.6 9.0 %all-to-all-done.14 = f32[4,384,128]{2,1,0:T(8,128)S(1)} async-done(((f32[4,384,128]{2,1,0:T(8,128)}), f32[4,384,128]{2,1,0:T(8,128)S(1)}, u32[]{:S(2)}, u32[]{:S(2)}) %all-to-all-start.14) | async-done | bytes 786464 | tf_op jit(solution)/shard_map/all_to_all | solution.py:409
  (75 shorter events, 7.7 us)
Async XLA Ops:
  7.2 17.0 %copy-start = (f32[3,256,128]{2,1,0:T(8,128)S(1)}, f32[3,256,128]{2,1,0:T(8,128)}, u32[]{:S(2)}) copy-start(f32[3,256,128]{2,1,0:T(8,128)} %param.13) | copy-start | bytes 1179652
  7.2 44.4 %all-gather.11.cloned.1.call-start = ((), (), s32[]{:S(2)}) async-start(), calls=%async_computation.15 | async-start | bytes 2359296 | tf_op jit(solution)/shard_map/all_gather | solution.py:211
  9.0 81.1 %all-gather.13.cloned.1.call-start = ((), (), s32[]{:S(2)}) async-start(), calls=%async_computation.16 | async-start | bytes 4718592 | tf_op jit(solution)/shard_map/all_gather | solution.py:239
  9.0 0.7 copy-start.12
  9.7 6.3 %copy-start.14 = (bf16[3,256,512]{2,1,0:T(8,128)(2,1)S(1)}, bf16[3,256,512]{2,1,0:T(8,128)(2,1)}, u32[]{:S(2)}) copy-start(bf16[3,256,512]{2,1,0:T(8,128)(2,1)} %param.12) | copy-start | bytes 2359300
  9.7 6.3 %slice-start = ((bf16[3,256,512]{2,1,0:T(8,128)(2,1)}), bf16[1,256,512]{2,1,0:T(8,128)(2,1)S(1)}, s32[]{:S(2)}) async-start(bf16[3,256,512]{2,1,0:T(8,128)(2,1)} %param.10), calls=%async_computation.20 | async-start | bytes 524288 | tf_op jit(solution)/shard_map/slice | solution.py:239
  15.9 1.1 slice-start.1
  16.9 7.2 %copy-start.13 = (s32[128]{0:T(128)S(1)}, s32[128]{0:T(128)}, u32[]{:S(2)}) copy-start(s32[128]{0:T(128)} %param.16) | copy-start | bytes 1540
  16.9 126.7 %all-gather.15.cloned.1.call-start = ((), (), s32[]{:S(2)}) async-start(), calls=%async_computation.17 | async-start | bytes 7077888 | tf_op jit(solution)/shard_map/all_gather | solution.py:240
  16.9 7.4 %copy-start.16 = (s32[128]{0:T(128)S(1)}, s32[128]{0:T(128)}, u32[]{:S(2)}) copy-start(s32[128]{0:T(128)} %param.17) | copy-start | bytes 1540
  16.9 7.4 %copy-start.17 = (f32[128]{0:T(128)S(1)}, f32[128]{0:T(128)}, u32[]{:S(2)}) copy-start(f32[128]{0:T(128)} %param.15) | copy-start | bytes 1540
  18.1 18.5 %all-to-all-start = ((f32[8,16,768]{2,1,0:T(8,128)}), f32[8,16,768]{2,1,0:T(8,128)S(1)}, u32[]{:S(2)}, u32[]{:S(2)}) async-start(f32[8,16,768]{2,1,0:T(8,128)} %shard_map.113), calls=%async_computation | async-start | bytes 786432 | tf_op jit(solution)/shard_map/all_to_all | solution.py:238
  51.6 1.7 copy-start.7
  53.3 12.4 %copy-start.8 = (bf16[8,256,512]{2,1,0:T(8,128)(2,1)S(1)}, bf16[8,256,512]{2,1,0:T(8,128)(2,1)}, u32[]{:S(2)}) copy-start(bf16[8,256,512]{2,1,0:T(8,128)(2,1)} %all-gather.11.cloned.1.call-done) | copy-start | bytes 6291460
  54.7 10.9 %all-to-all-start.2 = ((bf16[16,32,256]{2,1,0:T(8,128)(2,1)}), bf16[16,32,256]{2,1,0:T(8,128)(2,1)S(1)}, u32[]{:S(2)}, u32[]{:S(2)}) async-start(bf16[16,32,256]{2,1,0:T(8,128)(2,1)} %get-tuple-element.36), calls=%async_computation.2 | async-start | bytes 524288 | tf_op jit(solution)/shard_map/all_to_all | solution.py:266
  67.1 11.0 %all-to-all-start.3 = ((bf16[16,32,256]{2,1,0:T(8,128)(2,1)}), bf16[16,32,256]{2,1,0:T(8,128)(2,1)S(1)}, u32[]{:S(2)}, u32[]{:S(2)}) async-start(bf16[16,32,256]{2,1,0:T(8,128)(2,1)} %get-tuple-element.39), calls=%async_computation.3 | async-start | bytes 524288 | tf_op jit(solution)/shard_map/all_to_all | solution.py:266
  70.8 149.9 %all-gather.19.cloned.1.call-start = ((), (), s32[]{:S(2)}) async-start(), calls=%async_computation.19 | async-start | bytes 2359296 | tf_op jit(solution)/shard_map/all_gather | solution.py:341
  90.1 2.2 copy-start.4
  92.3 1.0 copy-start.9
  93.3 11.8 %copy-start.5 = (bf16[16,256,512]{2,1,0:T(8,128)(2,1)S(1)}, bf16[16,256,512]{2,1,0:T(8,128)(2,1)}, u32[]{:S(2)}) copy-start(bf16[16,256,512]{2,1,0:T(8,128)(2,1)} %all-gather.13.cloned.1.call-done) | copy-start | bytes 12582916
  118.2 11.1 %all-to-all-start.7 = ((bf16[16,32,256]{2,1,0:T(8,128)(2,1)}), bf16[16,32,256]{2,1,0:T(8,128)(2,1)S(1)}, u32[]{:S(2)}, u32[]{:S(2)}) async-start(bf16[16,32,256]{2,1,0:T(8,128)(2,1)} %get-tuple-element.48), calls=%async_computation.7 | async-start | bytes 524288 | tf_op jit(solution)/shard_map/all_to_all | solution.py:266
  122.0 99.7 %all-gather.17.cloned.1.call-start = ((), (), s32[]{:S(2)}) async-start(), calls=%async_computation.18 | async-start | bytes 2359296 | tf_op jit(solution)/shard_map/all_gather | solution.py:341
  129.3 2.2 copy-start.6
  131.5 12.1 %copy-start.10 = (bf16[16,32,256]{2,1,0:T(8,128)(2,1)S(1)}, bf16[16,32,256]{2,1,0:T(8,128)(2,1)}, u32[]{:S(2)}) copy-start(bf16[16,32,256]{2,1,0:T(8,128)(2,1)} %all_to_all.76.refs_0_.refs_2_) | copy-start | bytes 786436
  143.6 2.8 %copy-start.1 = (bf16[24,256,512]{2,1,0:T(8,128)(2,1)S(1)}, bf16[24,256,512]{2,1,0:T(8,128)(2,1)}, u32[]{:S(2)}) copy-start(bf16[24,256,512]{2,1,0:T(8,128)(2,1)} %all-gather.15.cloned.1.call-done) | copy-start | bytes 18874372
  146.4 0.9 copy-start.11
  147.3 12.0 %copy-start.2 = (bf16[24,256,512]{2,1,0:T(8,128)(2,1)S(1)}, bf16[24,256,512]{2,1,0:T(8,128)(2,1)}, u32[]{:S(2)}) copy-start(bf16[24,256,512]{2,1,0:T(8,128)(2,1)} %all-gather.15.cloned.1.call-done) | copy-start | bytes 18874372
  173.9 12.3 %all-to-all-start.11 = ((bf16[16,32,256]{2,1,0:T(8,128)(2,1)}), bf16[16,32,256]{2,1,0:T(8,128)(2,1)S(1)}, u32[]{:S(2)}, u32[]{:S(2)}) async-start(bf16[16,32,256]{2,1,0:T(8,128)(2,1)} %get-tuple-element.54), calls=%async_computation.11 | async-start | bytes 524288 | tf_op jit(solution)/shard_map/all_to_all | solution.py:266
  186.2 2.8 %copy-start.3 = (bf16[24,256,512]{2,1,0:T(8,128)(2,1)S(1)}, bf16[24,256,512]{2,1,0:T(8,128)(2,1)}, u32[]{:S(2)}) copy-start(bf16[24,256,512]{2,1,0:T(8,128)(2,1)} %all-gather.15.cloned.1.call-done) | copy-start | bytes 18874372
  190.4 10.8 %all-to-all-start.12 = ((bf16[16,32,256]{2,1,0:T(8,128)(2,1)}), bf16[16,32,256]{2,1,0:T(8,128)(2,1)S(1)}, u32[]{:S(2)}, u32[]{:S(2)}) async-start(bf16[16,32,256]{2,1,0:T(8,128)(2,1)} %get-tuple-element.57), calls=%async_computation.12 | async-start | bytes 524288 | tf_op jit(solution)/shard_map/all_to_all | solution.py:266
  202.0 27.7 %all-to-all-start.13 = ((bf16[8,32,640]{2,1,0:T(8,128)(2,1)}), bf16[8,32,640]{2,1,0:T(8,128)(2,1)S(1)}, u32[]{:S(2)}, u32[]{:S(2)}) async-start(bf16[8,32,640]{2,1,0:T(8,128)(2,1)} %shard_map.126), calls=%async_computation.13 | async-start | bytes 655360 | tf_op jit(solution)/shard_map/all_to_all | solution.py:367
  234.0 3.0 %collective-permute-start = (f32[4,384,128]{2,1,0:T(8,128)}, f32[4,384,128]{2,1,0:T(8,128)}, u32[]{:S(2)}, u32[]{:S(2)}) collective-permute-start(f32[4,384,128]{2,1,0:T(8,128)} %get-tuple-element.61), channel_id=1, source_target_pairs={{0,1},{1,0},{2,3},{3,2},{4,5},{5,4},{6,7},{7,6},{8,9},{9,8},{10,11... | collective-permute-start | bytes 2359304 | tf_op jit(solution)/shard_map/ppermute | solution.py:396
  239.1 16.6 %copy-start.15 = (f32[384,128]{1,0:T(8,128)S(1)}, f32[384,128]{1,0:T(8,128)}, u32[]{:S(2)}) copy-start(f32[384,128]{1,0:T(8,128)} %param.19) | copy-start | bytes 589828
  239.1 16.5 %all-to-all-start.14 = ((f32[4,384,128]{2,1,0:T(8,128)}), f32[4,384,128]{2,1,0:T(8,128)S(1)}, u32[]{:S(2)}, u32[]{:S(2)}) async-start(f32[4,384,128]{2,1,0:T(8,128)} %add.109), calls=%async_computation.14 | async-start | bytes 1572864 | tf_op jit(solution)/shard_map/all_to_all | solution.py:409
Sparse Core Ops, SparseCore 0:
  9.7 31.6 all-gather.10
  43.1 31.6 all-gather.12
  76.5 40.7 all-gather.14
  118.9 25.3 all-gather.18
  145.9 28.9 all-gather.16

commit v4 on v3

--- a/solution.py
+++ b/solution.py
@@ -12,7 +12,7 @@
 BF16 = jnp.bfloat16
 VMEM_LIMIT = 16 << 20
 LANES = 128
-CHUNK = 512
+CHUNK = 768
 
 
 def rows_product(pairs_ref, rows_ref, which):
@@ -43,20 +43,31 @@
         send_ref[peer] = pair
 
 
-def first_kernel(step, parts_ref, forcing_ref, rhs_ref, send_ref):
+def first_kernel(parts_ref, forcing_ref, send_ref):
     width = send_ref.shape[2]
-    rhs = forcing_ref[...] - jnp.sum(parts_ref[...], axis=0)
-    rhs_ref[...] = rhs
-    send_to_all(send_ref, pair_of(rhs[:, step * width : (step + 1) * width]))
+    rhs = forcing_ref[:, -width:] - jnp.sum(parts_ref[...], axis=0)
+    send_to_all(send_ref, pair_of(rhs))
 
 
 def rhs_kernel(step, uses, *refs):
-    rhs_ref, send_ref = refs[-2:]
+    forcing_ref, old_ref, send_ref = refs[-3:]
     width = send_ref.shape[2]
-    rhs = rhs_ref[:, step * width : (step + 1) * width]
+    here = slice(step * width, (step + 1) * width)
+    rhs = forcing_ref[:, here] - old_ref[:, here]
     for k, which in enumerate(uses):
         rhs = rhs - rows_product(refs[2 * k], refs[2 * k + 1], which)
     send_to_all(send_ref, pair_of(rhs))
+
+
+def load_kernel(from_ref, to_ref, sems):
+    count = from_ref.shape[0]
+    copies = [
+        pltpu.make_async_copy(from_ref.at[k], to_ref.at[k], sems.at[k]) for k in range(count)
+    ]
+    for copy in copies:
+        copy.start()
+    for copy in copies:
+        copy.wait()
 
 
 def first_term_kernel(which, pairs_ref, rows_ref, send_ref, total_ref):
@@ -113,9 +124,9 @@
     @pl.when(pl.program_id(0) == 0)
     def _():
         for k, got_ref in enumerate(gots):
-            cols, per, _, width = got_ref.shape
+            per, cols, _, width = got_ref.shape
             for j in range(per):
-                blocks = [got_ref[col, j] for col in range(cols)]
+                blocks = [got_ref[j, col] for col in range(cols)]
                 picked_ref[k, j * width : (j + 1) * width] = pick(blocks, hot_ref)
 
     out = None
@@ -141,34 +152,31 @@
     out_ref[0] = early_ref[0] + fold(product)
 
 
-def old_kernel(base_ref, t_ref, old_ref, starts_ref, out_ref, sum_ref):
+def old_kernel(base_ref, t_ref, old_ref, starts_ref, out_ref, rest_ref, sum_ref):
     k = pl.program_id(0)
     chunk = old_ref.shape[0]
+    steps, rows, _ = t_ref.shape
     row = base_ref[0] + k * chunk + lax.broadcasted_iota(jnp.int32, old_ref.shape, 0)
     old = jnp.where(row < starts_ref[...], old_ref[...].astype(F32), 0.0).astype(BF16)
-    part = jnp.concatenate(
-        [
-            lax.dot_general(
-                old, t_ref[step], (((0,), (1,)), ((), ())), preferred_element_type=F32
-            )
-            for step in range(t_ref.shape[0])
-        ],
-        axis=1,
-    )
-
-    @pl.when(k == 0)
-    def _():
-        sum_ref[...] = part
-
-    @pl.when(k > 0)
-    def _():
-        sum_ref[...] += part
+    for step in range(steps):
+        part = jnp.dot(t_ref[step], old, preferred_element_type=F32)
+        here = pl.ds(step * rows, rows)
+
+        @pl.when(k == 0)
+        def _():
+            sum_ref[here] = part
+
+        @pl.when(k > 0)
+        def _():
+            sum_ref[here] += part
 
     @pl.when(k == pl.num_programs(0) - 1)
     def _():
         group = out_ref.shape[1]
+        last = sum_ref[(steps - 1) * rows :].T
         for col in range(out_ref.shape[0]):
-            out_ref[col] = sum_ref[col * group : (col + 1) * group]
+            out_ref[col] = last[col * group : (col + 1) * group]
+        rest_ref[...] = sum_ref[: (steps - 1) * rows].T
 
 
 def call(kernel, outs, *args, flops=0):
@@ -189,6 +197,21 @@
 
 def in_hbm(values):
     return pltpu.with_memory_space_constraint(values, pltpu.HBM)
+
+
+def load(values):
+    (out,) = pl.pallas_call(
+        load_kernel,
+        out_shape=[pltpu.VMEM(values.shape, values.dtype)],
+        in_specs=[pl.BlockSpec(memory_space=pltpu.HBM)],
+        out_specs=[pl.BlockSpec(memory_space=pltpu.VMEM)],
+        scratch_shapes=[pltpu.SemaphoreType.DMA((values.shape[0],))],
+        compiler_params=pltpu.CompilerParams(vmem_limit_bytes=VMEM_LIMIT),
+        cost_estimate=pl.CostEstimate(
+            flops=0, bytes_accessed=values.size * values.dtype.itemsize, transcendentals=0
+        ),
+    )(in_hbm(values))
+    return out
 
 
 def body(t_upper, t_old, inverses, forcing, x_old, offsets, starts, column_map, z_cols, acc):
@@ -208,12 +231,15 @@
         return lax.dynamic_slice_in_dim(values, col_idx * group, group, 0)
 
     gather = functools.partial(lax.all_gather, axis_name="col", axis=0)
-    set_a = gather(inverses[2:3])
+    gathered = {2: gather(inverses[2:3])}
 
     old_base = steps * full_rows + col_idx * old_cols
-    (old_part,) = pl.pallas_call(
+    old_part, old_rest = pl.pallas_call(
         old_kernel,
-        out_shape=[shape((n_col, group, steps * row_block), F32)],
+        out_shape=[
+            shape((n_col, group, row_block), F32),
+            shape((width, (steps - 1) * row_block), F32),
+        ],
         grid_spec=pltpu.PrefetchScalarGridSpec(
             num_scalar_prefetch=1,
             grid=(old_cols // CHUNK,),
@@ -223,27 +249,21 @@
                 pl.BlockSpec((1, width), lambda k, base: (0, 0)),
             ],
             out_specs=[
-                pl.BlockSpec((n_col, group, steps * row_block), lambda k, base: (0, 0, 0))
+                pl.BlockSpec((n_col, group, row_block), lambda k, base: (0, 0, 0)),
+                pl.BlockSpec((width, (steps - 1) * row_block), lambda k, base: (0, 0)),
             ],
-            scratch_shapes=[pltpu.VMEM((width, steps * row_block), F32)],
+            scratch_shapes=[pltpu.VMEM((steps * row_block, width), F32)],
         ),
         compiler_params=pltpu.CompilerParams(vmem_limit_bytes=VMEM_LIMIT),
         cost_estimate=pl.CostEstimate(
             flops=2 * t_old.size * width, bytes_accessed=2 * t_old.size, transcendentals=0
         ),
-    )(old_base[None], in_hbm(t_old), in_hbm(x_old), starts[None, :])
-    old_part, upper_later, inverses_later = lax.optimization_barrier(
-        (old_part, t_upper, inverses)
-    )
+    )(old_base[None], in_hbm(t_old), in_hbm(x_old), in_hbm(starts[None, :]))
     old_part = lax.all_to_all(old_part, "col", 0, 0)
-    set_b = gather(jnp.concatenate([upper_later[2:3], inverses_later[1:2]]))
-    set_c = gather(jnp.concatenate([upper_later[:2], inverses_later[:1]]))
-    inv = {2: (set_a, 0), 1: (set_b, 1), 0: (set_c, 2)}
-    upper_of = {(1, 2): (set_b, 0), (0, 1): (set_c, 0), (0, 2): (set_c, 1)}
 
     core = col_idx % 2
-    my_starts = own_group(starts)[:, None]
-    my_offsets = own_group(offsets)[:, None]
+    my_starts = jnp.broadcast_to(own_group(starts)[:, None], (group, row_block))
+    my_offsets = jnp.broadcast_to(own_group(offsets)[:, None], (group, row_block))
     forcing_t = lax.dynamic_slice_in_dim(
         forcing.reshape(steps * row_block, width), col_idx * group, group, 1
     ).T
@@ -253,11 +273,14 @@
     value_of = order // (2 * group) * group + order % group
     target = jnp.concatenate([column_map, column_map + width])
     hot = ((half_of * width + value_of)[:, None] == target[None, :]).astype(BF16)
-    old_part, my_offsets, forcing_t, limits, hot = lax.optimization_barrier(
-        (old_part, my_offsets, forcing_t, limits, hot)
-    )
-
-    send_shape = shape((n_row, 2 * group, row_block), BF16)
+    old_part, my_offsets, forcing_t, limits, hot, t_upper, inverses = lax.optimization_barrier(
+        (old_part, my_offsets, forcing_t, limits, hot, t_upper, inverses)
+    )
+    gathered[1] = gather(jnp.concatenate([t_upper[2:3], inverses[1:2]]))
+    which_inv = {2: 0, 1: 1, 0: 2}
+    which_upper = {(1, 2): 0, (0, 1): 0, (0, 2): 1}
+
+    send_shape = pltpu.VMEM((n_row, 2 * group, row_block), BF16)
     vec_shape = shape((group, row_block), F32)
     own_shape = shape((2 * group, row_block), BF16)
     flops = 4 * group * row_block * full_rows
@@ -265,68 +288,17 @@
     def spread(send):
         return lax.all_to_all(send, "row", 0, 0)
 
-    rhs_all, send = call(
-        functools.partial(first_kernel, steps - 1),
-        [shape((group, steps * row_block), F32), send_shape],
-        old_part,
-        forcing_t,
-    )
-    whole = {}
-    own = {}
-    for step in reversed(range(steps)):
-        if step < steps - 1:
-            args = []
-            uses = []
-            for later in range(step + 1, steps):
-                rows, which = upper_of[step, later]
-                args += [whole[later], in_vmem(rows)]
-                uses.append(which)
-            (send,) = call(
-                functools.partial(rhs_kernel, step, uses),
-                [send_shape],
-                *args,
-                rhs_all,
-                flops=flops * len(uses),
-            )
-        rows, which = inv[step]
-        rows = in_vmem(rows)
-        send, total = call(
-            functools.partial(first_term_kernel, which),
-            [send_shape, vec_shape],
-            spread(send),
-            rows,
-            flops=flops,
-        )
-        for extra in range(1, NEUMANN):
-            if extra < NEUMANN - 1:
-                send, total = call(
-                    functools.partial(next_term_kernel, which),
-                    [send_shape, vec_shape],
-                    spread(send),
-                    rows,
-                    my_offsets,
-                    total,
-                    flops=flops,
-                )
-            else:
-                send, own[step] = call(
-                    functools.partial(last_term_kernel, which),
-                    [send_shape, own_shape],
-                    spread(send),
-                    rows,
-                    my_offsets,
-                    total,
-                    limits[step],
-                    flops=flops,
-                )
-        whole[step] = spread(send)
-
+    (send,) = call(first_kernel, [send_shape], old_part, forcing_t)
+    send, old_rest = lax.optimization_barrier((send, old_rest))
+    old_rest = lax.psum_scatter(old_rest, "col", scatter_dimension=0, tiled=True)
     early = list(range(1, steps))
     per = n_row // n_col
     z_rows = z_cols.shape[0]
     z_block = z_rows // n_col
     z_t = in_hbm(jnp.transpose(z_cols, (1, 0, 2)))
     z_params = pltpu.CompilerParams(vmem_limit_bytes=VMEM_LIMIT)
+    mine = []
+    everywhere = {}
 
     def cost(parts):
         return pl.CostEstimate(
@@ -335,28 +307,95 @@
             transcendentals=0,
         )
 
-    gots = []
-    mine = []
-    for step in early:
-        all_cols = gather(whole[step])
-        gots.append(lax.dynamic_slice_in_dim(all_cols, per * col_idx, per, 1))
-        rows = lax.dynamic_index_in_dim(all_cols, row_idx, 1, keepdims=False)
-        mine.append(lax.dynamic_slice_in_dim(rows, col_idx * share, share, 2))
-    (early_part,) = pl.pallas_call(
-        z_early_kernel,
-        out_shape=[shape((n_col, z_block, width), F32)],
-        grid=(n_col,),
-        in_specs=[pl.BlockSpec(got.shape, lambda i: (0, 0, 0, 0)) for got in gots]
-        + [
-            pl.BlockSpec(hot.shape, lambda i: (0, 0)),
-            pl.BlockSpec((pl.Element(steps - 1), pl.Element(z_block), pl.Element(col_block)),
-                         lambda i: (1, i * z_block, 0)),
-        ],
-        out_specs=[pl.BlockSpec((1, z_block, width), lambda i: (i, 0, 0))],
-        scratch_shapes=[pltpu.VMEM((steps - 1, col_block, 2 * width), BF16)],
-        compiler_params=z_params,
-        cost_estimate=cost(steps - 1),
-    )(*gots, hot, z_t)
+    def early_z():
+        gots = []
+        for step in early:
+            blocks = everywhere[step].reshape(n_row, n_col, 2 * group, row_block)
+            gots.append(lax.dynamic_slice_in_dim(blocks, per * col_idx, per, 0))
+            rows = lax.dynamic_index_in_dim(blocks, row_idx, 0, keepdims=False)
+            mine.append(lax.dynamic_slice_in_dim(rows, col_idx * share, share, 2))
+        (out,) = pl.pallas_call(
+            z_early_kernel,
+            out_shape=[shape((n_col, z_block, width), F32)],
+            grid=(n_col,),
+            in_specs=[pl.BlockSpec(got.shape, lambda i: (0, 0, 0, 0)) for got in gots]
+            + [
+                pl.BlockSpec(hot.shape, lambda i: (0, 0)),
+                pl.BlockSpec(
+                    (pl.Element(steps - 1), pl.Element(z_block), pl.Element(col_block)),
+                    lambda i: (1, i * z_block, 0),
+                ),
+            ],
+            out_specs=[pl.BlockSpec((1, z_block, width), lambda i: (i, 0, 0))],
+            scratch_shapes=[pltpu.VMEM((steps - 1, col_block, 2 * width), BF16)],
+            compiler_params=z_params,
+            cost_estimate=cost(steps - 1),
+        )(*gots, hot, z_t)
+        return out
+
+    whole = {}
+    own = {}
+    for step in reversed(range(steps)):
+        if step < steps - 1:
+            got, rows, old_rest = lax.optimization_barrier(
+                (whole[step + 1], gathered[step], old_rest)
+            )
+            rows = load(rows)
+            whole[step + 1] = got
+            args = []
+            for later in range(step + 1, steps):
+                args += [whole[later], rows]
+            (send,) = call(
+                functools.partial(
+                    rhs_kernel, step, [which_upper[step, j] for j in range(step + 1, steps)]
+                ),
+                [send_shape],
+                *args,
+                forcing_t,
+                old_rest,
+                flops=flops * (steps - 1 - step),
+            )
+            got = spread(send)
+        else:
+            got, rows = lax.optimization_barrier((spread(send), gathered[step]))
+            rows = load(rows)
+        which = which_inv[step]
+        send, total = call(
+            functools.partial(first_term_kernel, which),
+            [send_shape, vec_shape],
+            got,
+            rows,
+            flops=flops,
+        )
+        if step == steps - 1:
+            send, t_upper, inverses = lax.optimization_barrier((send, t_upper, inverses))
+            gathered[0] = gather(jnp.concatenate([t_upper[:2], inverses[:1]]))
+        for extra in range(1, NEUMANN - 1):
+            send, total = call(
+                functools.partial(next_term_kernel, which),
+                [send_shape, vec_shape],
+                spread(send),
+                rows,
+                my_offsets,
+                total,
+                flops=flops,
+            )
+        send, own[step] = call(
+            functools.partial(last_term_kernel, which),
+            [send_shape, own_shape],
+            spread(send),
+            rows,
+            my_offsets,
+            total,
+            limits[step],
+            flops=flops,
+        )
+        if step > 0:
+            everywhere[step] = lax.all_gather(own[step], ("row", "col"), axis=0)
+        else:
+            own[0], everywhere = lax.optimization_barrier((own[0], everywhere))
+        whole[step] = spread(send)
+    whole[0], early_part = lax.optimization_barrier((whole[0], early_z()))
 
     (send,) = call(
         columns_kernel,
@@ -379,7 +418,7 @@
     z_spec = pl.BlockSpec((1, z_block, col_block), lambda i, place: (0, 2 * i + place[0], 0))
     early_spec = pl.BlockSpec((1, z_block, width), lambda i, place: (2 * i + place[0], 0, 0))
     out_spec = pl.BlockSpec((1, z_block, width), lambda i, place: (i, 0, 0))
-    part_shape = shape((n_col // 2, z_block, width), F32)
+    part_shape = pltpu.VMEM((n_col // 2, z_block, width), F32)
     picked_shape = shape((col_block, 2 * width), BF16)
     theirs, picked = pl.pallas_call(
         z_first_kernel,

time: 265 us -> 345 us (1.30)
  waiting for transfers between devices: 58.8 us -> 142 us
  blocking collectives: 81.2 us -> 106 us
  starting transfers between devices: 47.6 us -> 26.1 us
  local copies, waits for them, and re-layouts: 21.7 us -> 10.3 us
  Pallas kernels: 34.5 us -> 39.1 us
    all_gather x5, waiting for transfers between devices: 0.06 us -> 107 us  [the longest x2 82.7 us: body(): everywhere[step] = lax.all_gather(own[step], ('row', 'col'), axis=0)]
    all_to_all x7 -> x9, blocking collectives: 81.2 us -> 106 us  [spread(): return lax.all_to_all(send, 'row', 0, 0)]
    all_to_all x5 -> x3, waiting for transfers between devices: 37.7 us -> 14.6 us  [spread(): return lax.all_to_all(send, 'row', 0, 0)]
    all_to_all x1, starting transfers between devices: 18.7 us -> 3.9 us  [body(): got = lax.all_to_all(send, 'col', 0, 0)]
    unnamed x38 -> x18, local copies, waits for them, and re-layouts: 15.2 us -> 3.68 us
    all_to_all x1, waiting for transfers between devices: 11.9 us -> 4.63 us  [body(): old_part = lax.all_to_all(old_part, 'col', 0, 0)]
    all_to_all x1, waiting for transfers between devices: 0.01 us -> 7.11 us  [body(): got = lax.all_to_all(send, 'col', 0, 0)]
    all_to_all x5 -> x3, starting transfers between devices: 18.1 us -> 11.1 us  [spread(): return lax.all_to_all(send, 'row', 0, 0)]
  transfers between devices with their start and end apart: 14 -> 13, of which waited for: 7 -> 8; matrix products, arithmetic and copies ran while one was open for 3% -> 2% of each run, Pallas kernels for 12% -> 10%
where the time goes in v4:
time: 345 us; the launch traced here: 343 us
  waiting for transfers between devices  142 us (41%)
  blocking collectives  106 us (31%)
  Pallas kernels  39.1 us (11%)
  starting transfers between devices  26.1 us (8%)
  between operations  14.5 us (4%)
  local copies, waits for them, and re-layouts  10.3 us (3%)
  other arithmetic  4.88 us (1%)
    all_to_all x9, blocking collectives, spread(): return lax.all_to_all(send, 'row', 0, 0)  106 us
    all_gather x2, waiting for transfers between devices, body(): everywhere[step] = lax.all_gather(own[step], ('row', 'col'), axis=0)  82.7 us
    all_gather x1, waiting for transfers between devices, body(): gathered[1] = gather(jnp.concatenate([t_upper[2:3], inverses[1:2]]))  23.9 us
    all_to_all x3, waiting for transfers between devices, spread(): return lax.all_to_all(send, 'row', 0, 0)  14.6 us
    pallas_call x13, Pallas kernels, call(): pl.pallas_call(kernel, out_shape=outs, in_specs=[pl.BlockSpec(memory_spac...  12.2 us
    all_to_all x3, starting transfers between devices, spread(): return lax.all_to_all(send, 'row', 0, 0)  11.1 us
    all_to_all x1, waiting for transfers between devices, body(): lax.all_to_all(ours + swapped, 'col', 0, 0, axis_index_groups=[list(range...  9.39 us
    all_to_all x1, waiting for transfers between devices, body(): got = lax.all_to_all(send, 'col', 0, 0)  7.11 us
  transfers between devices with their start and end apart: 13, of which 8 were waited for; matrix products, arithmetic and copies ran while one was open for 2% of the time, Pallas kernels for 10%

profile of v4, /device:TPU:1, one launch (start us, length us, event | category | flops | bytes accessed | tf_op | source)
XLA Modules:
  0.0 343.0 jit_solution(4388714274598169276)
XLA Ops:
  7.2 1.7 slice.21
  9.0 6.2 %shard_map.113 = (f32[8,16,256]{2,1,0:T(8,128)}, f32[128,512]{1,0:T(8,128)}) custom-call(s32[1]{0:T(128)} %bitcast.base_ref, bf16[3,256,3072]{2,1,0:T(8,128)(2,1)} %t_ref.1, bf16[3072,128]{1,0:T(8,128)(2,1)} %old_ref.1, s32[1,128]{1,0:T(1,128)} %bitcast.34), custom_call_target="tpu_custom_call" | custom-call | flops 603979776 | bytes 4718592 | tf_op jit(solution)/shard_map/pallas_call | solution.py:237
  15.2 6.1 %all-to-all-start = ((f32[8,16,256]{2,1,0:T(8,128)}), f32[8,16,256]{2,1,0:T(8,128)S(1)}, u32[]{:S(2)}, u32[]{:S(2)}) async-start(f32[8,16,256]{2,1,0:T(8,128)} %get-tuple-element.51), calls=%async_computation | async-start | bytes 262144 | tf_op jit(solution)/shard_map/all_to_all | solution.py:262
  21.9 4.6 %all-to-all-done.parts_ref = f32[8,16,256]{2,1,0:T(8,128)S(1)} async-done(((f32[8,16,256]{2,1,0:T(8,128)}), f32[8,16,256]{2,1,0:T(8,128)S(1)}, u32[]{:S(2)}, u32[]{:S(2)}) %all-to-all-start) | async-done | bytes 131104 | tf_op jit(solution)/shard_map/all_to_all | solution.py:262
  27.0 0.8 pad_maximum_fusion.1
  27.9 16.0 %all_to_all.75.pairs_ref = bf16[16,32,256]{2,1,0:T(8,128)(2,1)S(1)} all-to-all(bf16[16,32,256]{2,1,0:T(8,128)(2,1)S(1)} %shard_map.114), channel_id=1, replica_groups=mesh['row'=16,'col'=8] {'row'}, dimensions={0} | all-to-all | bytes 524288 | tf_op jit(solution)/shard_map/all_to_all | solution.py:289
  43.8 1.6 shard_map.115.rows_ref
  46.5 0.9 pad_maximum_fusion
  47.5 10.8 %all_to_all.76.pairs_ref = bf16[16,32,256]{2,1,0:T(8,128)(2,1)S(1)} all-to-all(bf16[16,32,256]{2,1,0:T(8,128)(2,1)S(1)} %get-tuple-element.61), channel_id=1, replica_groups=mesh['row'=16,'col'=8] {'row'}, dimensions={0} | all-to-all | bytes 524288 | tf_op jit(solution)/shard_map/all_to_all | solution.py:289
  59.1 10.8 %all_to_all.77.pairs_ref = bf16[16,32,256]{2,1,0:T(8,128)(2,1)S(1)} all-to-all(bf16[16,32,256]{2,1,0:T(8,128)(2,1)S(1)} %get-tuple-element.64), channel_id=1, replica_groups=mesh['row'=16,'col'=8] {'row'}, dimensions={0} | all-to-all | bytes 524288 | tf_op jit(solution)/shard_map/all_to_all | solution.py:289
  69.9 1.4 shard_map.118
  71.3 3.5 %all-to-all-start.4 = ((bf16[16,32,256]{2,1,0:T(8,128)(2,1)}), bf16[16,32,256]{2,1,0:T(8,128)(2,1)S(1)}, u32[]{:S(2)}, u32[]{:S(2)}) async-start(bf16[16,32,256]{2,1,0:T(8,128)(2,1)} %get-tuple-element.67), calls=%async_computation.4 | async-start | bytes 524288 | tf_op jit(solution)/shard_map/all_to_all | solution.py:289
  75.0 7.2 %all-to-all-done.4.refs_0_.refs_2_ = bf16[16,32,256]{2,1,0:T(8,128)(2,1)S(1)} async-done(((bf16[16,32,256]{2,1,0:T(8,128)(2,1)}), bf16[16,32,256]{2,1,0:T(8,128)(2,1)S(1)}, u32[]{:S(2)}, u32[]{:S(2)}) %all-to-all-start.4) | async-done | bytes 262176 | tf_op jit(solution)/shard_map/all_to_all | solution.py:289
  82.2 23.9 %all-gather.13.cloned.1.call-done = bf16[16,256,512]{2,1,0:T(8,128)(2,1)} async-done(((bf16[2,256,512]{2,1,0:T(8,128)(2,1)}), bf16[16,256,512]{2,1,0:T(8,128)(2,1)}) %all-gather.13.cloned.1.call-update) | async-done | bytes 4194320 | tf_op jit(solution)/shard_map/all_gather | solution.py:279
  106.0 2.2 shard_map.119.refs_1_.rows_ref
  108.3 0.7 shard_map.120
  109.0 14.1 %all_to_all.78.pairs_ref = bf16[16,32,256]{2,1,0:T(8,128)(2,1)S(1)} all-to-all(bf16[16,32,256]{2,1,0:T(8,128)(2,1)S(1)} %shard_map.120), channel_id=1, replica_groups=mesh['row'=16,'col'=8] {'row'}, dimensions={0} | all-to-all | bytes 524288 | tf_op jit(solution)/shard_map/all_to_all | solution.py:289
  123.9 10.9 %all_to_all.79.pairs_ref = bf16[16,32,256]{2,1,0:T(8,128)(2,1)S(1)} all-to-all(bf16[16,32,256]{2,1,0:T(8,128)(2,1)S(1)} %get-tuple-element.72), channel_id=1, replica_groups=mesh['row'=16,'col'=8] {'row'}, dimensions={0} | all-to-all | bytes 524288 | tf_op jit(solution)/shard_map/all_to_all | solution.py:289
  135.5 11.0 %all_to_all.80.pairs_ref = bf16[16,32,256]{2,1,0:T(8,128)(2,1)S(1)} all-to-all(bf16[16,32,256]{2,1,0:T(8,128)(2,1)S(1)} %get-tuple-element.74), channel_id=1, replica_groups=mesh['row'=16,'col'=8] {'row'}, dimensions={0} | all-to-all | bytes 524288 | tf_op jit(solution)/shard_map/all_to_all | solution.py:289
  146.5 1.3 shard_map.123
  147.8 10.8 %all_to_all.81.refs_0_ = bf16[16,32,256]{2,1,0:T(8,128)(2,1)S(1)} all-to-all(bf16[16,32,256]{2,1,0:T(8,128)(2,1)S(1)} %get-tuple-element.77), channel_id=1, replica_groups=mesh['row'=16,'col'=8] {'row'}, dimensions={0} | all-to-all | bytes 524288 | tf_op jit(solution)/shard_map/all_to_all | solution.py:289
  158.7 2.9 shard_map.124.refs_1_.refs_3_.rows_ref
  161.5 1.3 shard_map.125
  162.9 10.6 %all_to_all.82.pairs_ref = bf16[16,32,256]{2,1,0:T(8,128)(2,1)S(1)} all-to-all(bf16[16,32,256]{2,1,0:T(8,128)(2,1)S(1)} %shard_map.125), channel_id=1, replica_groups=mesh['row'=16,'col'=8] {'row'}, dimensions={0} | all-to-all | bytes 524288 | tf_op jit(solution)/shard_map/all_to_all | solution.py:289
  174.2 10.8 %all_to_all.83.pairs_ref = bf16[16,32,256]{2,1,0:T(8,128)(2,1)S(1)} all-to-all(bf16[16,32,256]{2,1,0:T(8,128)(2,1)S(1)} %get-tuple-element.83), channel_id=1, replica_groups=mesh['row'=16,'col'=8] {'row'}, dimensions={0} | all-to-all | bytes 524288 | tf_op jit(solution)/shard_map/all_to_all | solution.py:289
  185.0 1.5 shard_map.127
  186.4 3.5 %all-to-all-start.11 = ((bf16[16,32,256]{2,1,0:T(8,128)(2,1)}), bf16[16,32,256]{2,1,0:T(8,128)(2,1)S(1)}, u32[]{:S(2)}, u32[]{:S(2)}) async-start(bf16[16,32,256]{2,1,0:T(8,128)(2,1)} %get-tuple-element.85), calls=%async_computation.12 | async-start | bytes 524288 | tf_op jit(solution)/shard_map/all_to_all | solution.py:289
  190.0 7.4 %all-to-all-done.11.pairs_ref = bf16[16,32,256]{2,1,0:T(8,128)(2,1)S(1)} async-done(((bf16[16,32,256]{2,1,0:T(8,128)(2,1)}), bf16[16,32,256]{2,1,0:T(8,128)(2,1)S(1)}, u32[]{:S(2)}, u32[]{:S(2)}) %all-to-all-start.11) | async-done | bytes 262176 | tf_op jit(solution)/shard_map/all_to_all | solution.py:289
  197.4 2.8 copy-done.2
  200.1 1.5 shard_map.128
  201.6 16.2 %all-gather.19.cloned.1.call-done = bf16[4096,256]{1,0:T(8,128)(2,1)} async-done(((bf16[32,256]{1,0:T(8,128)(2,1)}), bf16[4096,256]{1,0:T(8,128)(2,1)}) %all-gather.19.cloned.1.call-update) | async-done | bytes 2097168 | tf_op jit(solution)/shard_map/all_gather | solution.py:394
  217.8 66.6 %all-gather.17.cloned.1.call-done = bf16[4096,256]{1,0:T(8,128)(2,1)} async-done(((bf16[32,256]{1,0:T(8,128)(2,1)}), bf16[4096,256]{1,0:T(8,128)(2,1)}) %all-gather.17.cloned.1.call-update) | async-done | bytes 2097168 | tf_op jit(solution)/shard_map/all_gather | solution.py:394
  284.3 4.1 %all-to-all-start.12 = ((bf16[16,32,256]{2,1,0:T(8,128)(2,1)}), bf16[16,32,256]{2,1,0:T(8,128)(2,1)S(1)}, u32[]{:S(2)}, u32[]{:S(2)}) async-start(bf16[16,32,256]{2,1,0:T(8,128)(2,1)} %get-tuple-element.88), calls=%async_computation.13 | async-start | bytes 524288 | tf_op jit(solution)/shard_map/all_to_all | solution.py:289
  288.4 1.0 constant_dynamic-slice_fusion.2.refs_1_
  289.4 1.0 constant_dynamic-slice_fusion.3.refs_0_
  290.4 7.0 %shard_map.129.early_ref = f32[8,384,128]{2,1,0:T(8,128)S(1)} custom-call(bf16[2,8,32,256]{3,2,1,0:T(8,128)(2,1)S(1)} %constant_dynamic-slice_fusion.3.refs_0_, bf16[2,8,32,256]{3,2,1,0:T(8,128)(2,1)S(1)} %constant_dynamic-slice_fusion.2.refs_1_, bf16[256,256]{1,0:T(8,128)(2,1)S(1)} %compare_convert_fusion.refs_2_.hot_ref, bf16[3,3072,512]{2,1,0:T(8,128)(2,1)} %bitcast.23), custom_call_target="tpu_custom_call" | custom-call | flops 1610612736 | bytes 6291456 | tf_op jit(solution)/shard_map/pallas_call | solution.py:317
  297.4 0.8 shard_map.130
  298.2 3.9 %all-to-all-start.13 = ((bf16[8,32,640]{2,1,0:T(8,128)(2,1)}), bf16[8,32,640]{2,1,0:T(8,128)(2,1)S(1)}, u32[]{:S(2)}, u32[]{:S(2)}) async-start(bf16[8,32,640]{2,1,0:T(8,128)(2,1)} %shard_map.130), calls=%async_computation.14 | async-start | bytes 655360 | tf_op jit(solution)/shard_map/all_to_all | solution.py:406
  302.1 7.1 %all-to-all-done.13.got_ref = bf16[8,32,640]{2,1,0:T(8,128)(2,1)S(1)} async-done(((bf16[8,32,640]{2,1,0:T(8,128)(2,1)}), bf16[8,32,640]{2,1,0:T(8,128)(2,1)S(1)}, u32[]{:S(2)}, u32[]{:S(2)}) %all-to-all-start.13) | async-done | bytes 327712 | tf_op jit(solution)/shard_map/all_to_all | solution.py:406
  309.2 4.2 %shard_map.131 = (f32[4,384,128]{2,1,0:T(8,128)}, bf16[512,256]{1,0:T(8,128)(2,1)S(1)}) custom-call(s32[1]{0:T(128)} %bitcast.16.place_ref, bf16[8,32,640]{2,1,0:T(8,128)(2,1)S(1)} %all-to-all-done.13.got_ref, bf16[256,256]{1,0:T(8,128)(2,1)S(1)} %compare_convert_fusion.refs_2_.hot_ref, bf16[3,3072,512]{2,1,0:T(8,128)(2,1)} %bitcast.24, ...), custom_call_target="tpu_custom_call" | custom-call | flops 805306368 | bytes 3145728 | tf_op jit(solution)/shard_map/pallas_call | solution.py:423
  313.4 1.1 collective-permute-start
  314.5 2.9 shard_map.132
  317.4 2.1 add.111
  319.5 3.6 %all-to-all-start.14 = ((f32[4,384,128]{2,1,0:T(8,128)}), f32[4,384,128]{2,1,0:T(8,128)S(1)}, u32[]{:S(2)}, u32[]{:S(2)}) async-start(f32[4,384,128]{2,1,0:T(8,128)} %add.111), calls=%async_computation.15 | async-start | bytes 1572864 | tf_op jit(solution)/shard_map/all_to_all | solution.py:448
  323.1 1.0 constant_dynamic-slice_fusion.1
  324.1 1.0 constant_dynamic-slice_fusion
  325.3 0.7 copy.17
  326.0 9.4 %all-to-all-done.14 = f32[4,384,128]{2,1,0:T(8,128)S(1)} async-done(((f32[4,384,128]{2,1,0:T(8,128)}), f32[4,384,128]{2,1,0:T(8,128)S(1)}, u32[]{:S(2)}, u32[]{:S(2)}) %all-to-all-start.14) | async-done | bytes 786464 | tf_op jit(solution)/shard_map/all_to_all | solution.py:448
  (62 shorter events, 6.2 us)
Async XLA Ops:
  7.2 14.3 %copy-start = (f32[3,256,128]{2,1,0:T(8,128)S(1)}, f32[3,256,128]{2,1,0:T(8,128)}, u32[]{:S(2)}) copy-start(f32[3,256,128]{2,1,0:T(8,128)} %param.13) | copy-start | bytes 1179652
  7.2 36.6 %all-gather.11.cloned.1.call-start = ((), (), s32[]{:S(2)}) async-start(), calls=%async_computation.17 | async-start | bytes 2359296 | tf_op jit(solution)/shard_map/all_gather | solution.py:234
  9.0 12.3 %copy-start.6 = (s32[128]{0:T(128)S(1)}, s32[128]{0:T(128)}, u32[]{:S(2)}) copy-start(s32[128]{0:T(128)} %param.17) | copy-start | bytes 1540
  9.0 12.8 %copy-start.7 = (f32[128]{0:T(128)S(1)}, f32[128]{0:T(128)}, u32[]{:S(2)}) copy-start(f32[128]{0:T(128)} %param.15) | copy-start | bytes 1540
  9.0 12.8 %copy-start.5 = (s32[128]{0:T(128)S(1)}, s32[128]{0:T(128)}, u32[]{:S(2)}) copy-start(s32[128]{0:T(128)} %param.16) | copy-start | bytes 1540
  15.2 11.7 %slice-start = ((bf16[3,256,512]{2,1,0:T(8,128)(2,1)}), bf16[1,256,512]{2,1,0:T(8,128)(2,1)S(1)}, s32[]{:S(2)}) async-start(bf16[3,256,512]{2,1,0:T(8,128)(2,1)} %param.10), calls=%async_computation.22 | async-start | bytes 524288 | tf_op jit(solution)/shard_map/slice | solution.py:279
  15.2 11.7 %slice-start.2 = ((bf16[3,256,512]{2,1,0:T(8,128)(2,1)}), bf16[1,256,512]{2,1,0:T(8,128)(2,1)S(1)}, s32[]{:S(2)}) async-start(bf16[3,256,512]{2,1,0:T(8,128)(2,1)} %param.12), calls=%async_computation.24 | async-start | bytes 524288 | tf_op jit(solution)/shard_map/slice | solution.py:279
  15.2 11.3 %all-to-all-start = ((f32[8,16,256]{2,1,0:T(8,128)}), f32[8,16,256]{2,1,0:T(8,128)S(1)}, u32[]{:S(2)}, u32[]{:S(2)}) async-start(f32[8,16,256]{2,1,0:T(8,128)} %get-tuple-element.51), calls=%async_computation | async-start | bytes 262144 | tf_op jit(solution)/shard_map/all_to_all | solution.py:262
  21.3 53.7 %reduce-scatter.2.cloned.1.call-start = ((), (), s32[]{:S(2)}) async-start(), calls=%async_computation.16 | async-start | bytes 294912 | tf_op jit(solution)/shard_map/reduce_scatter | solution.py:293
  26.9 79.2 %all-gather.13.cloned.1.call-start = ((), (), s32[]{:S(2)}) async-start(), calls=%async_computation.18 | async-start | bytes 4718592 | tf_op jit(solution)/shard_map/all_gather | solution.py:279
  27.8 130.8 %all-gather.15.cloned.1.call-start = ((), (), s32[]{:S(2)}) async-start(), calls=%async_computation.19 | async-start | bytes 7077888 | tf_op jit(solution)/shard_map/all_gather | solution.py:372
  45.4 1.0 slice-start.1
  45.4 1.1 slice-start.3
  47.5 170.3 %all-gather.19.cloned.1.call-start = ((), (), s32[]{:S(2)}) async-start(), calls=%async_computation.21 | async-start | bytes 2113536 | tf_op jit(solution)/shard_map/all_gather | solution.py:394
  71.3 10.8 %all-to-all-start.4 = ((bf16[16,32,256]{2,1,0:T(8,128)(2,1)}), bf16[16,32,256]{2,1,0:T(8,128)(2,1)S(1)}, u32[]{:S(2)}, u32[]{:S(2)}) async-start(bf16[16,32,256]{2,1,0:T(8,128)(2,1)} %get-tuple-element.67), calls=%async_computation.4 | async-start | bytes 524288 | tf_op jit(solution)/shard_map/all_to_all | solution.py:289
  74.9 209.5 %all-gather.17.cloned.1.call-start = ((), (), s32[]{:S(2)}) async-start(), calls=%async_computation.20 | async-start | bytes 2113536 | tf_op jit(solution)/shard_map/all_gather | solution.py:394
  106.0 2.2 copy-start.3
  161.5 23.5 %copy-start.1 = (bf16[8,3,256,512]{3,2,1,0:T(8,128)(2,1)}, bf16[8,3,256,512]{3,2,1,0:T(8,128)(2,1)S(1)}, u32[]{:S(2)}) copy-start(bf16[8,3,256,512]{3,2,1,0:T(8,128)(2,1)S(1)} %shard_map.124.refs_1_.refs_3_.rows_ref) | copy-start | bytes 18874372
  186.4 10.9 %all-to-all-start.11 = ((bf16[16,32,256]{2,1,0:T(8,128)(2,1)}), bf16[16,32,256]{2,1,0:T(8,128)(2,1)S(1)}, u32[]{:S(2)}, u32[]{:S(2)}) async-start(bf16[16,32,256]{2,1,0:T(8,128)(2,1)} %get-tuple-element.85), calls=%async_computation.12 | async-start | bytes 524288 | tf_op jit(solution)/shard_map/all_to_all | solution.py:289
  197.4 2.8 copy-start.2
  284.3 13.1 %all-to-all-start.12 = ((bf16[16,32,256]{2,1,0:T(8,128)(2,1)}), bf16[16,32,256]{2,1,0:T(8,128)(2,1)S(1)}, u32[]{:S(2)}, u32[]{:S(2)}) async-start(bf16[16,32,256]{2,1,0:T(8,128)(2,1)} %get-tuple-element.88), calls=%async_computation.13 | async-start | bytes 524288 | tf_op jit(solution)/shard_map/all_to_all | solution.py:289
  298.2 11.0 %all-to-all-start.13 = ((bf16[8,32,640]{2,1,0:T(8,128)(2,1)}), bf16[8,32,640]{2,1,0:T(8,128)(2,1)S(1)}, u32[]{:S(2)}, u32[]{:S(2)}) async-start(bf16[8,32,640]{2,1,0:T(8,128)(2,1)} %shard_map.130), calls=%async_computation.14 | async-start | bytes 655360 | tf_op jit(solution)/shard_map/all_to_all | solution.py:406
  313.4 4.0 %collective-permute-start = (f32[4,384,128]{2,1,0:T(8,128)}, f32[4,384,128]{2,1,0:T(8,128)}, u32[]{:S(2)}, u32[]{:S(2)}) collective-permute-start(f32[4,384,128]{2,1,0:T(8,128)} %get-tuple-element.99), channel_id=1, source_target_pairs={{0,1},{1,0},{2,3},{3,2},{4,5},{5,4},{6,7},{7,6},{8,9},{9,8},{10,11... | collective-permute-start | bytes 2359304 | tf_op jit(solution)/shard_map/ppermute | solution.py:435
  319.5 16.0 %copy-start.4 = (f32[384,128]{1,0:T(8,128)S(1)}, f32[384,128]{1,0:T(8,128)}, u32[]{:S(2)}) copy-start(f32[384,128]{1,0:T(8,128)} %param.19) | copy-start | bytes 589828
  319.5 16.0 %all-to-all-start.14 = ((f32[4,384,128]{2,1,0:T(8,128)}), f32[4,384,128]{2,1,0:T(8,128)S(1)}, u32[]{:S(2)}, u32[]{:S(2)}) async-start(f32[4,384,128]{2,1,0:T(8,128)} %add.111), calls=%async_computation.15 | async-start | bytes 1572864 | tf_op jit(solution)/shard_map/all_to_all | solution.py:448
Sparse Core Ops, SparseCore 0:
  9.7 28.9 all-gather.10
  41.1 29.3 reduce-scatter.1
  72.1 33.8 all-gather.12
  107.6 40.7 all-gather.14
  152.0 65.7 all-gather.18
  221.4 62.9 all-gather.16

commit v5 on v4

--- a/solution.py
+++ b/solution.py
@@ -43,17 +43,17 @@
         send_ref[peer] = pair
 
 
-def first_kernel(parts_ref, forcing_ref, send_ref):
+def first_kernel(parts_ref, forcing_ref, rest_ref, send_ref):
     width = send_ref.shape[2]
-    rhs = forcing_ref[:, -width:] - jnp.sum(parts_ref[...], axis=0)
-    send_to_all(send_ref, pair_of(rhs))
+    rhs = forcing_ref[...] - jnp.sum(parts_ref[...], axis=0)
+    rest_ref[...] = rhs[:, :-width]
+    send_to_all(send_ref, pair_of(rhs[:, -width:]))
 
 
 def rhs_kernel(step, uses, *refs):
-    forcing_ref, old_ref, send_ref = refs[-3:]
+    rhs_ref, send_ref = refs[-2:]
     width = send_ref.shape[2]
-    here = slice(step * width, (step + 1) * width)
-    rhs = forcing_ref[:, here] - old_ref[:, here]
+    rhs = rhs_ref[:, step * width : (step + 1) * width]
     for k, which in enumerate(uses):
         rhs = rhs - rows_product(refs[2 * k], refs[2 * k + 1], which)
     send_to_all(send_ref, pair_of(rhs))
@@ -89,6 +89,22 @@
     pair = pair_of(jnp.where(row < limit_ref[...], total, 0.0))
     own_ref[...] = pair
     send_to_all(send_ref, pair)
+
+
+def last_streamed_kernel(
+    which, pairs_ref, rows_ref, scale_ref, old_ref, limit_ref, send_ref, own_ref, tiles_ref, sems
+):
+    copies = [
+        pltpu.make_async_copy(rows_ref.at[k, which], tiles_ref.at[k, 0], sems.at[k])
+        for k in range(rows_ref.shape[0])
+    ]
+    for copy in copies:
+        copy.start()
+    for copy in copies:
+        copy.wait()
+    last_term_kernel(
+        0, pairs_ref, tiles_ref, scale_ref, old_ref, limit_ref, send_ref, own_ref
+    )
 
 
 def columns_kernel(whole_ref, own_ref, send_ref):
@@ -117,66 +133,87 @@
     return product[:, :half] + product[:, half:]
 
 
-def z_early_kernel(*refs):
+def z_early_kernel(place_ref, *refs):
     hot_ref, z_ref, out_ref, picked_ref = refs[-4:]
     gots = refs[:-4]
 
     @pl.when(pl.program_id(0) == 0)
     def _():
         for k, got_ref in enumerate(gots):
-            per, cols, _, width = got_ref.shape
+            cols, per, _, width = got_ref.shape
             for j in range(per):
-                blocks = [got_ref[j, col] for col in range(cols)]
+                blocks = [got_ref[col, j] for col in range(cols)]
                 picked_ref[k, j * width : (j + 1) * width] = pick(blocks, hot_ref)
 
     out = None
     for k in range(len(gots)):
         part = jnp.dot(z_ref[k], picked_ref[k], preferred_element_type=F32)
         out = part if out is None else out + part
-    out_ref[0] = fold(out)
-
-
-def z_first_kernel(place_ref, got_ref, hot_ref, z_ref, early_ref, out_ref, picked_ref):
+    out_ref[...] = fold(out).reshape(out_ref.shape)
+
+
+def z_tiles(place_ref, z_ref, early_ref, tiles_ref, adds_ref, sems):
+    copies = []
+    count, size, _ = tiles_ref.shape
+    for k in range(count):
+        block = 2 * k + place_ref[0]
+        rows = pl.ds(pl.multiple_of(block * size, size), size)
+        copies.append(
+            (
+                pltpu.make_async_copy(z_ref.at[0, rows], tiles_ref.at[k], sems.at[0, k]),
+                pltpu.make_async_copy(early_ref.at[block], adds_ref.at[k], sems.at[1, k]),
+            )
+        )
+        for copy in copies[-1]:
+            copy.start()
+    return copies
+
+
+def z_products(copies, picked, tiles_ref, adds_ref, out_ref):
+    for k, both in enumerate(copies):
+        for copy in both:
+            copy.wait()
+        product = jnp.dot(tiles_ref[k], picked, preferred_element_type=F32)
+        out_ref[k] = adds_ref[k] + fold(product)
+
+
+def z_first_kernel(
+    place_ref, got_ref, hot_ref, z_ref, early_ref, out_ref, picked_ref, tiles_ref, adds_ref, sems
+):
+    copies = z_tiles(place_ref, z_ref, early_ref, tiles_ref, adds_ref, sems)
     depth = z_ref.shape[2]
-
-    @pl.when(pl.program_id(0) == 0)
-    def _():
-        blocks = [got_ref[k, :, :depth] for k in range(got_ref.shape[0])]
-        picked_ref[...] = pick(blocks, hot_ref)
-
-    z_next_kernel(place_ref, picked_ref, z_ref, early_ref, out_ref)
-
-
-def z_next_kernel(place_ref, picked_ref, z_ref, early_ref, out_ref):
-    product = jnp.dot(z_ref[0], picked_ref[...], preferred_element_type=F32)
-    out_ref[0] = early_ref[0] + fold(product)
-
-
-def old_kernel(base_ref, t_ref, old_ref, starts_ref, out_ref, rest_ref, sum_ref):
+    picked_ref[...] = pick([got_ref[k, :, :depth] for k in range(got_ref.shape[0])], hot_ref)
+    z_products(copies, picked_ref[...], tiles_ref, adds_ref, out_ref)
+
+
+def z_next_kernel(place_ref, picked_ref, z_ref, early_ref, out_ref, tiles_ref, adds_ref, sems):
+    copies = z_tiles(place_ref, z_ref, early_ref, tiles_ref, adds_ref, sems)
+    z_products(copies, picked_ref[...], tiles_ref, adds_ref, out_ref)
+
+
+def old_kernel(base_ref, t_ref, old_ref, starts_ref, out_ref, sum_ref):
     k = pl.program_id(0)
     chunk = old_ref.shape[0]
     steps, rows, _ = t_ref.shape
     row = base_ref[0] + k * chunk + lax.broadcasted_iota(jnp.int32, old_ref.shape, 0)
     old = jnp.where(row < starts_ref[...], old_ref[...].astype(F32), 0.0).astype(BF16)
-    for step in range(steps):
-        part = jnp.dot(t_ref[step], old, preferred_element_type=F32)
-        here = pl.ds(step * rows, rows)
-
-        @pl.when(k == 0)
-        def _():
-            sum_ref[here] = part
-
-        @pl.when(k > 0)
-        def _():
-            sum_ref[here] += part
+    t = t_ref[...].reshape(steps * rows, chunk)
+    part = jnp.dot(t, old, preferred_element_type=F32)
+
+    @pl.when(k == 0)
+    def _():
+        sum_ref[...] = part
+
+    @pl.when(k > 0)
+    def _():
+        sum_ref[...] += part
 
     @pl.when(k == pl.num_programs(0) - 1)
     def _():
         group = out_ref.shape[1]
-        last = sum_ref[(steps - 1) * rows :].T
+        whole = sum_ref[...].T
         for col in range(out_ref.shape[0]):
-            out_ref[col] = last[col * group : (col + 1) * group]
-        rest_ref[...] = sum_ref[: (steps - 1) * rows].T
+            out_ref[col] = whole[col * group : (col + 1) * group]
 
 
 def call(kernel, outs, *args, flops=0):
@@ -234,11 +271,10 @@
     gathered = {2: gather(inverses[2:3])}
 
     old_base = steps * full_rows + col_idx * old_cols
-    old_part, old_rest = pl.pallas_call(
+    (old_part,) = pl.pallas_call(
         old_kernel,
         out_shape=[
-            shape((n_col, group, row_block), F32),
-            shape((width, (steps - 1) * row_block), F32),
+            shape((n_col, group, steps * row_block), F32),
         ],
         grid_spec=pltpu.PrefetchScalarGridSpec(
             num_scalar_prefetch=1,
@@ -249,8 +285,7 @@
                 pl.BlockSpec((1, width), lambda k, base: (0, 0)),
             ],
             out_specs=[
-                pl.BlockSpec((n_col, group, row_block), lambda k, base: (0, 0, 0)),
-                pl.BlockSpec((width, (steps - 1) * row_block), lambda k, base: (0, 0)),
+                pl.BlockSpec((n_col, group, steps * row_block), lambda k, base: (0, 0, 0)),
             ],
             scratch_shapes=[pltpu.VMEM((steps * row_block, width), F32)],
         ),
@@ -288,9 +323,8 @@
     def spread(send):
         return lax.all_to_all(send, "row", 0, 0)
 
-    (send,) = call(first_kernel, [send_shape], old_part, forcing_t)
-    send, old_rest = lax.optimization_barrier((send, old_rest))
-    old_rest = lax.psum_scatter(old_rest, "col", scatter_dimension=0, tiled=True)
+    rest_shape = shape((group, (steps - 1) * row_block), F32)
+    rhs_rest, send = call(first_kernel, [rest_shape, send_shape], old_part, forcing_t)
     early = list(range(1, steps))
     per = n_row // n_col
     z_rows = z_cols.shape[0]
@@ -310,36 +344,43 @@
     def early_z():
         gots = []
         for step in early:
-            blocks = everywhere[step].reshape(n_row, n_col, 2 * group, row_block)
-            gots.append(lax.dynamic_slice_in_dim(blocks, per * col_idx, per, 0))
-            rows = lax.dynamic_index_in_dim(blocks, row_idx, 0, keepdims=False)
+            blocks = everywhere[step]
+            gots.append(blocks)
+            rows = lax.dynamic_index_in_dim(blocks, row_idx, 1, keepdims=False)
             mine.append(lax.dynamic_slice_in_dim(rows, col_idx * share, share, 2))
+        tile = 2
         (out,) = pl.pallas_call(
             z_early_kernel,
-            out_shape=[shape((n_col, z_block, width), F32)],
-            grid=(n_col,),
-            in_specs=[pl.BlockSpec(got.shape, lambda i: (0, 0, 0, 0)) for got in gots]
-            + [
-                pl.BlockSpec(hot.shape, lambda i: (0, 0)),
-                pl.BlockSpec(
-                    (pl.Element(steps - 1), pl.Element(z_block), pl.Element(col_block)),
-                    lambda i: (1, i * z_block, 0),
-                ),
-            ],
-            out_specs=[pl.BlockSpec((1, z_block, width), lambda i: (i, 0, 0))],
-            scratch_shapes=[pltpu.VMEM((steps - 1, col_block, 2 * width), BF16)],
+            out_shape=[pltpu.HBM((n_col, z_block, width), F32)],
+            grid_spec=pltpu.PrefetchScalarGridSpec(
+                num_scalar_prefetch=1,
+                grid=(n_col // tile,),
+                in_specs=[
+                    pl.BlockSpec(
+                        (n_col, per, 2 * group, row_block), lambda i, place: (0, place[0], 0, 0)
+                    )
+                    for _ in gots
+                ]
+                + [
+                    pl.BlockSpec(hot.shape, lambda i, place: (0, 0)),
+                    pl.BlockSpec(
+                        (pl.Element(steps - 1), pl.Element(tile * z_block), pl.Element(col_block)),
+                        lambda i, place: (1, i * (tile * z_block), 0),
+                    ),
+                ],
+                out_specs=[pl.BlockSpec((tile, z_block, width), lambda i, place: (i, 0, 0))],
+                scratch_shapes=[pltpu.VMEM((steps - 1, col_block, 2 * width), BF16)],
+            ),
             compiler_params=z_params,
             cost_estimate=cost(steps - 1),
-        )(*gots, hot, z_t)
+        )(col_idx[None], *[in_hbm(got) for got in gots], hot, z_t)
         return out
 
     whole = {}
     own = {}
     for step in reversed(range(steps)):
         if step < steps - 1:
-            got, rows, old_rest = lax.optimization_barrier(
-                (whole[step + 1], gathered[step], old_rest)
-            )
+            got, rows = lax.optimization_barrier((whole[step + 1], gathered[step]))
             rows = load(rows)
             whole[step + 1] = got
             args = []
@@ -351,8 +392,7 @@
                 ),
                 [send_shape],
                 *args,
-                forcing_t,
-                old_rest,
+                rhs_rest,
                 flops=flops * (steps - 1 - step),
             )
             got = spread(send)
@@ -380,21 +420,39 @@
                 total,
                 flops=flops,
             )
-        send, own[step] = call(
-            functools.partial(last_term_kernel, which),
-            [send_shape, own_shape],
-            spread(send),
-            rows,
-            my_offsets,
-            total,
-            limits[step],
-            flops=flops,
-        )
         if step > 0:
-            everywhere[step] = lax.all_gather(own[step], ("row", "col"), axis=0)
+            send, own[step] = call(
+                functools.partial(last_term_kernel, which),
+                [send_shape, own_shape],
+                spread(send),
+                rows,
+                my_offsets,
+                total,
+                limits[step],
+                flops=flops,
+            )
         else:
+            vm = pl.BlockSpec(memory_space=pltpu.VMEM)
+            rows = gathered[0]
+            send, own[0] = pl.pallas_call(
+                functools.partial(last_streamed_kernel, which),
+                out_shape=[send_shape, own_shape],
+                in_specs=[vm, pl.BlockSpec(memory_space=pltpu.HBM), vm, vm, vm],
+                out_specs=[vm, vm],
+                scratch_shapes=[
+                    pltpu.VMEM((n_col, 1, row_block, col_block), BF16),
+                    pltpu.SemaphoreType.DMA((n_col,)),
+                ],
+                compiler_params=pltpu.CompilerParams(vmem_limit_bytes=VMEM_LIMIT),
+                cost_estimate=pl.CostEstimate(
+                    flops=flops, bytes_accessed=2 * row_block * full_rows, transcendentals=0
+                ),
+            )(spread(send), in_hbm(rows), my_offsets, total, limits[0])
+        if step == 0:
             own[0], everywhere = lax.optimization_barrier((own[0], everywhere))
         whole[step] = spread(send)
+        if step > 0:
+            everywhere[step] = gather(whole[step])
     whole[0], early_part = lax.optimization_barrier((whole[0], early_z()))
 
     (send,) = call(
@@ -412,23 +470,23 @@
     mine = mine[:, :, :group] + mine[:, :, group:]
     solved = jnp.transpose(mine, (0, 3, 1, 2)).reshape(steps, share, width)
 
-    def fixed(array_shape):
-        return pl.BlockSpec(array_shape, lambda i, place: (0,) * len(array_shape))
-
-    z_spec = pl.BlockSpec((1, z_block, col_block), lambda i, place: (0, 2 * i + place[0], 0))
-    early_spec = pl.BlockSpec((1, z_block, width), lambda i, place: (2 * i + place[0], 0, 0))
-    out_spec = pl.BlockSpec((1, z_block, width), lambda i, place: (i, 0, 0))
-    part_shape = pltpu.VMEM((n_col // 2, z_block, width), F32)
+    part_shape = shape((n_col // 2, z_block, width), F32)
     picked_shape = shape((col_block, 2 * width), BF16)
+    in_vm = pl.BlockSpec(memory_space=pltpu.VMEM)
+    in_hb = pl.BlockSpec(memory_space=pltpu.HBM)
+    scalar = pl.BlockSpec(memory_space=pltpu.SMEM)
+    scratch = [
+        pltpu.VMEM((n_col // 2, z_block, col_block), BF16),
+        pltpu.VMEM((n_col // 2, z_block, width), F32),
+        pltpu.SemaphoreType.DMA((2, n_col // 2)),
+    ]
+    early_part = in_hbm(early_part)
     theirs, picked = pl.pallas_call(
         z_first_kernel,
         out_shape=[part_shape, picked_shape],
-        grid_spec=pltpu.PrefetchScalarGridSpec(
-            num_scalar_prefetch=1,
-            grid=(n_col // 2,),
-            in_specs=[fixed(got.shape), fixed(hot.shape), z_spec, early_spec],
-            out_specs=[out_spec, fixed(picked_shape.shape)],
-        ),
+        in_specs=[scalar, in_vm, in_vm, in_hb, in_hb],
+        out_specs=[in_vm, in_vm],
+        scratch_shapes=scratch,
         compiler_params=z_params,
         cost_estimate=cost(1),
     )((1 - core)[None], got, hot, z_t, early_part)
@@ -436,12 +494,9 @@
     (ours,) = pl.pallas_call(
         z_next_kernel,
         out_shape=[part_shape],
-        grid_spec=pltpu.PrefetchScalarGridSpec(
-            num_scalar_prefetch=1,
-            grid=(n_col // 2,),
-            in_specs=[fixed(picked_shape.shape), z_spec, early_spec],
-            out_specs=[out_spec],
-        ),
+        in_specs=[scalar, in_vm, in_hb, in_hb],
+        out_specs=[in_vm],
+        scratch_shapes=scratch,
         compiler_params=z_params,
         cost_estimate=cost(1),
     )(core[None], picked, z_t, early_part)

time: 345 us -> 246 us (0.71)
  waiting for transfers between devices: 142 us -> 26.6 us
  blocking collectives: 106 us -> 123 us
  starting transfers between devices: 26.1 us -> 35.1 us
  local copies, waits for them, and re-layouts: 10.3 us -> 5.59 us
    all_gather x2, waiting for transfers between devices: 82.7 us -> 0.04 us  [body(): everywhere[step] = gather(whole[step])]
    all_gather x1, waiting for transfers between devices: 23.9 us -> 0.02 us  [body(): gathered[1] = gather(jnp.concatenate([t_upper[2:3], inverses[1:2]]))]
    all_to_all x9 -> x11, blocking collectives: 106 us -> 123 us  [spread(): return lax.all_to_all(send, 'row', 0, 0)]
    all_to_all x1, starting transfers between devices: 3.9 us -> 20.3 us  [body(): got = lax.all_to_all(send, 'col', 0, 0)]
    all_to_all x3 -> x1, waiting for transfers between devices: 14.6 us -> 1.44 us  [spread(): return lax.all_to_all(send, 'row', 0, 0)]
    all_to_all x3 -> x1, starting transfers between devices: 11.1 us -> 3.7 us  [spread(): return lax.all_to_all(send, 'row', 0, 0)]
    dynamic_slice x4 -> x0, local copies, waits for them, and re-layouts: 3.96 us -> none  [the longest x2 2.01 us: early_z(): mine.append(lax.dynamic_slice_in_dim(rows, col_idx * share, share, 2))]
    all_to_all x1, waiting for transfers between devices: 4.63 us -> 8.49 us  [body(): old_part = lax.all_to_all(old_part, 'col', 0, 0)]
  transfers between devices with their start and end apart: 13 -> 10, of which waited for: 8 -> 4; matrix products, arithmetic and copies ran while one was open for 2% -> 2% of each run, Pallas kernels for 10% -> 14%
where the time goes in v5:
time: 246 us; the launch traced here: 245 us
  blocking collectives  123 us (50%)
  Pallas kernels  36.6 us (15%)
  starting transfers between devices  35.1 us (14%)
  waiting for transfers between devices  26.6 us (11%)
  between operations  14.1 us (6%)
  local copies, waits for them, and re-layouts  5.59 us (2%)
  other arithmetic  3.8 us (2%)
    all_to_all x11, blocking collectives, spread(): return lax.all_to_all(send, 'row', 0, 0)  123 us
    all_to_all x1, starting transfers between devices, body(): got = lax.all_to_all(send, 'col', 0, 0)  20.3 us
    pallas_call x12, Pallas kernels, call(): pl.pallas_call(kernel, out_shape=outs, in_specs=[pl.BlockSpec(memory_spac...  9.89 us
    all_to_all x1, waiting for transfers between devices, body(): lax.all_to_all(ours + swapped, 'col', 0, 0, axis_index_groups=[list(range...  9.35 us
    all_to_all x1, waiting for transfers between devices, body(): old_part = lax.all_to_all(old_part, 'col', 0, 0)  8.49 us
    pallas_call x3, Pallas kernels, load(): pl.pallas_call(load_kernel, out_shape=[pltpu.VMEM(values.shape, values.dt...  7.27 us
    all_to_all x1, waiting for transfers between devices, body(): got = lax.all_to_all(send, 'col', 0, 0)  7.11 us
    pallas_call x1, Pallas kernels, early_z(): pl.pallas_call(z_early_kernel, out_shape=[pltpu.HBM((n_col, z_block, widt...  6.13 us
  transfers between devices with their start and end apart: 10, of which 4 were waited for; matrix products, arithmetic and copies ran while one was open for 2% of the time, Pallas kernels for 14%

profile of v5, /device:TPU:1, one launch (start us, length us, event | category | flops | bytes accessed | tf_op | source)
XLA Modules:
  0.0 244.7 jit_solution(3741109361982260711)
XLA Ops:
  7.2 1.7 slice.21
  9.0 5.2 %shard_map.113 = f32[8,16,768]{2,1,0:T(8,128)} custom-call(s32[1]{0:T(128)} %bitcast.base_ref, bf16[3,256,3072]{2,1,0:T(8,128)(2,1)} %t_ref.1, bf16[3072,128]{1,0:T(8,128)(2,1)} %old_ref.1, s32[1,128]{1,0:T(1,128)} %bitcast.36), custom_call_target="tpu_custom_call" | custom-call | flops 603979776 | bytes 4718592 | tf_op jit(solution)/shard_map/pallas_call | solution.py:274
  14.2 6.1 %all-to-all-start = ((f32[8,16,768]{2,1,0:T(8,128)}), f32[8,16,768]{2,1,0:T(8,128)S(1)}, u32[]{:S(2)}, u32[]{:S(2)}) async-start(f32[8,16,768]{2,1,0:T(8,128)} %shard_map.113), calls=%async_computation | async-start | bytes 786432 | tf_op jit(solution)/shard_map/all_to_all | solution.py:297
  20.9 8.5 %all-to-all-done.parts_ref = f32[8,16,768]{2,1,0:T(8,128)S(1)} async-done(((f32[8,16,768]{2,1,0:T(8,128)}), f32[8,16,768]{2,1,0:T(8,128)S(1)}, u32[]{:S(2)}, u32[]{:S(2)}) %all-to-all-start) | async-done | bytes 393248 | tf_op jit(solution)/shard_map/all_to_all | solution.py:297
  29.7 0.8 pad_maximum_fusion.1
  30.6 16.0 %all_to_all.75.pairs_ref = bf16[16,32,256]{2,1,0:T(8,128)(2,1)S(1)} all-to-all(bf16[16,32,256]{2,1,0:T(8,128)(2,1)S(1)} %get-tuple-element.47), channel_id=1, replica_groups=mesh['row'=16,'col'=8] {'row'}, dimensions={0} | all-to-all | bytes 524288 | tf_op jit(solution)/shard_map/all_to_all | solution.py:324
  46.7 1.6 shard_map.115.rows_ref
  48.3 0.7 shard_map.116
  49.0 0.3 slice-done.1
  49.4 1.0 pad_maximum_fusion
  50.4 10.7 %all_to_all.76.pairs_ref = bf16[16,32,256]{2,1,0:T(8,128)(2,1)S(1)} all-to-all(bf16[16,32,256]{2,1,0:T(8,128)(2,1)S(1)} %get-tuple-element.53), channel_id=1, replica_groups=mesh['row'=16,'col'=8] {'row'}, dimensions={0} | all-to-all | bytes 524288 | tf_op jit(solution)/shard_map/all_to_all | solution.py:324
  61.0 0.7 shard_map.117
  61.8 10.9 %all_to_all.77.pairs_ref = bf16[16,32,256]{2,1,0:T(8,128)(2,1)S(1)} all-to-all(bf16[16,32,256]{2,1,0:T(8,128)(2,1)S(1)} %get-tuple-element.56), channel_id=1, replica_groups=mesh['row'=16,'col'=8] {'row'}, dimensions={0} | all-to-all | bytes 524288 | tf_op jit(solution)/shard_map/all_to_all | solution.py:324
  72.7 1.3 shard_map.118
  74.0 11.0 %all_to_all.78.refs_0_.refs_2_ = bf16[16,32,256]{2,1,0:T(8,128)(2,1)} all-to-all(bf16[16,32,256]{2,1,0:T(8,128)(2,1)S(1)} %get-tuple-element.59), channel_id=1, replica_groups=mesh['row'=16,'col'=8] {'row'}, dimensions={0} | all-to-all | bytes 524288 | tf_op jit(solution)/shard_map/all_to_all | solution.py:324
  85.2 2.6 %shard_map.119.refs_1_.rows_ref = bf16[8,2,256,512]{3,2,1,0:T(8,128)(2,1)S(1)} custom-call(bf16[8,2,256,512]{3,2,1,0:T(8,128)(2,1)} %bitcast.29), custom_call_target="tpu_custom_call" | custom-call | bytes 4194304 | tf_op jit(solution)/shard_map/pallas_call | solution.py:240
  87.8 0.7 shard_map.120
  88.5 10.1 %all_to_all.79.pairs_ref = bf16[16,32,256]{2,1,0:T(8,128)(2,1)S(1)} all-to-all(bf16[16,32,256]{2,1,0:T(8,128)(2,1)S(1)} %shard_map.120), channel_id=1, replica_groups=mesh['row'=16,'col'=8] {'row'}, dimensions={0} | all-to-all | bytes 524288 | tf_op jit(solution)/shard_map/all_to_all | solution.py:324
  98.7 0.7 shard_map.121
  99.4 10.9 %all_to_all.80.pairs_ref = bf16[16,32,256]{2,1,0:T(8,128)(2,1)S(1)} all-to-all(bf16[16,32,256]{2,1,0:T(8,128)(2,1)S(1)} %get-tuple-element.63), channel_id=1, replica_groups=mesh['row'=16,'col'=8] {'row'}, dimensions={0} | all-to-all | bytes 524288 | tf_op jit(solution)/shard_map/all_to_all | solution.py:324
  110.3 0.7 shard_map.122
  111.1 10.9 %all_to_all.81.pairs_ref = bf16[16,32,256]{2,1,0:T(8,128)(2,1)S(1)} all-to-all(bf16[16,32,256]{2,1,0:T(8,128)(2,1)S(1)} %get-tuple-element.65), channel_id=1, replica_groups=mesh['row'=16,'col'=8] {'row'}, dimensions={0} | all-to-all | bytes 524288 | tf_op jit(solution)/shard_map/all_to_all | solution.py:324
  122.0 1.3 shard_map.123
  123.3 10.6 %all_to_all.82.refs_0_ = bf16[16,32,256]{2,1,0:T(8,128)(2,1)} all-to-all(bf16[16,32,256]{2,1,0:T(8,128)(2,1)S(1)} %get-tuple-element.68), channel_id=1, replica_groups=mesh['row'=16,'col'=8] {'row'}, dimensions={0} | all-to-all | bytes 524288 | tf_op jit(solution)/shard_map/all_to_all | solution.py:324
  134.0 3.1 %shard_map.124.refs_1_.refs_3_.rows_ref = bf16[8,3,256,512]{3,2,1,0:T(8,128)(2,1)S(1)} custom-call(bf16[8,3,256,512]{3,2,1,0:T(8,128)(2,1)} %bitcast.27), custom_call_target="tpu_custom_call" | custom-call | bytes 6291456 | tf_op jit(solution)/shard_map/pallas_call | solution.py:240
  137.1 1.3 shard_map.125
  138.4 10.4 %all_to_all.83.pairs_ref = bf16[16,32,256]{2,1,0:T(8,128)(2,1)S(1)} all-to-all(bf16[16,32,256]{2,1,0:T(8,128)(2,1)S(1)} %shard_map.125), channel_id=1, replica_groups=mesh['row'=16,'col'=8] {'row'}, dimensions={0} | all-to-all | bytes 524288 | tf_op jit(solution)/shard_map/all_to_all | solution.py:324
  148.8 0.7 shard_map.126
  149.5 10.7 %all_to_all.84.pairs_ref = bf16[16,32,256]{2,1,0:T(8,128)(2,1)S(1)} all-to-all(bf16[16,32,256]{2,1,0:T(8,128)(2,1)S(1)} %get-tuple-element.73), channel_id=1, replica_groups=mesh['row'=16,'col'=8] {'row'}, dimensions={0} | all-to-all | bytes 524288 | tf_op jit(solution)/shard_map/all_to_all | solution.py:324
  160.2 0.7 shard_map.127
  160.9 10.8 %all_to_all.85.pairs_ref = bf16[16,32,256]{2,1,0:T(8,128)(2,1)S(1)} all-to-all(bf16[16,32,256]{2,1,0:T(8,128)(2,1)S(1)} %get-tuple-element.75), channel_id=1, replica_groups=mesh['row'=16,'col'=8] {'row'}, dimensions={0} | all-to-all | bytes 524288 | tf_op jit(solution)/shard_map/all_to_all | solution.py:324
  171.7 3.0 %shard_map.128 = (bf16[16,32,256]{2,1,0:T(8,128)(2,1)}, bf16[32,256]{1,0:T(8,128)(2,1)S(1)}) custom-call(bf16[16,32,256]{2,1,0:T(8,128)(2,1)S(1)} %all_to_all.85.pairs_ref, bf16[8,3,256,512]{3,2,1,0:T(8,128)(2,1)} %bitcast.28, f32[16,256]{1,0:T(8,128)S(1)} %broadcast_in_dim.35.scale_ref, f32[16,256]{1,0:T(8,128)S(1)} %get-tuple-element.76.old_ref, ...), custom_call_target="tpu_custom_call" | custom-call | flops 67108864 | bytes 2097152 | tf_op jit(solution)/shard_map/pallas_call | solution.py:437
  174.7 3.7 %all-to-all-start.12 = ((bf16[16,32,256]{2,1,0:T(8,128)(2,1)}), bf16[16,32,256]{2,1,0:T(8,128)(2,1)S(1)}, u32[]{:S(2)}, u32[]{:S(2)}) async-start(bf16[16,32,256]{2,1,0:T(8,128)(2,1)} %get-tuple-element.78), calls=%async_computation.12 | async-start | bytes 524288 | tf_op jit(solution)/shard_map/all_to_all | solution.py:324
  178.5 6.1 %shard_map.129.early_ref = f32[8,384,128]{2,1,0:T(8,128)} custom-call(s32[1]{0:T(128)} %bitcast.7.place_ref, bf16[8,16,32,256]{3,2,1,0:T(8,128)(2,1)} %bitcast.32, bf16[8,16,32,256]{3,2,1,0:T(8,128)(2,1)} %bitcast.30, bf16[256,256]{1,0:T(8,128)(2,1)S(1)} %compare_convert_fusion.refs_2_.hot_ref, bf16[3,3072,512]{2,1,0:T(8,128)(2,1)} %bitcast.24), custom_call_target="tpu_custom_call" | custom-call | flops 1610612736 | bytes 6291456 | tf_op jit(solution)/shard_map/pallas_call | solution.py:352
  184.6 1.4 all-to-all-done.12.whole_ref
  186.0 0.8 shard_map.130
  186.8 20.3 %all-to-all-start.13 = ((bf16[8,32,640]{2,1,0:T(8,128)(2,1)}), bf16[8,32,640]{2,1,0:T(8,128)(2,1)S(1)}, u32[]{:S(2)}, u32[]{:S(2)}) async-start(bf16[8,32,640]{2,1,0:T(8,128)(2,1)} %shard_map.130), calls=%async_computation.13 | async-start | bytes 655360 | tf_op jit(solution)/shard_map/all_to_all | solution.py:464
  207.1 7.1 %all-to-all-done.13.got_ref = bf16[8,32,640]{2,1,0:T(8,128)(2,1)S(1)} async-done(((bf16[8,32,640]{2,1,0:T(8,128)(2,1)}), bf16[8,32,640]{2,1,0:T(8,128)(2,1)S(1)}, u32[]{:S(2)}, u32[]{:S(2)}) %all-to-all-start.13) | async-done | bytes 327712 | tf_op jit(solution)/shard_map/all_to_all | solution.py:464
  214.2 2.5 %shard_map.131 = (f32[4,384,128]{2,1,0:T(8,128)S(1)}, bf16[512,256]{1,0:T(8,128)(2,1)S(1)}) custom-call(s32[1]{0:T(128)} %bitcast.17.place_ref, bf16[8,32,640]{2,1,0:T(8,128)(2,1)S(1)} %all-to-all-done.13.got_ref, bf16[256,256]{1,0:T(8,128)(2,1)S(1)} %compare_convert_fusion.refs_2_.hot_ref, bf16[3,3072,512]{2,1,0:T(8,128)(2,1)} %bitcast.25, ...), custom_call_target="tpu_custom_call" | custom-call | flops 805306368 | bytes 3145728 | tf_op jit(solution)/shard_map/pallas_call | solution.py:484
  216.8 1.2 collective-permute-start
  218.0 2.5 %shard_map.132 = f32[4,384,128]{2,1,0:T(8,128)S(1)} custom-call(s32[1]{0:T(128)} %bitcast.16.place_ref, bf16[512,256]{1,0:T(8,128)(2,1)S(1)} %get-tuple-element.86.picked_ref, bf16[3,3072,512]{2,1,0:T(8,128)(2,1)} %bitcast.26, f32[8,384,128]{2,1,0:T(8,128)} %shard_map.129.early_ref), custom_call_target="tpu_custom_call" | custom-call | flops 805306368 | bytes 3145728 | tf_op jit(solution)/shard_map/pallas_call | solution.py:494
  220.5 1.0 add.104
  221.5 3.6 %all-to-all-start.14 = ((f32[4,384,128]{2,1,0:T(8,128)}), f32[4,384,128]{2,1,0:T(8,128)S(1)}, u32[]{:S(2)}, u32[]{:S(2)}) async-start(f32[4,384,128]{2,1,0:T(8,128)} %add.104), calls=%async_computation.14 | async-start | bytes 1572864 | tf_op jit(solution)/shard_map/all_to_all | solution.py:503
  225.1 1.0 dynamic-slice_bitcast_fusion.1
  226.1 1.0 dynamic-slice_bitcast_fusion
  227.4 0.7 copy.16
  228.1 9.3 %all-to-all-done.14 = f32[4,384,128]{2,1,0:T(8,128)S(1)} async-done(((f32[4,384,128]{2,1,0:T(8,128)}), f32[4,384,128]{2,1,0:T(8,128)S(1)}, u32[]{:S(2)}, u32[]{:S(2)}) %all-to-all-start.14) | async-done | bytes 786464 | tf_op jit(solution)/shard_map/all_to_all | solution.py:503
  237.5 0.7 add.105
  (53 shorter events, 1.6 us)
Async XLA Ops:
  7.2 13.1 %copy-start = (f32[3,256,128]{2,1,0:T(8,128)S(1)}, f32[3,256,128]{2,1,0:T(8,128)}, u32[]{:S(2)}) copy-start(f32[3,256,128]{2,1,0:T(8,128)} %param.13) | copy-start | bytes 1179652
  7.2 39.5 %all-gather.11.cloned.1.call-start = ((), (), s32[]{:S(2)}) async-start(), calls=%async_computation.15 | async-start | bytes 2359296 | tf_op jit(solution)/shard_map/all_gather | solution.py:271
  9.0 11.5 %copy-start.5 = (s32[128]{0:T(128)S(1)}, s32[128]{0:T(128)}, u32[]{:S(2)}) copy-start(s32[128]{0:T(128)} %param.17) | copy-start | bytes 1540
  9.0 11.5 %copy-start.4 = (s32[128]{0:T(128)S(1)}, s32[128]{0:T(128)}, u32[]{:S(2)}) copy-start(s32[128]{0:T(128)} %param.16) | copy-start | bytes 1540
  9.0 11.7 %copy-start.6 = (f32[128]{0:T(128)S(1)}, f32[128]{0:T(128)}, u32[]{:S(2)}) copy-start(f32[128]{0:T(128)} %param.15) | copy-start | bytes 1540
  14.2 15.5 %slice-start = ((bf16[3,256,512]{2,1,0:T(8,128)(2,1)}), bf16[1,256,512]{2,1,0:T(8,128)(2,1)S(1)}, s32[]{:S(2)}) async-start(bf16[3,256,512]{2,1,0:T(8,128)(2,1)} %param.10), calls=%async_computation.20 | async-start | bytes 524288 | tf_op jit(solution)/shard_map/slice | solution.py:314
  14.2 15.5 %slice-start.2 = ((bf16[3,256,512]{2,1,0:T(8,128)(2,1)}), bf16[1,256,512]{2,1,0:T(8,128)(2,1)S(1)}, s32[]{:S(2)}) async-start(bf16[3,256,512]{2,1,0:T(8,128)(2,1)} %param.12), calls=%async_computation.22 | async-start | bytes 524288 | tf_op jit(solution)/shard_map/slice | solution.py:314
  14.2 15.2 %all-to-all-start = ((f32[8,16,768]{2,1,0:T(8,128)}), f32[8,16,768]{2,1,0:T(8,128)S(1)}, u32[]{:S(2)}, u32[]{:S(2)}) async-start(f32[8,16,768]{2,1,0:T(8,128)} %shard_map.113), calls=%async_computation | async-start | bytes 786432 | tf_op jit(solution)/shard_map/all_to_all | solution.py:297
  20.3 64.8 %all-gather.13.cloned.1.call-start = ((), (), s32[]{:S(2)}) async-start(), calls=%async_computation.16 | async-start | bytes 4718592 | tf_op jit(solution)/shard_map/all_gather | solution.py:314
  30.6 103.4 %all-gather.15.cloned.1.call-start = ((), (), s32[]{:S(2)}) async-start(), calls=%async_computation.17 | async-start | bytes 7077888 | tf_op jit(solution)/shard_map/all_gather | solution.py:412
  48.2 1.0 slice-start.1
  48.3 1.1 slice-start.3
  50.3 128.1 %all-gather.19.cloned.1.call-start = ((), (), s32[]{:S(2)}) async-start(), calls=%async_computation.19 | async-start | bytes 2359296 | tf_op jit(solution)/shard_map/all_gather | solution.py:455
  85.1 93.4 %all-gather.17.cloned.1.call-start = ((), (), s32[]{:S(2)}) async-start(), calls=%async_computation.18 | async-start | bytes 2359296 | tf_op jit(solution)/shard_map/all_gather | solution.py:455
  85.1 2.6 %copy-start.1 = (bf16[16,32,256]{2,1,0:T(8,128)(2,1)S(1)}, bf16[16,32,256]{2,1,0:T(8,128)(2,1)}, u32[]{:S(2)}) copy-start(bf16[16,32,256]{2,1,0:T(8,128)(2,1)} %all_to_all.78.refs_0_.refs_2_) | copy-start | bytes 786436
  134.0 3.1 %copy-start.2 = (bf16[16,32,256]{2,1,0:T(8,128)(2,1)S(1)}, bf16[16,32,256]{2,1,0:T(8,128)(2,1)}, u32[]{:S(2)}) copy-start(bf16[16,32,256]{2,1,0:T(8,128)(2,1)} %all_to_all.82.refs_0_) | copy-start | bytes 786436
  174.7 11.3 %all-to-all-start.12 = ((bf16[16,32,256]{2,1,0:T(8,128)(2,1)}), bf16[16,32,256]{2,1,0:T(8,128)(2,1)S(1)}, u32[]{:S(2)}, u32[]{:S(2)}) async-start(bf16[16,32,256]{2,1,0:T(8,128)(2,1)} %get-tuple-element.78), calls=%async_computation.12 | async-start | bytes 524288 | tf_op jit(solution)/shard_map/all_to_all | solution.py:324
  186.8 27.4 %all-to-all-start.13 = ((bf16[8,32,640]{2,1,0:T(8,128)(2,1)}), bf16[8,32,640]{2,1,0:T(8,128)(2,1)S(1)}, u32[]{:S(2)}, u32[]{:S(2)}) async-start(bf16[8,32,640]{2,1,0:T(8,128)(2,1)} %shard_map.130), calls=%async_computation.13 | async-start | bytes 655360 | tf_op jit(solution)/shard_map/all_to_all | solution.py:464
  216.8 3.8 %collective-permute-start = (f32[4,384,128]{2,1,0:T(8,128)S(1)}, f32[4,384,128]{2,1,0:T(8,128)S(1)}, u32[]{:S(2)}, u32[]{:S(2)}) collective-permute-start(f32[4,384,128]{2,1,0:T(8,128)S(1)} %get-tuple-element.87), channel_id=1, source_target_pairs={{0,1},{1,0},{2,3},{3,2},{4,5},{5,4},{6,7},{7,6},{8,9},{9,8},{10,11... | collective-permute-start | bytes 2359304 | tf_op jit(solution)/shard_map/ppermute | solution.py:493
  221.5 16.0 %copy-start.3 = (f32[384,128]{1,0:T(8,128)S(1)}, f32[384,128]{1,0:T(8,128)}, u32[]{:S(2)}) copy-start(f32[384,128]{1,0:T(8,128)} %param.19) | copy-start | bytes 589828
  221.5 15.9 %all-to-all-start.14 = ((f32[4,384,128]{2,1,0:T(8,128)}), f32[4,384,128]{2,1,0:T(8,128)S(1)}, u32[]{:S(2)}, u32[]{:S(2)}) async-start(f32[4,384,128]{2,1,0:T(8,128)} %add.104), calls=%async_computation.14 | async-start | bytes 1572864 | tf_op jit(solution)/shard_map/all_to_all | solution.py:503
Sparse Core Ops, SparseCore 0:
  9.7 30.3 all-gather.10
  41.8 32.8 all-gather.12
  76.4 40.7 all-gather.14
  118.8 25.3 all-gather.18
  145.8 25.6 all-gather.16

commit v6 on v5

--- a/solution.py
+++ b/solution.py
@@ -15,12 +15,14 @@
 CHUNK = 768
 
 
-def rows_product(pairs_ref, rows_ref, which):
+def rows_product(pairs_ref, rows_ref, which, copies=None):
     blocks, _, width = pairs_ref.shape
     per = blocks // rows_ref.shape[0]
     out = None
     for block in range(blocks):
         first = (block % per) * width
+        if copies is not None and first == 0:
+            copies[block // per].wait()
         part = lax.dot_general(
             pairs_ref[block],
             rows_ref[block // per, which, :, first : first + width],
@@ -50,24 +52,42 @@
     send_to_all(send_ref, pair_of(rhs[:, -width:]))
 
 
+def stream(rows_ref, uses, tiles_ref, sems):
+    copies = []
+    for k, which in enumerate(uses):
+        copies.append(
+            [
+                pltpu.make_async_copy(rows_ref.at[j, which], tiles_ref.at[j, k], sems.at[j, k])
+                for j in range(rows_ref.shape[0])
+            ]
+        )
+        for copy in copies[-1]:
+            copy.start()
+    return copies
+
+
 def rhs_kernel(step, uses, *refs):
-    rhs_ref, send_ref = refs[-2:]
+    rows_ref, rhs_ref, send_ref, tiles_ref, sems, pairs_ref, pair_sems = refs[-7:]
+    count = len(uses)
+    firsts = [
+        pltpu.make_async_copy(refs[k], pairs_ref.at[k], pair_sems.at[k]) for k in range(count)
+    ]
+    for copy in firsts:
+        copy.start()
+    copies = stream(rows_ref, uses, tiles_ref, sems)
     width = send_ref.shape[2]
     rhs = rhs_ref[:, step * width : (step + 1) * width]
-    for k, which in enumerate(uses):
-        rhs = rhs - rows_product(refs[2 * k], refs[2 * k + 1], which)
+    for k in range(count):
+        firsts[k].wait()
+        rhs = rhs - rows_product(pairs_ref.at[k], tiles_ref, k, copies[k])
     send_to_all(send_ref, pair_of(rhs))
 
 
-def load_kernel(from_ref, to_ref, sems):
-    count = from_ref.shape[0]
-    copies = [
-        pltpu.make_async_copy(from_ref.at[k], to_ref.at[k], sems.at[k]) for k in range(count)
-    ]
-    for copy in copies:
-        copy.start()
-    for copy in copies:
-        copy.wait()
+def first_streamed_kernel(which, pairs_ref, rows_ref, send_ref, total_ref, tiles_ref, sems):
+    copies = stream(rows_ref, [which], tiles_ref, sems)
+    term = rows_product(pairs_ref, tiles_ref, 0, copies[0])
+    total_ref[...] = term
+    send_to_all(send_ref, pair_of(term))
 
 
 def first_term_kernel(which, pairs_ref, rows_ref, send_ref, total_ref):
@@ -89,22 +109,6 @@
     pair = pair_of(jnp.where(row < limit_ref[...], total, 0.0))
     own_ref[...] = pair
     send_to_all(send_ref, pair)
-
-
-def last_streamed_kernel(
-    which, pairs_ref, rows_ref, scale_ref, old_ref, limit_ref, send_ref, own_ref, tiles_ref, sems
-):
-    copies = [
-        pltpu.make_async_copy(rows_ref.at[k, which], tiles_ref.at[k, 0], sems.at[k])
-        for k in range(rows_ref.shape[0])
-    ]
-    for copy in copies:
-        copy.start()
-    for copy in copies:
-        copy.wait()
-    last_term_kernel(
-        0, pairs_ref, tiles_ref, scale_ref, old_ref, limit_ref, send_ref, own_ref
-    )
 
 
 def columns_kernel(whole_ref, own_ref, send_ref):
@@ -236,19 +240,33 @@
     return pltpu.with_memory_space_constraint(values, pltpu.HBM)
 
 
-def load(values):
-    (out,) = pl.pallas_call(
-        load_kernel,
-        out_shape=[pltpu.VMEM(values.shape, values.dtype)],
-        in_specs=[pl.BlockSpec(memory_space=pltpu.HBM)],
-        out_specs=[pl.BlockSpec(memory_space=pltpu.VMEM)],
-        scratch_shapes=[pltpu.SemaphoreType.DMA((values.shape[0],))],
+def call_streamed(kernel, uses, outs, vectors, rows, rest=(), stream_vectors=False, flops=0):
+    vm = pl.BlockSpec(memory_space=pltpu.VMEM)
+    hb = pl.BlockSpec(memory_space=pltpu.HBM)
+    cols, _, height, width = rows.shape
+    scratch = [
+        pltpu.VMEM((cols, len(uses), height, width), rows.dtype),
+        pltpu.SemaphoreType.DMA((cols, len(uses))),
+    ]
+    if stream_vectors:
+        scratch += [
+            pltpu.VMEM((len(vectors), *vectors[0].shape), vectors[0].dtype),
+            pltpu.SemaphoreType.DMA((len(vectors),)),
+        ]
+        vectors = [in_hbm(vector) for vector in vectors]
+    return pl.pallas_call(
+        kernel,
+        out_shape=outs,
+        in_specs=[hb if stream_vectors else vm] * len(vectors) + [hb] + [vm] * len(rest),
+        out_specs=[vm] * len(outs),
+        scratch_shapes=scratch,
         compiler_params=pltpu.CompilerParams(vmem_limit_bytes=VMEM_LIMIT),
         cost_estimate=pl.CostEstimate(
-            flops=0, bytes_accessed=values.size * values.dtype.itemsize, transcendentals=0
+            flops=flops,
+            bytes_accessed=2 * len(uses) * cols * height * width,
+            transcendentals=0,
         ),
-    )(in_hbm(values))
-    return out
+    )(*vectors, in_hbm(rows), *rest)
 
 
 def body(t_upper, t_old, inverses, forcing, x_old, offsets, starts, column_map, z_cols, acc):
@@ -268,7 +286,6 @@
         return lax.dynamic_slice_in_dim(values, col_idx * group, group, 0)
 
     gather = functools.partial(lax.all_gather, axis_name="col", axis=0)
-    gathered = {2: gather(inverses[2:3])}
 
     old_base = steps * full_rows + col_idx * old_cols
     (old_part,) = pl.pallas_call(
@@ -294,6 +311,8 @@
             flops=2 * t_old.size * width, bytes_accessed=2 * t_old.size, transcendentals=0
         ),
     )(old_base[None], in_hbm(t_old), in_hbm(x_old), in_hbm(starts[None, :]))
+    old_part, inverses = lax.optimization_barrier((old_part, inverses))
+    gathered = {2: gather(inverses[2:3])}
     old_part = lax.all_to_all(old_part, "col", 0, 0)
 
     core = col_idx % 2
@@ -317,7 +336,7 @@
 
     send_shape = pltpu.VMEM((n_row, 2 * group, row_block), BF16)
     vec_shape = shape((group, row_block), F32)
-    own_shape = shape((2 * group, row_block), BF16)
+    own_shape = pltpu.VMEM((2 * group, row_block), BF16)
     flops = 4 * group * row_block * full_rows
 
     def spread(send):
@@ -380,36 +399,39 @@
     own = {}
     for step in reversed(range(steps)):
         if step < steps - 1:
-            got, rows = lax.optimization_barrier((whole[step + 1], gathered[step]))
-            rows = load(rows)
-            whole[step + 1] = got
-            args = []
-            for later in range(step + 1, steps):
-                args += [whole[later], rows]
-            (send,) = call(
-                functools.partial(
-                    rhs_kernel, step, [which_upper[step, j] for j in range(step + 1, steps)]
-                ),
+            later = range(step + 1, steps)
+            uses = [which_upper[step, j] for j in later]
+            (send,) = call_streamed(
+                functools.partial(rhs_kernel, step, uses),
+                uses,
                 [send_shape],
-                *args,
-                rhs_rest,
-                flops=flops * (steps - 1 - step),
+                [whole[j] for j in later],
+                gathered[step],
+                [rhs_rest],
+                stream_vectors=True,
+                flops=flops * len(uses),
             )
-            got = spread(send)
-        else:
-            got, rows = lax.optimization_barrier((spread(send), gathered[step]))
-            rows = load(rows)
         which = which_inv[step]
-        send, total = call(
-            functools.partial(first_term_kernel, which),
-            [send_shape, vec_shape],
-            got,
-            rows,
-            flops=flops,
-        )
+        rows = in_vmem(gathered[step])
         if step == steps - 1:
+            send, total = call_streamed(
+                functools.partial(first_streamed_kernel, which),
+                [which],
+                [send_shape, vec_shape],
+                [spread(send)],
+                gathered[step],
+                flops=flops,
+            )
             send, t_upper, inverses = lax.optimization_barrier((send, t_upper, inverses))
             gathered[0] = gather(jnp.concatenate([t_upper[:2], inverses[:1]]))
+        else:
+            send, total = call(
+                functools.partial(first_term_kernel, which),
+                [send_shape, vec_shape],
+                spread(send),
+                rows,
+                flops=flops,
+            )
         for extra in range(1, NEUMANN - 1):
             send, total = call(
                 functools.partial(next_term_kernel, which),
@@ -420,34 +442,16 @@
                 total,
                 flops=flops,
             )
-        if step > 0:
-            send, own[step] = call(
-                functools.partial(last_term_kernel, which),
-                [send_shape, own_shape],
-                spread(send),
-                rows,
-                my_offsets,
-                total,
-                limits[step],
-                flops=flops,
-            )
-        else:
-            vm = pl.BlockSpec(memory_space=pltpu.VMEM)
-            rows = gathered[0]
-            send, own[0] = pl.pallas_call(
-                functools.partial(last_streamed_kernel, which),
-                out_shape=[send_shape, own_shape],
-                in_specs=[vm, pl.BlockSpec(memory_space=pltpu.HBM), vm, vm, vm],
-                out_specs=[vm, vm],
-                scratch_shapes=[
-                    pltpu.VMEM((n_col, 1, row_block, col_block), BF16),
-                    pltpu.SemaphoreType.DMA((n_col,)),
-                ],
-                compiler_params=pltpu.CompilerParams(vmem_limit_bytes=VMEM_LIMIT),
-                cost_estimate=pl.CostEstimate(
-                    flops=flops, bytes_accessed=2 * row_block * full_rows, transcendentals=0
-                ),
-            )(spread(send), in_hbm(rows), my_offsets, total, limits[0])
+        send, own[step] = call(
+            functools.partial(last_term_kernel, which),
+            [send_shape, own_shape],
+            spread(send),
+            rows,
+            my_offsets,
+            total,
+            limits[step],
+            flops=flops,
+        )
         if step == 0:
             own[0], everywhere = lax.optimization_barrier((own[0], everywhere))
         whole[step] = spread(send)

time: 246 us -> 243 us (0.988)
  blocking collectives: 123 us -> 126 us
  starting transfers between devices: 35.1 us -> 32.2 us
    all_to_all x11, blocking collectives: 123 us -> 126 us  [spread(): return lax.all_to_all(send, 'row', 0, 0)]
    all_to_all x1, starting transfers between devices: 20.3 us -> 17.7 us  [body(): got = lax.all_to_all(send, 'col', 0, 0)]
    pallas_call x12 -> x10, Pallas kernels: 9.89 us -> 8.54 us  [call(): pl.pallas_call(kernel, out_shape=outs, in_specs=[pl.BlockSpec(memory_spac...]
    pallas_call x4 -> x3, Pallas kernels: 10.3 us -> 10.6 us  [call_streamed(): pl.pallas_call(kernel, out_shape=outs, in_specs=[hb if stream_vectors els...]
  transfers between devices with their start and end apart: 10 -> 10, of which waited for: 4 -> 4; matrix products, arithmetic and copies ran while one was open for 2% -> 2% of each run, Pallas kernels for 14% -> 11%
where the time goes in v6:
time: 243 us; the launch traced here: 242 us
  blocking collectives  126 us (52%)
  Pallas kernels  35.5 us (15%)
  starting transfers between devices  32.2 us (13%)
  waiting for transfers between devices  26.1 us (11%)
  between operations  14.1 us (6%)
  local copies, waits for them, and re-layouts  4.28 us (2%)
  other arithmetic  3.77 us (2%)
    all_to_all x11, blocking collectives, spread(): return lax.all_to_all(send, 'row', 0, 0)  126 us
    all_to_all x1, starting transfers between devices, body(): got = lax.all_to_all(send, 'col', 0, 0)  17.7 us
    pallas_call x3, Pallas kernels, call_streamed(): pl.pallas_call(kernel, out_shape=outs, in_specs=[hb if stream_vectors els...  10.6 us
    all_to_all x1, waiting for transfers between devices, body(): lax.all_to_all(ours + swapped, 'col', 0, 0, axis_index_groups=[list(range...  9.35 us
    pallas_call x10, Pallas kernels, call(): pl.pallas_call(kernel, out_shape=outs, in_specs=[pl.BlockSpec(memory_spac...  8.54 us
    all_to_all x1, waiting for transfers between devices, body(): got = lax.all_to_all(send, 'col', 0, 0)  7.09 us
    all_to_all x1, waiting for transfers between devices, body(): old_part = lax.all_to_all(old_part, 'col', 0, 0)  7.07 us
    pallas_call x1, Pallas kernels, early_z(): pl.pallas_call(z_early_kernel, out_shape=[pltpu.HBM((n_col, z_block, widt...  6.11 us
  transfers between devices with their start and end apart: 10, of which 4 were waited for; matrix products, arithmetic and copies ran while one was open for 2% of the time, Pallas kernels for 11%

profile of v6, /device:TPU:1, one launch (start us, length us, event | category | flops | bytes accessed | tf_op | source)
XLA Modules:
  0.0 241.8 jit_solution(11951247512634997725)
XLA Ops:
  7.2 5.2 %shard_map.113 = f32[8,16,768]{2,1,0:T(8,128)} custom-call(s32[1]{0:T(128)} %bitcast.base_ref, bf16[3,256,3072]{2,1,0:T(8,128)(2,1)} %t_ref.1, bf16[3072,128]{1,0:T(8,128)(2,1)} %old_ref.1, s32[1,128]{1,0:T(1,128)} %bitcast.43), custom_call_target="tpu_custom_call" | custom-call | flops 603979776 | bytes 4718592 | tf_op jit(solution)/shard_map/pallas_call | solution.py:291
  12.5 0.7 slice.21
  13.3 6.0 %all-to-all-start = ((f32[8,16,768]{2,1,0:T(8,128)}), f32[8,16,768]{2,1,0:T(8,128)S(1)}, u32[]{:S(2)}, u32[]{:S(2)}) async-start(f32[8,16,768]{2,1,0:T(8,128)} %shard_map.113), calls=%async_computation | async-start | bytes 786432 | tf_op jit(solution)/shard_map/all_to_all | solution.py:316
  19.3 0.2 constant_dynamic-slice_fusion
  19.6 0.1 copy.17
  19.8 0.1 compare_convert_fusion.refs_2_.hot_ref
  19.9 7.1 %all-to-all-done.parts_ref = f32[8,16,768]{2,1,0:T(8,128)S(1)} async-done(((f32[8,16,768]{2,1,0:T(8,128)}), f32[8,16,768]{2,1,0:T(8,128)S(1)}, u32[]{:S(2)}, u32[]{:S(2)}) %all-to-all-start) | async-done | bytes 393248 | tf_op jit(solution)/shard_map/all_to_all | solution.py:316
  27.3 0.8 pad_maximum_fusion.1
  28.2 14.7 %all_to_all.75.pairs_ref = bf16[16,32,256]{2,1,0:T(8,128)(2,1)S(1)} all-to-all(bf16[16,32,256]{2,1,0:T(8,128)(2,1)S(1)} %get-tuple-element.45), channel_id=1, replica_groups=mesh['row'=16,'col'=8] {'row'}, dimensions={0} | all-to-all | bytes 524288 | tf_op jit(solution)/shard_map/all_to_all | solution.py:343
  42.9 2.5 %shard_map.115 = (bf16[16,32,256]{2,1,0:T(8,128)(2,1)S(1)}, f32[16,256]{1,0:T(8,128)S(1)}) custom-call(bf16[16,32,256]{2,1,0:T(8,128)(2,1)S(1)} %all_to_all.75.pairs_ref, bf16[8,1,256,512]{3,2,1,0:T(8,128)(2,1)} %bitcast.31), custom_call_target="tpu_custom_call" | custom-call | flops 67108864 | bytes 2097152 | tf_op jit(solution)/shard_map/pallas_call | solution.py:257
  45.5 0.9 pad_maximum_fusion
  46.5 13.5 %all_to_all.76.pairs_ref = bf16[16,32,256]{2,1,0:T(8,128)(2,1)S(1)} all-to-all(bf16[16,32,256]{2,1,0:T(8,128)(2,1)S(1)} %get-tuple-element.49), channel_id=1, replica_groups=mesh['row'=16,'col'=8] {'row'}, dimensions={0} | all-to-all | bytes 524288 | tf_op jit(solution)/shard_map/all_to_all | solution.py:343
  60.0 0.7 shard_map.116
  60.8 10.9 %all_to_all.77.pairs_ref = bf16[16,32,256]{2,1,0:T(8,128)(2,1)S(1)} all-to-all(bf16[16,32,256]{2,1,0:T(8,128)(2,1)S(1)} %get-tuple-element.52), channel_id=1, replica_groups=mesh['row'=16,'col'=8] {'row'}, dimensions={0} | all-to-all | bytes 524288 | tf_op jit(solution)/shard_map/all_to_all | solution.py:343
  71.6 1.3 shard_map.117
  73.0 11.1 %all_to_all.78.refs_0_.refs_1_ = bf16[16,32,256]{2,1,0:T(8,128)(2,1)} all-to-all(bf16[16,32,256]{2,1,0:T(8,128)(2,1)S(1)} %get-tuple-element.55), channel_id=1, replica_groups=mesh['row'=16,'col'=8] {'row'}, dimensions={0} | all-to-all | bytes 524288 | tf_op jit(solution)/shard_map/all_to_all | solution.py:343
  84.2 3.1 %shard_map.118 = bf16[16,32,256]{2,1,0:T(8,128)(2,1)S(1)} custom-call(bf16[16,32,256]{2,1,0:T(8,128)(2,1)} %all_to_all.78.refs_0_.refs_1_, bf16[8,2,256,512]{3,2,1,0:T(8,128)(2,1)} %bitcast.27, f32[16,512]{1,0:T(8,128)S(1)} %get-tuple-element.56.refs_2_.refs_3_), custom_call_target="tpu_custom_call" | custom-call | flops 67108864 | bytes 2097152 | tf_op jit(solution)/shard_map/pallas_call | solution.py:257
  87.3 10.7 %all_to_all.79.pairs_ref = bf16[16,32,256]{2,1,0:T(8,128)(2,1)S(1)} all-to-all(bf16[16,32,256]{2,1,0:T(8,128)(2,1)S(1)} %shard_map.118), channel_id=1, replica_groups=mesh['row'=16,'col'=8] {'row'}, dimensions={0} | all-to-all | bytes 524288 | tf_op jit(solution)/shard_map/all_to_all | solution.py:343
  98.0 0.7 shard_map.119
  98.8 10.9 %all_to_all.80.pairs_ref = bf16[16,32,256]{2,1,0:T(8,128)(2,1)S(1)} all-to-all(bf16[16,32,256]{2,1,0:T(8,128)(2,1)S(1)} %get-tuple-element.57), channel_id=1, replica_groups=mesh['row'=16,'col'=8] {'row'}, dimensions={0} | all-to-all | bytes 524288 | tf_op jit(solution)/shard_map/all_to_all | solution.py:343
  109.7 0.7 shard_map.120
  110.4 10.9 %all_to_all.81.pairs_ref = bf16[16,32,256]{2,1,0:T(8,128)(2,1)S(1)} all-to-all(bf16[16,32,256]{2,1,0:T(8,128)(2,1)S(1)} %get-tuple-element.59), channel_id=1, replica_groups=mesh['row'=16,'col'=8] {'row'}, dimensions={0} | all-to-all | bytes 524288 | tf_op jit(solution)/shard_map/all_to_all | solution.py:343
  121.3 1.3 shard_map.121
  122.7 10.6 %all_to_all.82.refs_0_ = bf16[16,32,256]{2,1,0:T(8,128)(2,1)} all-to-all(bf16[16,32,256]{2,1,0:T(8,128)(2,1)S(1)} %get-tuple-element.62), channel_id=1, replica_groups=mesh['row'=16,'col'=8] {'row'}, dimensions={0} | all-to-all | bytes 524288 | tf_op jit(solution)/shard_map/all_to_all | solution.py:343
  133.3 4.9 %shard_map.122 = bf16[16,32,256]{2,1,0:T(8,128)(2,1)S(1)} custom-call(bf16[16,32,256]{2,1,0:T(8,128)(2,1)} %all_to_all.82.refs_0_, bf16[16,32,256]{2,1,0:T(8,128)(2,1)} %all_to_all.78.refs_0_.refs_1_, bf16[8,3,256,512]{3,2,1,0:T(8,128)(2,1)} %bitcast.23, f32[16,512]{1,0:T(8,128)S(1)} %get-tuple-element.56.refs_2_.refs_3_), custom_call_target="tpu_custom_call" | custom-call | flops 134217728 | bytes 4194304 | tf_op jit(solution)/shard_map/pallas_call | solution.py:257
  138.3 10.6 %all_to_all.83.pairs_ref = bf16[16,32,256]{2,1,0:T(8,128)(2,1)S(1)} all-to-all(bf16[16,32,256]{2,1,0:T(8,128)(2,1)S(1)} %shard_map.122), channel_id=1, replica_groups=mesh['row'=16,'col'=8] {'row'}, dimensions={0} | all-to-all | bytes 524288 | tf_op jit(solution)/shard_map/all_to_all | solution.py:343
  148.9 0.7 shard_map.123
  149.7 10.5 %all_to_all.84.pairs_ref = bf16[16,32,256]{2,1,0:T(8,128)(2,1)S(1)} all-to-all(bf16[16,32,256]{2,1,0:T(8,128)(2,1)S(1)} %get-tuple-element.65), channel_id=1, replica_groups=mesh['row'=16,'col'=8] {'row'}, dimensions={0} | all-to-all | bytes 524288 | tf_op jit(solution)/shard_map/all_to_all | solution.py:343
  160.2 0.7 shard_map.124
  160.9 11.3 %all_to_all.85.pairs_ref = bf16[16,32,256]{2,1,0:T(8,128)(2,1)S(1)} all-to-all(bf16[16,32,256]{2,1,0:T(8,128)(2,1)S(1)} %get-tuple-element.67), channel_id=1, replica_groups=mesh['row'=16,'col'=8] {'row'}, dimensions={0} | all-to-all | bytes 524288 | tf_op jit(solution)/shard_map/all_to_all | solution.py:343
  172.2 1.4 shard_map.125
  173.6 3.5 %all-to-all-start.12 = ((bf16[16,32,256]{2,1,0:T(8,128)(2,1)}), bf16[16,32,256]{2,1,0:T(8,128)(2,1)S(1)}, u32[]{:S(2)}, u32[]{:S(2)}) async-start(bf16[16,32,256]{2,1,0:T(8,128)(2,1)} %get-tuple-element.70), calls=%async_computation.12 | async-start | bytes 524288 | tf_op jit(solution)/shard_map/all_to_all | solution.py:343
  177.2 6.1 %shard_map.126.early_ref = f32[8,384,128]{2,1,0:T(8,128)} custom-call(s32[1]{0:T(128)} %bitcast.7.place_ref, bf16[8,16,32,256]{3,2,1,0:T(8,128)(2,1)} %bitcast.40, bf16[8,16,32,256]{3,2,1,0:T(8,128)(2,1)} %bitcast.38, bf16[256,256]{1,0:T(8,128)(2,1)S(1)} %compare_convert_fusion.refs_2_.hot_ref, bf16[3,3072,512]{2,1,0:T(8,128)(2,1)} %bitcast.35), custom_call_target="tpu_custom_call" | custom-call | flops 1610612736 | bytes 6291456 | tf_op jit(solution)/shard_map/pallas_call | solution.py:371
  183.3 2.4 %all-to-all-done.12.whole_ref = bf16[16,32,256]{2,1,0:T(8,128)(2,1)S(1)} async-done(((bf16[16,32,256]{2,1,0:T(8,128)(2,1)}), bf16[16,32,256]{2,1,0:T(8,128)(2,1)S(1)}, u32[]{:S(2)}, u32[]{:S(2)}) %all-to-all-start.12) | async-done | bytes 262176 | tf_op jit(solution)/shard_map/all_to_all | solution.py:343
  185.7 0.8 shard_map.127
  186.5 17.7 %all-to-all-start.13 = ((bf16[8,32,640]{2,1,0:T(8,128)(2,1)}), bf16[8,32,640]{2,1,0:T(8,128)(2,1)S(1)}, u32[]{:S(2)}, u32[]{:S(2)}) async-start(bf16[8,32,640]{2,1,0:T(8,128)(2,1)} %shard_map.127), calls=%async_computation.13 | async-start | bytes 655360 | tf_op jit(solution)/shard_map/all_to_all | solution.py:468
  204.2 7.1 %all-to-all-done.13.got_ref = bf16[8,32,640]{2,1,0:T(8,128)(2,1)S(1)} async-done(((bf16[8,32,640]{2,1,0:T(8,128)(2,1)}), bf16[8,32,640]{2,1,0:T(8,128)(2,1)S(1)}, u32[]{:S(2)}, u32[]{:S(2)}) %all-to-all-start.13) | async-done | bytes 327712 | tf_op jit(solution)/shard_map/all_to_all | solution.py:468
  211.3 2.5 %shard_map.128 = (f32[4,384,128]{2,1,0:T(8,128)S(1)}, bf16[512,256]{1,0:T(8,128)(2,1)S(1)}) custom-call(s32[1]{0:T(128)} %bitcast.17.place_ref, bf16[8,32,640]{2,1,0:T(8,128)(2,1)S(1)} %all-to-all-done.13.got_ref, bf16[256,256]{1,0:T(8,128)(2,1)S(1)} %compare_convert_fusion.refs_2_.hot_ref, bf16[3,3072,512]{2,1,0:T(8,128)(2,1)} %bitcast.36, ...), custom_call_target="tpu_custom_call" | custom-call | flops 805306368 | bytes 3145728 | tf_op jit(solution)/shard_map/pallas_call | solution.py:488
  213.9 1.2 collective-permute-start
  215.1 2.5 %shard_map.129 = f32[4,384,128]{2,1,0:T(8,128)S(1)} custom-call(s32[1]{0:T(128)} %bitcast.16.place_ref, bf16[512,256]{1,0:T(8,128)(2,1)S(1)} %get-tuple-element.78.picked_ref, bf16[3,3072,512]{2,1,0:T(8,128)(2,1)} %bitcast.37, f32[8,384,128]{2,1,0:T(8,128)} %shard_map.126.early_ref), custom_call_target="tpu_custom_call" | custom-call | flops 805306368 | bytes 3145728 | tf_op jit(solution)/shard_map/pallas_call | solution.py:498
  217.6 1.0 add.104
  218.6 3.6 %all-to-all-start.14 = ((f32[4,384,128]{2,1,0:T(8,128)}), f32[4,384,128]{2,1,0:T(8,128)S(1)}, u32[]{:S(2)}, u32[]{:S(2)}) async-start(f32[4,384,128]{2,1,0:T(8,128)} %add.104), calls=%async_computation.14 | async-start | bytes 1572864 | tf_op jit(solution)/shard_map/all_to_all | solution.py:507
  222.2 1.0 dynamic-slice_bitcast_fusion
  223.3 1.0 dynamic-slice_bitcast_fusion.1
  224.3 0.1 dynamic-slice_bitcast_fusion.2
  224.5 0.7 copy.16
  225.2 9.3 %all-to-all-done.14 = f32[4,384,128]{2,1,0:T(8,128)S(1)} async-done(((f32[4,384,128]{2,1,0:T(8,128)}), f32[4,384,128]{2,1,0:T(8,128)S(1)}, u32[]{:S(2)}, u32[]{:S(2)}) %all-to-all-start.14) | async-done | bytes 786464 | tf_op jit(solution)/shard_map/all_to_all | solution.py:507
  234.6 0.7 add.105
  (54 shorter events, 1.0 us)
Async XLA Ops:
  7.2 12.1 %copy-start = (f32[3,256,128]{2,1,0:T(8,128)S(1)}, f32[3,256,128]{2,1,0:T(8,128)}, u32[]{:S(2)}) copy-start(f32[3,256,128]{2,1,0:T(8,128)} %param.13) | copy-start | bytes 1179652
  7.2 35.7 %all-gather.11.cloned.1.call-start = ((), (), s32[]{:S(2)}) async-start(), calls=%async_computation.15 | async-start | bytes 2359296 | tf_op jit(solution)/shard_map/all_gather | solution.py:315
  7.2 5.3 %copy-start.4 = (bf16[3,256,512]{2,1,0:T(8,128)(2,1)S(1)}, bf16[3,256,512]{2,1,0:T(8,128)(2,1)}, u32[]{:S(2)}) copy-start(bf16[3,256,512]{2,1,0:T(8,128)(2,1)} %param.12) | copy-start | bytes 2359300
  12.5 7.0 %copy-start.7 = (s32[128]{0:T(128)S(1)}, s32[128]{0:T(128)}, u32[]{:S(2)}) copy-start(s32[128]{0:T(128)} %param.17) | copy-start | bytes 1540
  12.5 7.0 %copy-start.6 = (s32[128]{0:T(128)S(1)}, s32[128]{0:T(128)}, u32[]{:S(2)}) copy-start(s32[128]{0:T(128)} %param.16) | copy-start | bytes 1540
  12.5 7.1 %copy-start.8 = (f32[128]{0:T(128)S(1)}, f32[128]{0:T(128)}, u32[]{:S(2)}) copy-start(f32[128]{0:T(128)} %param.15) | copy-start | bytes 1540
  12.5 14.7 %slice-start = ((bf16[3,256,512]{2,1,0:T(8,128)(2,1)}), bf16[1,256,512]{2,1,0:T(8,128)(2,1)S(1)}, s32[]{:S(2)}) async-start(bf16[3,256,512]{2,1,0:T(8,128)(2,1)} %param.10), calls=%async_computation.20 | async-start | bytes 524288 | tf_op jit(solution)/shard_map/slice | solution.py:333
  12.5 14.7 %slice-start.2 = ((bf16[3,256,512]{2,1,0:T(8,128)(2,1)}), bf16[1,256,512]{2,1,0:T(8,128)(2,1)S(1)}, s32[]{:S(2)}) async-start(bf16[3,256,512]{2,1,0:T(8,128)(2,1)} %param.12), calls=%async_computation.22 | async-start | bytes 524288 | tf_op jit(solution)/shard_map/slice | solution.py:333
  13.3 13.7 %all-to-all-start = ((f32[8,16,768]{2,1,0:T(8,128)}), f32[8,16,768]{2,1,0:T(8,128)S(1)}, u32[]{:S(2)}, u32[]{:S(2)}) async-start(f32[8,16,768]{2,1,0:T(8,128)} %shard_map.113), calls=%async_computation | async-start | bytes 786432 | tf_op jit(solution)/shard_map/all_to_all | solution.py:316
  19.3 64.9 %all-gather.13.cloned.1.call-start = ((), (), s32[]{:S(2)}) async-start(), calls=%async_computation.16 | async-start | bytes 4718592 | tf_op jit(solution)/shard_map/all_gather | solution.py:333
  28.1 105.2 %all-gather.15.cloned.1.call-start = ((), (), s32[]{:S(2)}) async-start(), calls=%async_computation.17 | async-start | bytes 7077888 | tf_op jit(solution)/shard_map/all_gather | solution.py:426
  42.9 2.5 %slice-start.3 = ((bf16[3,256,512]{2,1,0:T(8,128)(2,1)}), bf16[1,256,512]{2,1,0:T(8,128)(2,1)S(1)}, s32[]{:S(2)}) async-start(bf16[3,256,512]{2,1,0:T(8,128)(2,1)} %param.12), calls=%async_computation.23 | async-start | bytes 524288 | tf_op jit(solution)/shard_map/slice | solution.py:426
  42.9 2.5 %slice-start.1 = ((bf16[3,256,512]{2,1,0:T(8,128)(2,1)}), bf16[2,256,512]{2,1,0:T(8,128)(2,1)S(1)}, s32[]{:S(2)}) async-start(bf16[3,256,512]{2,1,0:T(8,128)(2,1)} %param.10), calls=%async_computation.21 | async-start | bytes 1048576 | tf_op jit(solution)/shard_map/slice | solution.py:426
  45.4 14.6 %copy-start.3 = (bf16[8,256,512]{2,1,0:T(8,128)(2,1)S(1)}, bf16[8,256,512]{2,1,0:T(8,128)(2,1)}, u32[]{:S(2)}) copy-start(bf16[8,256,512]{2,1,0:T(8,128)(2,1)} %all-gather.11.cloned.1.call-done) | copy-start | bytes 6291460
  46.4 130.7 %all-gather.19.cloned.1.call-start = ((), (), s32[]{:S(2)}) async-start(), calls=%async_computation.19 | async-start | bytes 2359296 | tf_op jit(solution)/shard_map/all_gather | solution.py:459
  84.1 93.1 %all-gather.17.cloned.1.call-start = ((), (), s32[]{:S(2)}) async-start(), calls=%async_computation.18 | async-start | bytes 2359296 | tf_op jit(solution)/shard_map/all_gather | solution.py:459
  84.1 13.9 %copy-start.2 = (bf16[16,256,512]{2,1,0:T(8,128)(2,1)S(1)}, bf16[16,256,512]{2,1,0:T(8,128)(2,1)}, u32[]{:S(2)}) copy-start(bf16[16,256,512]{2,1,0:T(8,128)(2,1)} %all-gather.13.cloned.1.call-done) | copy-start | bytes 12582916
  133.3 15.6 %copy-start.1 = (bf16[24,256,512]{2,1,0:T(8,128)(2,1)S(1)}, bf16[24,256,512]{2,1,0:T(8,128)(2,1)}, u32[]{:S(2)}) copy-start(bf16[24,256,512]{2,1,0:T(8,128)(2,1)} %all-gather.15.cloned.1.call-done) | copy-start | bytes 18874372
  173.6 12.1 %all-to-all-start.12 = ((bf16[16,32,256]{2,1,0:T(8,128)(2,1)}), bf16[16,32,256]{2,1,0:T(8,128)(2,1)S(1)}, u32[]{:S(2)}, u32[]{:S(2)}) async-start(bf16[16,32,256]{2,1,0:T(8,128)(2,1)} %get-tuple-element.70), calls=%async_computation.12 | async-start | bytes 524288 | tf_op jit(solution)/shard_map/all_to_all | solution.py:343
  186.5 24.8 %all-to-all-start.13 = ((bf16[8,32,640]{2,1,0:T(8,128)(2,1)}), bf16[8,32,640]{2,1,0:T(8,128)(2,1)S(1)}, u32[]{:S(2)}, u32[]{:S(2)}) async-start(bf16[8,32,640]{2,1,0:T(8,128)(2,1)} %shard_map.127), calls=%async_computation.13 | async-start | bytes 655360 | tf_op jit(solution)/shard_map/all_to_all | solution.py:468
  213.9 3.8 %collective-permute-start = (f32[4,384,128]{2,1,0:T(8,128)S(1)}, f32[4,384,128]{2,1,0:T(8,128)S(1)}, u32[]{:S(2)}, u32[]{:S(2)}) collective-permute-start(f32[4,384,128]{2,1,0:T(8,128)S(1)} %get-tuple-element.79), channel_id=1, source_target_pairs={{0,1},{1,0},{2,3},{3,2},{4,5},{5,4},{6,7},{7,6},{8,9},{9,8},{10,11... | collective-permute-start | bytes 2359304 | tf_op jit(solution)/shard_map/ppermute | solution.py:497
  218.6 16.0 %copy-start.5 = (f32[384,128]{1,0:T(8,128)S(1)}, f32[384,128]{1,0:T(8,128)}, u32[]{:S(2)}) copy-start(f32[384,128]{1,0:T(8,128)} %param.19) | copy-start | bytes 589828
  218.6 15.9 %all-to-all-start.14 = ((f32[4,384,128]{2,1,0:T(8,128)}), f32[4,384,128]{2,1,0:T(8,128)S(1)}, u32[]{:S(2)}, u32[]{:S(2)}) async-start(f32[4,384,128]{2,1,0:T(8,128)} %add.104), calls=%async_computation.14 | async-start | bytes 1572864 | tf_op jit(solution)/shard_map/all_to_all | solution.py:507
Sparse Core Ops, SparseCore 0:
  13.4 28.8 all-gather.10
  44.1 32.4 all-gather.12
  78.2 40.8 all-gather.14
  120.7 25.3 all-gather.18
  147.7 25.6 all-gather.16

commit v7 on v6

--- a/solution.py
+++ b/solution.py
@@ -12,7 +12,7 @@
 BF16 = jnp.bfloat16
 VMEM_LIMIT = 16 << 20
 LANES = 128
-CHUNK = 768
+CHUNK = 1536
 
 
 def rows_product(pairs_ref, rows_ref, which, copies=None):
@@ -327,10 +327,13 @@
     value_of = order // (2 * group) * group + order % group
     target = jnp.concatenate([column_map, column_map + width])
     hot = ((half_of * width + value_of)[:, None] == target[None, :]).astype(BF16)
-    old_part, my_offsets, forcing_t, limits, hot, t_upper, inverses = lax.optimization_barrier(
-        (old_part, my_offsets, forcing_t, limits, hot, t_upper, inverses)
+    hot, t_upper, inverses = lax.optimization_barrier((hot, t_upper, inverses))
+    set_b = jnp.concatenate([t_upper[2:3], inverses[1:2]])
+    set_c = jnp.concatenate([t_upper[:2], inverses[:1]])
+    old_part, my_offsets, forcing_t, limits, hot, set_b, set_c = lax.optimization_barrier(
+        (old_part, my_offsets, forcing_t, limits, hot, set_b, set_c)
     )
-    gathered[1] = gather(jnp.concatenate([t_upper[2:3], inverses[1:2]]))
+    gathered[1] = gather(set_b)
     which_inv = {2: 0, 1: 1, 0: 2}
     which_upper = {(1, 2): 0, (0, 1): 0, (0, 2): 1}
 
@@ -422,8 +425,8 @@
                 gathered[step],
                 flops=flops,
             )
-            send, t_upper, inverses = lax.optimization_barrier((send, t_upper, inverses))
-            gathered[0] = gather(jnp.concatenate([t_upper[:2], inverses[:1]]))
+            send, set_c = lax.optimization_barrier((send, set_c))
+            gathered[0] = gather(set_c)
         else:
             send, total = call(
                 functools.partial(first_term_kernel, which),

time: 243 us -> 241 us (level)
  waiting for transfers between devices: 26.1 us -> 23.5 us
  transfers between devices with their start and end apart: 10 -> 10, of which waited for: 4 -> 5; matrix products, arithmetic and copies ran while one was open for 2% -> 2% of each run, Pallas kernels for 11% -> 11%
where the time goes in v7:
time: 241 us; the launch traced here: 240 us
  blocking collectives  126 us (52%)
  Pallas kernels  34.7 us (14%)
  starting transfers between devices  33 us (14%)
  waiting for transfers between devices  23.5 us (10%)
  between operations  14.1 us (6%)
  local copies, waits for them, and re-layouts  4.53 us (2%)
  other arithmetic  3.78 us (2%)
    all_to_all x11, blocking collectives, spread(): return lax.all_to_all(send, 'row', 0, 0)  126 us
    all_to_all x1, starting transfers between devices, body(): got = lax.all_to_all(send, 'col', 0, 0)  18.3 us
    pallas_call x3, Pallas kernels, call_streamed(): pl.pallas_call(kernel, out_shape=outs, in_specs=[hb if stream_vectors els...  10.6 us
    all_to_all x1, waiting for transfers between devices, body(): lax.all_to_all(ours + swapped, 'col', 0, 0, axis_index_groups=[list(range...  9.35 us
    pallas_call x10, Pallas kernels, call(): pl.pallas_call(kernel, out_shape=outs, in_specs=[pl.BlockSpec(memory_spac...  8.57 us
    all_to_all x1, waiting for transfers between devices, body(): got = lax.all_to_all(send, 'col', 0, 0)  7.09 us
    pallas_call x1, Pallas kernels, early_z(): pl.pallas_call(z_early_kernel, out_shape=[pltpu.HBM((n_col, z_block, widt...  6.13 us
    all_to_all x1, starting transfers between devices, body(): old_part = lax.all_to_all(old_part, 'col', 0, 0)  5.97 us
  transfers between devices with their start and end apart: 10, of which 5 were waited for; matrix products, arithmetic and copies ran while one was open for 2% of the time, Pallas kernels for 11%

profile of v7, /device:TPU:1, one launch (start us, length us, event | category | flops | bytes accessed | tf_op | source)
XLA Modules:
  0.0 240.1 jit_solution(9119458844828598231)
XLA Ops:
  7.3 4.4 %shard_map.113 = f32[8,16,768]{2,1,0:T(8,128)} custom-call(s32[1]{0:T(128)} %bitcast.base_ref, bf16[3,256,3072]{2,1,0:T(8,128)(2,1)} %t_ref.1, bf16[3072,128]{1,0:T(8,128)(2,1)} %old_ref.1, s32[1,128]{1,0:T(1,128)} %bitcast.43), custom_call_target="tpu_custom_call" | custom-call | flops 603979776 | bytes 4718592 | tf_op jit(solution)/shard_map/pallas_call | solution.py:291
  11.6 0.7 slice.25
  12.4 6.0 %all-to-all-start = ((f32[8,16,768]{2,1,0:T(8,128)}), f32[8,16,768]{2,1,0:T(8,128)S(1)}, u32[]{:S(2)}, u32[]{:S(2)}) async-start(f32[8,16,768]{2,1,0:T(8,128)} %shard_map.113), calls=%async_computation | async-start | bytes 786432 | tf_op jit(solution)/shard_map/all_to_all | solution.py:316
  18.6 0.2 constant_dynamic-slice_fusion
  18.8 0.1 copy.17
  19.1 0.2 slice-done
  19.3 0.8 pad_maximum_fusion.1
  20.2 0.9 pad_maximum_fusion
  21.1 4.9 %all-to-all-done.parts_ref = f32[8,16,768]{2,1,0:T(8,128)S(1)} async-done(((f32[8,16,768]{2,1,0:T(8,128)}), f32[8,16,768]{2,1,0:T(8,128)S(1)}, u32[]{:S(2)}, u32[]{:S(2)}) %all-to-all-start) | async-done | bytes 393248 | tf_op jit(solution)/shard_map/all_to_all | solution.py:316
  26.4 14.7 %all_to_all.75.pairs_ref = bf16[16,32,256]{2,1,0:T(8,128)(2,1)S(1)} all-to-all(bf16[16,32,256]{2,1,0:T(8,128)(2,1)S(1)} %get-tuple-element.50), channel_id=1, replica_groups=mesh['row'=16,'col'=8] {'row'}, dimensions={0} | all-to-all | bytes 524288 | tf_op jit(solution)/shard_map/all_to_all | solution.py:346
  41.2 0.3 all-gather.11.cloned.1.call-done
  41.4 2.6 %shard_map.115 = (bf16[16,32,256]{2,1,0:T(8,128)(2,1)S(1)}, f32[16,256]{1,0:T(8,128)S(1)}) custom-call(bf16[16,32,256]{2,1,0:T(8,128)(2,1)S(1)} %all_to_all.75.pairs_ref, bf16[8,1,256,512]{3,2,1,0:T(8,128)(2,1)} %bitcast.31), custom_call_target="tpu_custom_call" | custom-call | flops 67108864 | bytes 2097152 | tf_op jit(solution)/shard_map/pallas_call | solution.py:257
  44.1 14.1 %all_to_all.76.pairs_ref = bf16[16,32,256]{2,1,0:T(8,128)(2,1)S(1)} all-to-all(bf16[16,32,256]{2,1,0:T(8,128)(2,1)S(1)} %get-tuple-element.53), channel_id=1, replica_groups=mesh['row'=16,'col'=8] {'row'}, dimensions={0} | all-to-all | bytes 524288 | tf_op jit(solution)/shard_map/all_to_all | solution.py:346
  58.2 0.7 shard_map.116
  58.9 10.9 %all_to_all.77.pairs_ref = bf16[16,32,256]{2,1,0:T(8,128)(2,1)S(1)} all-to-all(bf16[16,32,256]{2,1,0:T(8,128)(2,1)S(1)} %get-tuple-element.56), channel_id=1, replica_groups=mesh['row'=16,'col'=8] {'row'}, dimensions={0} | all-to-all | bytes 524288 | tf_op jit(solution)/shard_map/all_to_all | solution.py:346
  69.8 1.3 shard_map.117
  71.1 11.1 %all_to_all.78.refs_0_.refs_1_ = bf16[16,32,256]{2,1,0:T(8,128)(2,1)} all-to-all(bf16[16,32,256]{2,1,0:T(8,128)(2,1)S(1)} %get-tuple-element.59), channel_id=1, replica_groups=mesh['row'=16,'col'=8] {'row'}, dimensions={0} | all-to-all | bytes 524288 | tf_op jit(solution)/shard_map/all_to_all | solution.py:346
  82.3 3.1 %shard_map.118 = bf16[16,32,256]{2,1,0:T(8,128)(2,1)S(1)} custom-call(bf16[16,32,256]{2,1,0:T(8,128)(2,1)} %all_to_all.78.refs_0_.refs_1_, bf16[8,2,256,512]{3,2,1,0:T(8,128)(2,1)} %bitcast.27, f32[16,512]{1,0:T(8,128)S(1)} %get-tuple-element.61.refs_2_.refs_3_), custom_call_target="tpu_custom_call" | custom-call | flops 67108864 | bytes 2097152 | tf_op jit(solution)/shard_map/pallas_call | solution.py:257
  85.5 10.7 %all_to_all.79.pairs_ref = bf16[16,32,256]{2,1,0:T(8,128)(2,1)S(1)} all-to-all(bf16[16,32,256]{2,1,0:T(8,128)(2,1)S(1)} %shard_map.118), channel_id=1, replica_groups=mesh['row'=16,'col'=8] {'row'}, dimensions={0} | all-to-all | bytes 524288 | tf_op jit(solution)/shard_map/all_to_all | solution.py:346
  96.2 0.7 shard_map.119
  96.9 10.9 %all_to_all.80.pairs_ref = bf16[16,32,256]{2,1,0:T(8,128)(2,1)S(1)} all-to-all(bf16[16,32,256]{2,1,0:T(8,128)(2,1)S(1)} %get-tuple-element.62), channel_id=1, replica_groups=mesh['row'=16,'col'=8] {'row'}, dimensions={0} | all-to-all | bytes 524288 | tf_op jit(solution)/shard_map/all_to_all | solution.py:346
  107.9 0.7 shard_map.120
  108.6 10.9 %all_to_all.81.pairs_ref = bf16[16,32,256]{2,1,0:T(8,128)(2,1)S(1)} all-to-all(bf16[16,32,256]{2,1,0:T(8,128)(2,1)S(1)} %get-tuple-element.64), channel_id=1, replica_groups=mesh['row'=16,'col'=8] {'row'}, dimensions={0} | all-to-all | bytes 524288 | tf_op jit(solution)/shard_map/all_to_all | solution.py:346
  119.5 1.3 shard_map.121
  120.8 10.9 %all_to_all.82.refs_0_ = bf16[16,32,256]{2,1,0:T(8,128)(2,1)} all-to-all(bf16[16,32,256]{2,1,0:T(8,128)(2,1)S(1)} %get-tuple-element.67), channel_id=1, replica_groups=mesh['row'=16,'col'=8] {'row'}, dimensions={0} | all-to-all | bytes 524288 | tf_op jit(solution)/shard_map/all_to_all | solution.py:346
  131.8 4.9 %shard_map.122 = bf16[16,32,256]{2,1,0:T(8,128)(2,1)S(1)} custom-call(bf16[16,32,256]{2,1,0:T(8,128)(2,1)} %all_to_all.82.refs_0_, bf16[16,32,256]{2,1,0:T(8,128)(2,1)} %all_to_all.78.refs_0_.refs_1_, bf16[8,3,256,512]{3,2,1,0:T(8,128)(2,1)} %bitcast.23, f32[16,512]{1,0:T(8,128)S(1)} %get-tuple-element.61.refs_2_.refs_3_), custom_call_target="tpu_custom_call" | custom-call | flops 134217728 | bytes 4194304 | tf_op jit(solution)/shard_map/pallas_call | solution.py:257
  136.7 10.7 %all_to_all.83.pairs_ref = bf16[16,32,256]{2,1,0:T(8,128)(2,1)S(1)} all-to-all(bf16[16,32,256]{2,1,0:T(8,128)(2,1)S(1)} %shard_map.122), channel_id=1, replica_groups=mesh['row'=16,'col'=8] {'row'}, dimensions={0} | all-to-all | bytes 524288 | tf_op jit(solution)/shard_map/all_to_all | solution.py:346
  147.5 0.7 shard_map.123
  148.2 10.5 %all_to_all.84.pairs_ref = bf16[16,32,256]{2,1,0:T(8,128)(2,1)S(1)} all-to-all(bf16[16,32,256]{2,1,0:T(8,128)(2,1)S(1)} %get-tuple-element.69), channel_id=1, replica_groups=mesh['row'=16,'col'=8] {'row'}, dimensions={0} | all-to-all | bytes 524288 | tf_op jit(solution)/shard_map/all_to_all | solution.py:346
  158.7 0.7 shard_map.124
  159.4 10.9 %all_to_all.85.pairs_ref = bf16[16,32,256]{2,1,0:T(8,128)(2,1)S(1)} all-to-all(bf16[16,32,256]{2,1,0:T(8,128)(2,1)S(1)} %get-tuple-element.71), channel_id=1, replica_groups=mesh['row'=16,'col'=8] {'row'}, dimensions={0} | all-to-all | bytes 524288 | tf_op jit(solution)/shard_map/all_to_all | solution.py:346
  170.3 1.4 shard_map.125
  171.8 3.7 %all-to-all-start.12 = ((bf16[16,32,256]{2,1,0:T(8,128)(2,1)}), bf16[16,32,256]{2,1,0:T(8,128)(2,1)S(1)}, u32[]{:S(2)}, u32[]{:S(2)}) async-start(bf16[16,32,256]{2,1,0:T(8,128)(2,1)} %get-tuple-element.74), calls=%async_computation.12 | async-start | bytes 524288 | tf_op jit(solution)/shard_map/all_to_all | solution.py:346
  175.6 6.1 %shard_map.126.early_ref = f32[8,384,128]{2,1,0:T(8,128)} custom-call(s32[1]{0:T(128)} %bitcast.7.place_ref, bf16[8,16,32,256]{3,2,1,0:T(8,128)(2,1)} %bitcast.40, bf16[8,16,32,256]{3,2,1,0:T(8,128)(2,1)} %bitcast.38, bf16[256,256]{1,0:T(8,128)(2,1)S(1)} %compare_convert_fusion.refs_2_.hot_ref, bf16[3,3072,512]{2,1,0:T(8,128)(2,1)} %bitcast.35), custom_call_target="tpu_custom_call" | custom-call | flops 1610612736 | bytes 6291456 | tf_op jit(solution)/shard_map/pallas_call | solution.py:374
  181.7 1.7 all-to-all-done.12.whole_ref
  183.4 0.8 shard_map.127
  184.2 18.3 %all-to-all-start.13 = ((bf16[8,32,640]{2,1,0:T(8,128)(2,1)}), bf16[8,32,640]{2,1,0:T(8,128)(2,1)S(1)}, u32[]{:S(2)}, u32[]{:S(2)}) async-start(bf16[8,32,640]{2,1,0:T(8,128)(2,1)} %shard_map.127), calls=%async_computation.13 | async-start | bytes 655360 | tf_op jit(solution)/shard_map/all_to_all | solution.py:471
  202.5 7.1 %all-to-all-done.13.got_ref = bf16[8,32,640]{2,1,0:T(8,128)(2,1)S(1)} async-done(((bf16[8,32,640]{2,1,0:T(8,128)(2,1)}), bf16[8,32,640]{2,1,0:T(8,128)(2,1)S(1)}, u32[]{:S(2)}, u32[]{:S(2)}) %all-to-all-start.13) | async-done | bytes 327712 | tf_op jit(solution)/shard_map/all_to_all | solution.py:471
  209.6 2.5 %shard_map.128 = (f32[4,384,128]{2,1,0:T(8,128)S(1)}, bf16[512,256]{1,0:T(8,128)(2,1)S(1)}) custom-call(s32[1]{0:T(128)} %bitcast.17.place_ref, bf16[8,32,640]{2,1,0:T(8,128)(2,1)S(1)} %all-to-all-done.13.got_ref, bf16[256,256]{1,0:T(8,128)(2,1)S(1)} %compare_convert_fusion.refs_2_.hot_ref, bf16[3,3072,512]{2,1,0:T(8,128)(2,1)} %bitcast.36, ...), custom_call_target="tpu_custom_call" | custom-call | flops 805306368 | bytes 3145728 | tf_op jit(solution)/shard_map/pallas_call | solution.py:491
  212.1 1.2 collective-permute-start
  213.3 2.5 %shard_map.129 = f32[4,384,128]{2,1,0:T(8,128)S(1)} custom-call(s32[1]{0:T(128)} %bitcast.16.place_ref, bf16[512,256]{1,0:T(8,128)(2,1)S(1)} %get-tuple-element.82.picked_ref, bf16[3,3072,512]{2,1,0:T(8,128)(2,1)} %bitcast.37, f32[8,384,128]{2,1,0:T(8,128)} %shard_map.126.early_ref), custom_call_target="tpu_custom_call" | custom-call | flops 805306368 | bytes 3145728 | tf_op jit(solution)/shard_map/pallas_call | solution.py:501
  215.9 1.0 add.104
  216.9 3.6 %all-to-all-start.14 = ((f32[4,384,128]{2,1,0:T(8,128)}), f32[4,384,128]{2,1,0:T(8,128)S(1)}, u32[]{:S(2)}, u32[]{:S(2)}) async-start(f32[4,384,128]{2,1,0:T(8,128)} %add.104), calls=%async_computation.14 | async-start | bytes 1572864 | tf_op jit(solution)/shard_map/all_to_all | solution.py:510
  220.5 1.0 dynamic-slice_bitcast_fusion
  221.5 1.0 dynamic-slice_bitcast_fusion.1
  222.7 0.7 copy.16
  223.4 9.3 %all-to-all-done.14 = f32[4,384,128]{2,1,0:T(8,128)S(1)} async-done(((f32[4,384,128]{2,1,0:T(8,128)}), f32[4,384,128]{2,1,0:T(8,128)S(1)}, u32[]{:S(2)}, u32[]{:S(2)}) %all-to-all-start.14) | async-done | bytes 786464 | tf_op jit(solution)/shard_map/all_to_all | solution.py:510
  232.8 0.7 add.105
  (51 shorter events, 1.3 us)
Async XLA Ops:
  7.2 11.5 %copy-start = (f32[3,256,128]{2,1,0:T(8,128)S(1)}, f32[3,256,128]{2,1,0:T(8,128)}, u32[]{:S(2)}) copy-start(f32[3,256,128]{2,1,0:T(8,128)} %param.13) | copy-start | bytes 1179652
  7.2 34.3 %all-gather.11.cloned.1.call-start = ((), (), s32[]{:S(2)}) async-start(), calls=%async_computation.15 | async-start | bytes 2359296 | tf_op jit(solution)/shard_map/all_gather | solution.py:315
  7.2 4.4 %copy-start.4 = (bf16[3,256,512]{2,1,0:T(8,128)(2,1)S(1)}, bf16[3,256,512]{2,1,0:T(8,128)(2,1)}, u32[]{:S(2)}) copy-start(bf16[3,256,512]{2,1,0:T(8,128)(2,1)} %param.12) | copy-start | bytes 2359300
  7.2 11.2 %copy-start.7 = (s32[128]{0:T(128)S(1)}, s32[128]{0:T(128)}, u32[]{:S(2)}) copy-start(s32[128]{0:T(128)} %param.17) | copy-start | bytes 1540
  11.6 6.9 %copy-start.8 = (f32[128]{0:T(128)S(1)}, f32[128]{0:T(128)}, u32[]{:S(2)}) copy-start(f32[128]{0:T(128)} %param.15) | copy-start | bytes 1540
  12.4 13.7 %all-to-all-start = ((f32[8,16,768]{2,1,0:T(8,128)}), f32[8,16,768]{2,1,0:T(8,128)S(1)}, u32[]{:S(2)}, u32[]{:S(2)}) async-start(f32[8,16,768]{2,1,0:T(8,128)} %shard_map.113), calls=%async_computation | async-start | bytes 786432 | tf_op jit(solution)/shard_map/all_to_all | solution.py:316
  18.3 0.7 copy-start.6
  18.3 1.0 slice-start
  18.4 64.0 %all-gather.13.cloned.1.call-start = ((), (), s32[]{:S(2)}) async-start(), calls=%async_computation.16 | async-start | bytes 4718592 | tf_op jit(solution)/shard_map/all_gather | solution.py:336
  18.5 1.6 slice-start.1
  26.4 105.4 %all-gather.15.cloned.1.call-start = ((), (), s32[]{:S(2)}) async-start(), calls=%async_computation.17 | async-start | bytes 7077888 | tf_op jit(solution)/shard_map/all_gather | solution.py:429
  41.4 16.8 %copy-start.3 = (bf16[8,256,512]{2,1,0:T(8,128)(2,1)S(1)}, bf16[8,256,512]{2,1,0:T(8,128)(2,1)}, u32[]{:S(2)}) copy-start(bf16[8,256,512]{2,1,0:T(8,128)(2,1)} %all-gather.11.cloned.1.call-done) | copy-start | bytes 6291460
  44.0 131.5 %all-gather.19.cloned.1.call-start = ((), (), s32[]{:S(2)}) async-start(), calls=%async_computation.19 | async-start | bytes 2359296 | tf_op jit(solution)/shard_map/all_gather | solution.py:462
  82.3 93.3 %all-gather.17.cloned.1.call-start = ((), (), s32[]{:S(2)}) async-start(), calls=%async_computation.18 | async-start | bytes 2359296 | tf_op jit(solution)/shard_map/all_gather | solution.py:462
  82.3 13.9 %copy-start.2 = (bf16[16,256,512]{2,1,0:T(8,128)(2,1)S(1)}, bf16[16,256,512]{2,1,0:T(8,128)(2,1)}, u32[]{:S(2)}) copy-start(bf16[16,256,512]{2,1,0:T(8,128)(2,1)} %all-gather.13.cloned.1.call-done) | copy-start | bytes 12582916
  131.8 15.7 %copy-start.1 = (bf16[24,256,512]{2,1,0:T(8,128)(2,1)S(1)}, bf16[24,256,512]{2,1,0:T(8,128)(2,1)}, u32[]{:S(2)}) copy-start(bf16[24,256,512]{2,1,0:T(8,128)(2,1)} %all-gather.15.cloned.1.call-done) | copy-start | bytes 18874372
  171.8 11.6 %all-to-all-start.12 = ((bf16[16,32,256]{2,1,0:T(8,128)(2,1)}), bf16[16,32,256]{2,1,0:T(8,128)(2,1)S(1)}, u32[]{:S(2)}, u32[]{:S(2)}) async-start(bf16[16,32,256]{2,1,0:T(8,128)(2,1)} %get-tuple-element.74), calls=%async_computation.12 | async-start | bytes 524288 | tf_op jit(solution)/shard_map/all_to_all | solution.py:346
  184.2 25.4 %all-to-all-start.13 = ((bf16[8,32,640]{2,1,0:T(8,128)(2,1)}), bf16[8,32,640]{2,1,0:T(8,128)(2,1)S(1)}, u32[]{:S(2)}, u32[]{:S(2)}) async-start(bf16[8,32,640]{2,1,0:T(8,128)(2,1)} %shard_map.127), calls=%async_computation.13 | async-start | bytes 655360 | tf_op jit(solution)/shard_map/all_to_all | solution.py:471
  212.1 3.8 %collective-permute-start = (f32[4,384,128]{2,1,0:T(8,128)S(1)}, f32[4,384,128]{2,1,0:T(8,128)S(1)}, u32[]{:S(2)}, u32[]{:S(2)}) collective-permute-start(f32[4,384,128]{2,1,0:T(8,128)S(1)} %get-tuple-element.83), channel_id=1, source_target_pairs={{0,1},{1,0},{2,3},{3,2},{4,5},{5,4},{6,7},{7,6},{8,9},{9,8},{10,11... | collective-permute-start | bytes 2359304 | tf_op jit(solution)/shard_map/ppermute | solution.py:500
  216.8 16.0 %copy-start.5 = (f32[384,128]{1,0:T(8,128)S(1)}, f32[384,128]{1,0:T(8,128)}, u32[]{:S(2)}) copy-start(f32[384,128]{1,0:T(8,128)} %param.19) | copy-start | bytes 589828
  216.9 15.9 %all-to-all-start.14 = ((f32[4,384,128]{2,1,0:T(8,128)}), f32[4,384,128]{2,1,0:T(8,128)S(1)}, u32[]{:S(2)}, u32[]{:S(2)}) async-start(f32[4,384,128]{2,1,0:T(8,128)} %add.104), calls=%async_computation.14 | async-start | bytes 1572864 | tf_op jit(solution)/shard_map/all_to_all | solution.py:510
Sparse Core Ops, SparseCore 0:
  12.5 28.8 all-gather.10
  43.2 32.4 all-gather.12
  77.3 40.7 all-gather.14
  119.7 25.3 all-gather.18
  146.7 25.6 all-gather.16

commit v8 on v7

--- a/solution.py
+++ b/solution.py
@@ -102,12 +102,13 @@
     send_to_all(send_ref, pair_of(term))
 
 
-def last_term_kernel(which, pairs_ref, rows_ref, scale_ref, old_ref, limit_ref, send_ref, own_ref):
+def last_term_kernel(which, pairs_ref, rows_ref, scale_ref, old_ref, limit_ref, send_ref, *own_ref):
     term = rows_product(pairs_ref, rows_ref, which) * scale_ref[...]
     total = old_ref[...] + term
     row = lax.broadcasted_iota(jnp.int32, total.shape, 1)
     pair = pair_of(jnp.where(row < limit_ref[...], total, 0.0))
-    own_ref[...] = pair
+    if own_ref:
+        own_ref[0][...] = pair
     send_to_all(send_ref, pair)
 
 
@@ -445,9 +446,9 @@
                 total,
                 flops=flops,
             )
-        send, own[step] = call(
+        send, *own[step] = call(
             functools.partial(last_term_kernel, which),
-            [send_shape, own_shape],
+            [send_shape] if step else [send_shape, own_shape],
             spread(send),
             rows,
             my_offsets,
@@ -456,7 +457,7 @@
             flops=flops,
         )
         if step == 0:
-            own[0], everywhere = lax.optimization_barrier((own[0], everywhere))
+            own[0], everywhere = lax.optimization_barrier((own[0][0], everywhere))
         whole[step] = spread(send)
         if step > 0:
             everywhere[step] = gather(whole[step])

time: 241 us -> 240 us (level)
  no operation moved by 1% of the time
where the time goes in v8:
time: 240 us; the launch traced here: 239 us
  blocking collectives  126 us (52%)
  Pallas kernels  33.5 us (14%)
  starting transfers between devices  33.1 us (14%)
  waiting for transfers between devices  23.1 us (10%)
  between operations  14.1 us (6%)
  local copies, waits for them, and re-layouts  4.53 us (2%)
  other arithmetic  3.81 us (2%)
    all_to_all x11, blocking collectives, spread(): return lax.all_to_all(send, 'row', 0, 0)  126 us
    all_to_all x1, starting transfers between devices, body(): got = lax.all_to_all(send, 'col', 0, 0)  18.3 us
    pallas_call x3, Pallas kernels, call_streamed(): pl.pallas_call(kernel, out_shape=outs, in_specs=[hb if stream_vectors els...  10.6 us
    all_to_all x1, waiting for transfers between devices, body(): lax.all_to_all(ours + swapped, 'col', 0, 0, axis_index_groups=[list(range...  9.35 us
    pallas_call x10, Pallas kernels, call(): pl.pallas_call(kernel, out_shape=outs, in_specs=[pl.BlockSpec(memory_spac...  7.34 us
    all_to_all x1, waiting for transfers between devices, body(): got = lax.all_to_all(send, 'col', 0, 0)  7.09 us
    pallas_call x1, Pallas kernels, early_z(): pl.pallas_call(z_early_kernel, out_shape=[pltpu.HBM((n_col, z_block, widt...  6.11 us
    all_to_all x1, starting transfers between devices, body(): old_part = lax.all_to_all(old_part, 'col', 0, 0)  5.97 us
  transfers between devices with their start and end apart: 10, of which 5 were waited for; matrix products, arithmetic and copies ran while one was open for 2% of the time, Pallas kernels for 11%

profile of v8, /device:TPU:1, one launch (start us, length us, event | category | flops | bytes accessed | tf_op | source)
XLA Modules:
  0.0 238.6 jit_solution(17389270411270031272)
XLA Ops:
  7.3 4.4 %shard_map.113 = f32[8,16,768]{2,1,0:T(8,128)} custom-call(s32[1]{0:T(128)} %bitcast.base_ref, bf16[3,256,3072]{2,1,0:T(8,128)(2,1)} %t_ref.1, bf16[3072,128]{1,0:T(8,128)(2,1)} %old_ref.1, s32[1,128]{1,0:T(1,128)} %bitcast.43), custom_call_target="tpu_custom_call" | custom-call | flops 603979776 | bytes 4718592 | tf_op jit(solution)/shard_map/pallas_call | solution.py:292
  11.6 0.7 slice.25
  12.4 6.0 %all-to-all-start = ((f32[8,16,768]{2,1,0:T(8,128)}), f32[8,16,768]{2,1,0:T(8,128)S(1)}, u32[]{:S(2)}, u32[]{:S(2)}) async-start(f32[8,16,768]{2,1,0:T(8,128)} %shard_map.113), calls=%async_computation | async-start | bytes 786432 | tf_op jit(solution)/shard_map/all_to_all | solution.py:317
  18.7 0.2 constant_dynamic-slice_fusion
  18.8 0.1 copy.17
  19.1 0.2 slice-done
  19.3 0.8 pad_maximum_fusion.1
  20.2 1.0 pad_maximum_fusion
  21.1 4.9 %all-to-all-done.parts_ref = f32[8,16,768]{2,1,0:T(8,128)S(1)} async-done(((f32[8,16,768]{2,1,0:T(8,128)}), f32[8,16,768]{2,1,0:T(8,128)S(1)}, u32[]{:S(2)}, u32[]{:S(2)}) %all-to-all-start) | async-done | bytes 393248 | tf_op jit(solution)/shard_map/all_to_all | solution.py:317
  26.5 14.7 %all_to_all.75.pairs_ref = bf16[16,32,256]{2,1,0:T(8,128)(2,1)S(1)} all-to-all(bf16[16,32,256]{2,1,0:T(8,128)(2,1)S(1)} %get-tuple-element.48), channel_id=1, replica_groups=mesh['row'=16,'col'=8] {'row'}, dimensions={0} | all-to-all | bytes 524288 | tf_op jit(solution)/shard_map/all_to_all | solution.py:347
  41.2 0.3 all-gather.11.cloned.1.call-done
  41.4 2.6 %shard_map.115 = (bf16[16,32,256]{2,1,0:T(8,128)(2,1)S(1)}, f32[16,256]{1,0:T(8,128)S(1)}) custom-call(bf16[16,32,256]{2,1,0:T(8,128)(2,1)S(1)} %all_to_all.75.pairs_ref, bf16[8,1,256,512]{3,2,1,0:T(8,128)(2,1)} %bitcast.31), custom_call_target="tpu_custom_call" | custom-call | flops 67108864 | bytes 2097152 | tf_op jit(solution)/shard_map/pallas_call | solution.py:258
  44.1 14.1 %all_to_all.76.pairs_ref = bf16[16,32,256]{2,1,0:T(8,128)(2,1)S(1)} all-to-all(bf16[16,32,256]{2,1,0:T(8,128)(2,1)S(1)} %get-tuple-element.51), channel_id=1, replica_groups=mesh['row'=16,'col'=8] {'row'}, dimensions={0} | all-to-all | bytes 524288 | tf_op jit(solution)/shard_map/all_to_all | solution.py:347
  58.2 0.7 shard_map.116
  59.0 10.9 %all_to_all.77.pairs_ref = bf16[16,32,256]{2,1,0:T(8,128)(2,1)S(1)} all-to-all(bf16[16,32,256]{2,1,0:T(8,128)(2,1)S(1)} %get-tuple-element.54), channel_id=1, replica_groups=mesh['row'=16,'col'=8] {'row'}, dimensions={0} | all-to-all | bytes 524288 | tf_op jit(solution)/shard_map/all_to_all | solution.py:347
  69.8 0.7 shard_map.117
  70.5 11.1 %all_to_all.78.refs_0_.refs_1_ = bf16[16,32,256]{2,1,0:T(8,128)(2,1)} all-to-all(bf16[16,32,256]{2,1,0:T(8,128)(2,1)S(1)} %shard_map.117), channel_id=1, replica_groups=mesh['row'=16,'col'=8] {'row'}, dimensions={0} | all-to-all | bytes 524288 | tf_op jit(solution)/shard_map/all_to_all | solution.py:347
  81.8 3.1 %shard_map.118 = bf16[16,32,256]{2,1,0:T(8,128)(2,1)S(1)} custom-call(bf16[16,32,256]{2,1,0:T(8,128)(2,1)} %all_to_all.78.refs_0_.refs_1_, bf16[8,2,256,512]{3,2,1,0:T(8,128)(2,1)} %bitcast.27, f32[16,512]{1,0:T(8,128)S(1)} %get-tuple-element.58.refs_2_.refs_3_), custom_call_target="tpu_custom_call" | custom-call | flops 67108864 | bytes 2097152 | tf_op jit(solution)/shard_map/pallas_call | solution.py:258
  84.9 10.7 %all_to_all.79.pairs_ref = bf16[16,32,256]{2,1,0:T(8,128)(2,1)S(1)} all-to-all(bf16[16,32,256]{2,1,0:T(8,128)(2,1)S(1)} %shard_map.118), channel_id=1, replica_groups=mesh['row'=16,'col'=8] {'row'}, dimensions={0} | all-to-all | bytes 524288 | tf_op jit(solution)/shard_map/all_to_all | solution.py:347
  95.6 0.7 shard_map.119
  96.3 10.9 %all_to_all.80.pairs_ref = bf16[16,32,256]{2,1,0:T(8,128)(2,1)S(1)} all-to-all(bf16[16,32,256]{2,1,0:T(8,128)(2,1)S(1)} %get-tuple-element.59), channel_id=1, replica_groups=mesh['row'=16,'col'=8] {'row'}, dimensions={0} | all-to-all | bytes 524288 | tf_op jit(solution)/shard_map/all_to_all | solution.py:347
  107.3 0.7 shard_map.120
  108.0 10.9 %all_to_all.81.pairs_ref = bf16[16,32,256]{2,1,0:T(8,128)(2,1)S(1)} all-to-all(bf16[16,32,256]{2,1,0:T(8,128)(2,1)S(1)} %get-tuple-element.61), channel_id=1, replica_groups=mesh['row'=16,'col'=8] {'row'}, dimensions={0} | all-to-all | bytes 524288 | tf_op jit(solution)/shard_map/all_to_all | solution.py:347
  118.9 0.7 shard_map.121
  119.6 11.0 %all_to_all.82.refs_0_ = bf16[16,32,256]{2,1,0:T(8,128)(2,1)} all-to-all(bf16[16,32,256]{2,1,0:T(8,128)(2,1)S(1)} %shard_map.121), channel_id=1, replica_groups=mesh['row'=16,'col'=8] {'row'}, dimensions={0} | all-to-all | bytes 524288 | tf_op jit(solution)/shard_map/all_to_all | solution.py:347
  130.7 4.9 %shard_map.122 = bf16[16,32,256]{2,1,0:T(8,128)(2,1)S(1)} custom-call(bf16[16,32,256]{2,1,0:T(8,128)(2,1)} %all_to_all.82.refs_0_, bf16[16,32,256]{2,1,0:T(8,128)(2,1)} %all_to_all.78.refs_0_.refs_1_, bf16[8,3,256,512]{3,2,1,0:T(8,128)(2,1)} %bitcast.23, f32[16,512]{1,0:T(8,128)S(1)} %get-tuple-element.58.refs_2_.refs_3_), custom_call_target="tpu_custom_call" | custom-call | flops 134217728 | bytes 4194304 | tf_op jit(solution)/shard_map/pallas_call | solution.py:258
  135.6 10.7 %all_to_all.83.pairs_ref = bf16[16,32,256]{2,1,0:T(8,128)(2,1)S(1)} all-to-all(bf16[16,32,256]{2,1,0:T(8,128)(2,1)S(1)} %shard_map.122), channel_id=1, replica_groups=mesh['row'=16,'col'=8] {'row'}, dimensions={0} | all-to-all | bytes 524288 | tf_op jit(solution)/shard_map/all_to_all | solution.py:347
  146.3 0.7 shard_map.123
  147.0 10.9 %all_to_all.84.pairs_ref = bf16[16,32,256]{2,1,0:T(8,128)(2,1)S(1)} all-to-all(bf16[16,32,256]{2,1,0:T(8,128)(2,1)S(1)} %get-tuple-element.65), channel_id=1, replica_groups=mesh['row'=16,'col'=8] {'row'}, dimensions={0} | all-to-all | bytes 524288 | tf_op jit(solution)/shard_map/all_to_all | solution.py:347
  157.9 0.7 shard_map.124
  158.7 10.6 %all_to_all.85.pairs_ref = bf16[16,32,256]{2,1,0:T(8,128)(2,1)S(1)} all-to-all(bf16[16,32,256]{2,1,0:T(8,128)(2,1)S(1)} %get-tuple-element.67), channel_id=1, replica_groups=mesh['row'=16,'col'=8] {'row'}, dimensions={0} | all-to-all | bytes 524288 | tf_op jit(solution)/shard_map/all_to_all | solution.py:347
  169.2 1.4 shard_map.125
  170.7 3.7 %all-to-all-start.12 = ((bf16[16,32,256]{2,1,0:T(8,128)(2,1)}), bf16[16,32,256]{2,1,0:T(8,128)(2,1)S(1)}, u32[]{:S(2)}, u32[]{:S(2)}) async-start(bf16[16,32,256]{2,1,0:T(8,128)(2,1)} %get-tuple-element.70), calls=%async_computation.12 | async-start | bytes 524288 | tf_op jit(solution)/shard_map/all_to_all | solution.py:347
  174.5 6.1 %shard_map.126.early_ref = f32[8,384,128]{2,1,0:T(8,128)} custom-call(s32[1]{0:T(128)} %bitcast.7.place_ref, bf16[8,16,32,256]{3,2,1,0:T(8,128)(2,1)} %bitcast.40, bf16[8,16,32,256]{3,2,1,0:T(8,128)(2,1)} %bitcast.38, bf16[256,256]{1,0:T(8,128)(2,1)S(1)} %compare_convert_fusion.refs_2_.hot_ref, bf16[3,3072,512]{2,1,0:T(8,128)(2,1)} %bitcast.35), custom_call_target="tpu_custom_call" | custom-call | flops 1610612736 | bytes 6291456 | tf_op jit(solution)/shard_map/pallas_call | solution.py:375
  180.6 1.3 all-to-all-done.12.whole_ref
  181.8 0.8 shard_map.127
  182.6 18.3 %all-to-all-start.13 = ((bf16[8,32,640]{2,1,0:T(8,128)(2,1)}), bf16[8,32,640]{2,1,0:T(8,128)(2,1)S(1)}, u32[]{:S(2)}, u32[]{:S(2)}) async-start(bf16[8,32,640]{2,1,0:T(8,128)(2,1)} %shard_map.127), calls=%async_computation.13 | async-start | bytes 655360 | tf_op jit(solution)/shard_map/all_to_all | solution.py:472
  200.9 7.1 %all-to-all-done.13.got_ref = bf16[8,32,640]{2,1,0:T(8,128)(2,1)S(1)} async-done(((bf16[8,32,640]{2,1,0:T(8,128)(2,1)}), bf16[8,32,640]{2,1,0:T(8,128)(2,1)S(1)}, u32[]{:S(2)}, u32[]{:S(2)}) %all-to-all-start.13) | async-done | bytes 327712 | tf_op jit(solution)/shard_map/all_to_all | solution.py:472
  208.0 2.5 %shard_map.128 = (f32[4,384,128]{2,1,0:T(8,128)S(1)}, bf16[512,256]{1,0:T(8,128)(2,1)S(1)}) custom-call(s32[1]{0:T(128)} %bitcast.17.place_ref, bf16[8,32,640]{2,1,0:T(8,128)(2,1)S(1)} %all-to-all-done.13.got_ref, bf16[256,256]{1,0:T(8,128)(2,1)S(1)} %compare_convert_fusion.refs_2_.hot_ref, bf16[3,3072,512]{2,1,0:T(8,128)(2,1)} %bitcast.36, ...), custom_call_target="tpu_custom_call" | custom-call | flops 805306368 | bytes 3145728 | tf_op jit(solution)/shard_map/pallas_call | solution.py:492
  210.6 1.2 collective-permute-start
  211.8 2.5 %shard_map.129 = f32[4,384,128]{2,1,0:T(8,128)S(1)} custom-call(s32[1]{0:T(128)} %bitcast.16.place_ref, bf16[512,256]{1,0:T(8,128)(2,1)S(1)} %get-tuple-element.78.picked_ref, bf16[3,3072,512]{2,1,0:T(8,128)(2,1)} %bitcast.37, f32[8,384,128]{2,1,0:T(8,128)} %shard_map.126.early_ref), custom_call_target="tpu_custom_call" | custom-call | flops 805306368 | bytes 3145728 | tf_op jit(solution)/shard_map/pallas_call | solution.py:502
  214.3 1.0 add.104
  215.3 3.6 %all-to-all-start.14 = ((f32[4,384,128]{2,1,0:T(8,128)}), f32[4,384,128]{2,1,0:T(8,128)S(1)}, u32[]{:S(2)}, u32[]{:S(2)}) async-start(f32[4,384,128]{2,1,0:T(8,128)} %add.104), calls=%async_computation.14 | async-start | bytes 1572864 | tf_op jit(solution)/shard_map/all_to_all | solution.py:511
  219.0 1.0 dynamic-slice_bitcast_fusion
  220.0 1.0 dynamic-slice_bitcast_fusion.1
  221.2 0.7 copy.16
  221.9 9.4 %all-to-all-done.14 = f32[4,384,128]{2,1,0:T(8,128)S(1)} async-done(((f32[4,384,128]{2,1,0:T(8,128)}), f32[4,384,128]{2,1,0:T(8,128)S(1)}, u32[]{:S(2)}, u32[]{:S(2)}) %all-to-all-start.14) | async-done | bytes 786464 | tf_op jit(solution)/shard_map/all_to_all | solution.py:511
  231.3 0.7 add.105
  (51 shorter events, 1.3 us)
Async XLA Ops:
  7.2 11.5 %copy-start = (f32[3,256,128]{2,1,0:T(8,128)S(1)}, f32[3,256,128]{2,1,0:T(8,128)}, u32[]{:S(2)}) copy-start(f32[3,256,128]{2,1,0:T(8,128)} %param.13) | copy-start | bytes 1179652
  7.2 34.3 %all-gather.11.cloned.1.call-start = ((), (), s32[]{:S(2)}) async-start(), calls=%async_computation.15 | async-start | bytes 2359296 | tf_op jit(solution)/shard_map/all_gather | solution.py:316
  7.2 4.4 %copy-start.4 = (bf16[3,256,512]{2,1,0:T(8,128)(2,1)S(1)}, bf16[3,256,512]{2,1,0:T(8,128)(2,1)}, u32[]{:S(2)}) copy-start(bf16[3,256,512]{2,1,0:T(8,128)(2,1)} %param.12) | copy-start | bytes 2359300
  7.2 11.2 %copy-start.7 = (s32[128]{0:T(128)S(1)}, s32[128]{0:T(128)}, u32[]{:S(2)}) copy-start(s32[128]{0:T(128)} %param.17) | copy-start | bytes 1540
  11.6 6.9 %copy-start.8 = (f32[128]{0:T(128)S(1)}, f32[128]{0:T(128)}, u32[]{:S(2)}) copy-start(f32[128]{0:T(128)} %param.15) | copy-start | bytes 1540
  12.4 13.7 %all-to-all-start = ((f32[8,16,768]{2,1,0:T(8,128)}), f32[8,16,768]{2,1,0:T(8,128)S(1)}, u32[]{:S(2)}, u32[]{:S(2)}) async-start(f32[8,16,768]{2,1,0:T(8,128)} %shard_map.113), calls=%async_computation | async-start | bytes 786432 | tf_op jit(solution)/shard_map/all_to_all | solution.py:317
  18.4 0.7 copy-start.6
  18.4 1.0 slice-start
  18.4 63.4 %all-gather.13.cloned.1.call-start = ((), (), s32[]{:S(2)}) async-start(), calls=%async_computation.16 | async-start | bytes 4718592 | tf_op jit(solution)/shard_map/all_gather | solution.py:337
  18.5 1.6 slice-start.1
  26.4 104.3 %all-gather.15.cloned.1.call-start = ((), (), s32[]{:S(2)}) async-start(), calls=%async_computation.17 | async-start | bytes 7077888 | tf_op jit(solution)/shard_map/all_gather | solution.py:430
  41.4 16.8 %copy-start.3 = (bf16[8,256,512]{2,1,0:T(8,128)(2,1)S(1)}, bf16[8,256,512]{2,1,0:T(8,128)(2,1)}, u32[]{:S(2)}) copy-start(bf16[8,256,512]{2,1,0:T(8,128)(2,1)} %all-gather.11.cloned.1.call-done) | copy-start | bytes 6291460
  44.0 130.4 %all-gather.19.cloned.1.call-start = ((), (), s32[]{:S(2)}) async-start(), calls=%async_computation.19 | async-start | bytes 2359296 | tf_op jit(solution)/shard_map/all_gather | solution.py:463
  81.7 92.8 %all-gather.17.cloned.1.call-start = ((), (), s32[]{:S(2)}) async-start(), calls=%async_computation.18 | async-start | bytes 2359296 | tf_op jit(solution)/shard_map/all_gather | solution.py:463
  81.7 13.9 %copy-start.2 = (bf16[16,256,512]{2,1,0:T(8,128)(2,1)S(1)}, bf16[16,256,512]{2,1,0:T(8,128)(2,1)}, u32[]{:S(2)}) copy-start(bf16[16,256,512]{2,1,0:T(8,128)(2,1)} %all-gather.13.cloned.1.call-done) | copy-start | bytes 12582916
  130.7 15.6 %copy-start.1 = (bf16[24,256,512]{2,1,0:T(8,128)(2,1)S(1)}, bf16[24,256,512]{2,1,0:T(8,128)(2,1)}, u32[]{:S(2)}) copy-start(bf16[24,256,512]{2,1,0:T(8,128)(2,1)} %all-gather.15.cloned.1.call-done) | copy-start | bytes 18874372
  170.7 11.2 %all-to-all-start.12 = ((bf16[16,32,256]{2,1,0:T(8,128)(2,1)}), bf16[16,32,256]{2,1,0:T(8,128)(2,1)S(1)}, u32[]{:S(2)}, u32[]{:S(2)}) async-start(bf16[16,32,256]{2,1,0:T(8,128)(2,1)} %get-tuple-element.70), calls=%async_computation.12 | async-start | bytes 524288 | tf_op jit(solution)/shard_map/all_to_all | solution.py:347
  182.6 25.4 %all-to-all-start.13 = ((bf16[8,32,640]{2,1,0:T(8,128)(2,1)}), bf16[8,32,640]{2,1,0:T(8,128)(2,1)S(1)}, u32[]{:S(2)}, u32[]{:S(2)}) async-start(bf16[8,32,640]{2,1,0:T(8,128)(2,1)} %shard_map.127), calls=%async_computation.13 | async-start | bytes 655360 | tf_op jit(solution)/shard_map/all_to_all | solution.py:472
  210.6 3.8 %collective-permute-start = (f32[4,384,128]{2,1,0:T(8,128)S(1)}, f32[4,384,128]{2,1,0:T(8,128)S(1)}, u32[]{:S(2)}, u32[]{:S(2)}) collective-permute-start(f32[4,384,128]{2,1,0:T(8,128)S(1)} %get-tuple-element.79), channel_id=1, source_target_pairs={{0,1},{1,0},{2,3},{3,2},{4,5},{5,4},{6,7},{7,6},{8,9},{9,8},{10,11... | collective-permute-start | bytes 2359304 | tf_op jit(solution)/shard_map/ppermute | solution.py:501
  215.3 16.0 %copy-start.5 = (f32[384,128]{1,0:T(8,128)S(1)}, f32[384,128]{1,0:T(8,128)}, u32[]{:S(2)}) copy-start(f32[384,128]{1,0:T(8,128)} %param.19) | copy-start | bytes 589828
  215.3 15.9 %all-to-all-start.14 = ((f32[4,384,128]{2,1,0:T(8,128)}), f32[4,384,128]{2,1,0:T(8,128)S(1)}, u32[]{:S(2)}, u32[]{:S(2)}) async-start(f32[4,384,128]{2,1,0:T(8,128)} %add.104), calls=%async_computation.14 | async-start | bytes 1572864 | tf_op jit(solution)/shard_map/all_to_all | solution.py:511
Sparse Core Ops, SparseCore 0:
  12.5 28.8 all-gather.10
  43.2 32.4 all-gather.12
  77.3 40.7 all-gather.14
  119.7 25.3 all-gather.18
  146.7 25.6 all-gather.16
